TPU v7x, 32 devices: a whole 2x2x4 slice. The times are simulated.
32 devices in a mesh: dp: 4 (over z), row: 2 (over core), col: 4 (over y, x).
Axes of the slice: x: 2, y: 2, z: 4, core: 2. Of those that a mesh axis runs over, the one named last changes fastest.
Arguments:
- hidden_in: bfloat16 [4096, 2048], P(('dp', 'row', 'col')), may hold values from -6 to 6
- cotangent: bfloat16 [4096, 2048], P(('dp', 'row', 'col')), may hold values from -6 to 6
- norm_attn: float32 [2048], replicated, may hold values from 0.5 to 1.5
- w_query: bfloat16 [2048, 2048], P('col', 'row'), may hold values from -0.125 to 0.125
- w_key: bfloat16 [2048, 2048], P('col', 'row'), may hold values from -0.125 to 0.125
- w_value: bfloat16 [2048, 2048], P('col', 'row'), may hold values from -0.125 to 0.125
- query_gain: float32 [2048], replicated, may hold values from 0.5 to 1.5
- key_gain: float32 [2048], replicated, may hold values from 0.5 to 1.5
- w_out: bfloat16 [2048, 2048], P('row', 'col'), may hold values from -1 to 1
- norm_moe: float32 [2048], replicated, may hold values from 0.5 to 1.5
- w_router: bfloat16 [2048, 16], replicated, may hold values from -0.09375 to 0.09375
- w_gate: bfloat16 [16, 2048, 1024], P(('dp', 'col'), None, 'row'), may hold values from -0.125 to 0.125
- w_up: bfloat16 [16, 2048, 1024], P(('dp', 'col'), None, 'row'), may hold values from -0.125 to 0.125
- w_down: bfloat16 [16, 1024, 2048], P(('dp', 'col'), 'row'), may hold values from -2 to 2
- routes: int32 [4096, 8], P(('dp', 'row', 'col')), may hold values from 0 to 15, all different within a row; in each aligned block of 128 rows (0 to 127, 128 to 255, ...) at most 128 rows name the same one
Outputs:
- block_out: bfloat16 [4096, 2048], P(('dp', 'row', 'col'))
- grad_input: float32 [4096, 2048], P(('dp', 'row', 'col'))
- grad_norm_attn: float32 [2048], replicated
- grad_query: float32 [2048, 2048], P('col', 'row')
- grad_key: float32 [2048, 2048], P('col', 'row')
- grad_value: float32 [2048, 2048], P('col', 'row')
- grad_query_gain: float32 [2048], replicated
- grad_key_gain: float32 [2048], replicated
- grad_out_proj: float32 [2048, 2048], P('row', 'col')
- grad_norm_moe: float32 [2048], replicated
- grad_router: float32 [2048, 16], replicated
- grad_gate: float32 [16, 2048, 1024], P(('dp', 'col'), None, 'row')
- grad_up: float32 [16, 2048, 1024], P(('dp', 'col'), None, 'row')
- grad_down: float32 [16, 1024, 2048], P(('dp', 'col'), 'row')
Inputs may be any that keep to these rules, and one draw needn't show every extreme that they name: `routes`: each row names 8 different experts. Among the 128 rows of one device no expert is named more than 128 times, and in some devices' rows one expert is named exactly 128 times.
All inputs are finite; a program needn't handle non-finite values.
Results may differ from a plain program's by a relative error of at most 0.019.
Values may be sent and summed in bfloat16 or wider, within the bound.
A program may use at most 320 MiB of HBM per device.

v0:
```python
import jax
import jax.numpy as jnp
from jax import lax
from jax.sharding import PartitionSpec as P

HEAD_DIM = 128
SEQ_LEN = 1024


EPSILON = 1e-05
THETA = 10000.0
MASKED = -1e30


def inverse_rms(values):
    return lax.rsqrt(jnp.mean(values * values, axis=-1, keepdims=True) + EPSILON)


def norm_backward(values, inv_scale, gain_row, upstream):
    weighted = gain_row * upstream
    inner_sum = jnp.sum(weighted * values, axis=-1, keepdims=True)
    grad_values = inv_scale * weighted - values * inv_scale**3 * inner_sum / values.shape[-1]
    return (grad_values, jnp.sum(upstream * values * inv_scale, axis=0))


def contract_rows(left, right):
    return lax.dot_general(
        left, right, (((0,), (0,)), ((), ())), preferred_element_type=jnp.float32
    )


def contract_cols(left, right):
    return lax.dot_general(
        left, right, (((1,), (1,)), ((), ())), preferred_element_type=jnp.float32
    )


def turn_tables(total_rows, seq_length, head_width):
    positions = (jnp.arange(total_rows) % seq_length).astype(jnp.float32)
    inverse = THETA ** (-jnp.arange(0, head_width, 2, dtype=jnp.float32) / head_width)
    angles = positions[:, None] * inverse[None, :]
    angles = jnp.concatenate([angles, angles], axis=-1)
    return (jnp.cos(angles)[:, None, :], jnp.sin(angles)[:, None, :])


def rotate(values, cosine, sine_table):
    middle = values.shape[-1] // 2
    turned = jnp.concatenate([-values[..., middle:], values[..., :middle]], axis=-1)
    return values * cosine + turned * sine_table


def unrotate(upstream, cosine, sine_table):
    middle = upstream.shape[-1] // 2
    turned_part = upstream * sine_table
    return upstream * cosine + jnp.concatenate(
        [turned_part[..., middle:], -turned_part[..., :middle]], axis=-1
    )


def attend_forward(pieces):
    queries, key_rows, value_rows = pieces
    length = queries.shape[0]
    block_rows = min(512, length)
    outputs = []
    sums_log = []
    for first_row in range(0, length, block_rows):
        finish = first_row + block_rows
        scores = jnp.einsum(
            "qhd,khd->hqk",
            queries[first_row:finish],
            key_rows[:finish],
            preferred_element_type=jnp.float32,
        )
        causal = (first_row + jnp.arange(block_rows))[:, None] >= jnp.arange(finish)[None, :]
        scores = jnp.where(causal[None], scores, MASKED)
        highest = jnp.max(scores, axis=-1, keepdims=True)
        weights = jnp.exp(scores - highest)
        totals = jnp.sum(weights, axis=-1, keepdims=True)
        weights = (weights / totals).astype(jnp.bfloat16)
        outputs.append(
            jnp.einsum(
                "hqk,khd->qhd", weights, value_rows[:finish], preferred_element_type=jnp.float32
            )
        )
        sums_log.append((highest + jnp.log(totals))[..., 0])
    return (jnp.concatenate(outputs, axis=0), jnp.concatenate(sums_log, axis=1))


def attend_backward(pieces):
    queries, key_rows, value_rows, grad_out, sums_log = pieces
    length = queries.shape[0]
    block_rows = min(512, length)
    grad_queries = []
    grad_keys = jnp.zeros(key_rows.shape, jnp.float32)
    grad_values = jnp.zeros(value_rows.shape, jnp.float32)
    for first_row in range(0, length, block_rows):
        finish = first_row + block_rows
        scores = jnp.einsum(
            "qhd,khd->hqk",
            queries[first_row:finish],
            key_rows[:finish],
            preferred_element_type=jnp.float32,
        )
        causal = (first_row + jnp.arange(block_rows))[:, None] >= jnp.arange(finish)[None, :]
        scores = jnp.where(causal[None], scores, MASKED)
        weights = jnp.exp(scores - sums_log[:, first_row:finish, None])
        grad_weights = jnp.einsum(
            "qhd,khd->hqk",
            grad_out[first_row:finish],
            value_rows[:finish],
            preferred_element_type=jnp.float32,
        )
        centre = jnp.sum(weights * grad_weights, axis=-1, keepdims=True)
        grad_scores = (weights * (grad_weights - centre)).astype(jnp.bfloat16)
        grad_queries.append(
            jnp.einsum(
                "hqk,khd->qhd", grad_scores, key_rows[:finish], preferred_element_type=jnp.float32
            )
        )
        grad_keys = grad_keys.at[:finish].add(
            jnp.einsum(
                "hqk,qhd->khd",
                grad_scores,
                queries[first_row:finish],
                preferred_element_type=jnp.float32,
            )
        )
        grad_values = grad_values.at[:finish].add(
            jnp.einsum(
                "hqk,qhd->khd",
                weights.astype(jnp.bfloat16),
                grad_out[first_row:finish],
                preferred_element_type=jnp.float32,
            )
        )
    return (jnp.concatenate(grad_queries, axis=0), grad_keys, grad_values)


def to_columns(payload):
    return lax.all_to_all(payload, "col", split_axis=1, concat_axis=0, tiled=True)


def to_blocks(payload):
    return lax.all_to_all(payload, "col", split_axis=0, concat_axis=1, tiled=True)


def token_gather(payload):
    return lax.all_gather(payload, "row", axis=0, tiled=True)


def token_reduce(payload):
    return lax.psum_scatter(payload, "row", scatter_dimension=0, tiled=True)


def heads_reduce(payload):
    return lax.psum_scatter(payload, "col", scatter_dimension=2, tiled=True)


def heads_gather(payload):
    return lax.all_gather(payload, "col", axis=2, tiled=True)


def head_norms(first_part, second_part):
    return lax.psum((first_part, second_part), ("row", "col"))


def dispatch(payload):
    return lax.all_to_all(payload, ("dp", "col"), split_axis=0, concat_axis=0, tiled=True)


def slot_gather(payload):
    return lax.all_gather(payload, "row", axis=0, tiled=True)


def slot_reduce(term_fn, count_rows):
    return lax.psum_scatter(
        term_fn(jnp.int32(0), count_rows * lax.axis_size("row")),
        "row",
        scatter_dimension=0,
        tiled=True,
    )


def per_device(
    hidden_in,
    cotangent,
    norm_attn,
    w_query,
    w_key,
    w_value,
    query_gain,
    key_gain,
    w_out,
    norm_moe,
    w_router,
    w_gate,
    w_up,
    w_down,
    routes,
):
    inputs = hidden_in.astype(jnp.float32)
    upstream = cotangent.astype(jnp.float32)
    token_count, top_count = routes.shape
    model_width = inputs.shape[1]
    inv_input = inverse_rms(inputs)
    normal_x = (inputs * inv_input * norm_attn).astype(jnp.bfloat16)
    gathered_x = token_gather(to_columns(normal_x))
    group_tokens = gathered_x.shape[0]
    stacked = jnp.stack(
        [
            jnp.dot(gathered_x, w_query, preferred_element_type=jnp.float32),
            jnp.dot(gathered_x, w_key, preferred_element_type=jnp.float32),
            jnp.dot(gathered_x, w_value, preferred_element_type=jnp.float32),
        ]
    )
    head_parts = heads_reduce(stacked)
    query_raw = head_parts[0]
    key_raw = head_parts[1]
    value_heads = head_parts[2].astype(jnp.bfloat16)
    local_width = query_raw.shape[1]
    head_count = local_width // HEAD_DIM
    query_square, key_square = head_norms(
        jnp.sum(query_raw * query_raw, axis=-1), jnp.sum(key_raw * key_raw, axis=-1)
    )
    inv_query = lax.rsqrt(query_square / model_width + EPSILON)[:, None]
    inv_key = lax.rsqrt(key_square / model_width + EPSILON)[:, None]
    offset = (lax.axis_index("row") * lax.axis_size("col") + lax.axis_index("col")) * local_width
    gain_query = lax.dynamic_slice_in_dim(query_gain, offset, local_width)
    gain_key = lax.dynamic_slice_in_dim(key_gain, offset, local_width)
    cosine, sine_table = turn_tables(group_tokens, SEQ_LEN, HEAD_DIM)
    head_shape = (group_tokens, head_count, HEAD_DIM)
    seq_shape = (group_tokens // SEQ_LEN, SEQ_LEN, head_count, HEAD_DIM)
    query_heads = (
        rotate((query_raw * inv_query * gain_query).reshape(head_shape), cosine, sine_table)
        * HEAD_DIM ** (-0.5)
    ).astype(jnp.bfloat16)
    key_heads = rotate(
        (key_raw * inv_key * gain_key).reshape(head_shape), cosine, sine_table
    ).astype(jnp.bfloat16)
    query_seq = query_heads.reshape(seq_shape)
    key_seq = key_heads.reshape(seq_shape)
    value_seq = value_heads.reshape(seq_shape)
    mixed, sums_log = lax.map(attend_forward, (query_seq, key_seq, value_seq))
    mixed_heads = mixed.reshape(group_tokens, local_width).astype(jnp.bfloat16)
    gathered_heads = heads_gather(mixed_heads[None])[0]
    attn_part = jnp.dot(gathered_heads, w_out, preferred_element_type=jnp.float32)
    state_rows = inputs + to_blocks(token_reduce(attn_part))
    inv_state = inverse_rms(state_rows)
    normal_h = (state_rows * inv_state * norm_moe).astype(jnp.bfloat16)
    logits = jnp.dot(normal_h, w_router, preferred_element_type=jnp.float32)
    expert_count = logits.shape[1]
    shifted = jnp.exp(logits - jnp.max(logits, axis=-1, keepdims=True))
    probabilities = shifted / jnp.sum(shifted, axis=-1, keepdims=True)
    selected = (routes[:, :, None] == jnp.arange(expert_count)[None, None, :]).astype(jnp.float32)
    route_prob = jnp.sum(selected * probabilities[:, None, :], axis=-1)
    capacity = 2 * token_count * top_count // expert_count
    flat_routes = routes.reshape(-1)
    route_onehot = (flat_routes[:, None] == jnp.arange(expert_count)[None, :]).astype(jnp.int32)
    slot_index = jnp.sum((jnp.cumsum(route_onehot, axis=0) - route_onehot) * route_onehot, axis=1)
    destination = flat_routes * capacity + slot_index
    route_total = token_count * top_count
    source = (
        jnp.full((expert_count * capacity,), route_total, jnp.int32)
        .at[destination]
        .set(jnp.arange(route_total, dtype=jnp.int32))
    )
    source_token = source // top_count
    padded_h = jnp.concatenate([normal_h, jnp.zeros((1, model_width), jnp.bfloat16)], axis=0)
    received = dispatch(padded_h[source_token])
    gate_use = w_gate[0]
    up_use = w_up[0]
    down_use = w_down[0]
    work_rows = slot_gather(received)
    gate_rows = jnp.dot(work_rows, gate_use, preferred_element_type=jnp.float32)
    up_rows = jnp.dot(work_rows, up_use, preferred_element_type=jnp.float32)
    sigmoid_gate = jax.nn.sigmoid(gate_rows)
    silu_gate = gate_rows * sigmoid_gate
    active = (silu_gate * up_rows).astype(jnp.bfloat16)

    def down_term(start_row, count_rows):
        piece_rows = lax.dynamic_slice_in_dim(active, start_row, count_rows, 0)
        return jnp.dot(piece_rows, down_use, preferred_element_type=jnp.float32)

    expert_out = slot_reduce(down_term, received.shape[0]).astype(jnp.bfloat16)
    returned = dispatch(expert_out)
    padded_back = jnp.concatenate([returned, jnp.zeros((1, model_width), jnp.bfloat16)], axis=0)
    route_out = (
        padded_back[destination].reshape(token_count, top_count, model_width).astype(jnp.float32)
    )
    mixture = jnp.sum(route_prob[:, :, None] * route_out, axis=1)
    block_out = (state_rows + mixture).astype(jnp.bfloat16)
    route_grad_prob = jnp.sum(upstream[:, None, :] * route_out, axis=-1)
    grad_probs = jnp.sum(selected * route_grad_prob[:, :, None], axis=1)
    grad_logits = (
        probabilities * (grad_probs - jnp.sum(probabilities * grad_probs, axis=-1, keepdims=True))
    ).astype(jnp.bfloat16)
    route_grad = (
        (route_prob[:, :, None] * upstream[:, None, :])
        .astype(jnp.bfloat16)
        .reshape(route_total, model_width)
    )
    padded_grad = jnp.concatenate([route_grad, jnp.zeros((1, model_width), jnp.bfloat16)], axis=0)
    grad_slots = dispatch(padded_grad[source])
    grad_rows = slot_gather(grad_slots)
    grad_active = contract_cols(grad_rows, down_use)
    grad_gate_rows = (
        grad_active * up_rows * sigmoid_gate * (1.0 + gate_rows * (1.0 - sigmoid_gate))
    ).astype(jnp.bfloat16)
    grad_up_rows = (grad_active * silu_gate).astype(jnp.bfloat16)
    grad_down_w = contract_rows(active, grad_rows)
    grad_gate_w = contract_rows(work_rows, grad_gate_rows)
    grad_up_w = contract_rows(work_rows, grad_up_rows)

    def entry_term(start_row, count_rows):
        gate_piece = lax.dynamic_slice_in_dim(grad_gate_rows, start_row, count_rows, 0)
        up_piece = lax.dynamic_slice_in_dim(grad_up_rows, start_row, count_rows, 0)
        return contract_cols(gate_piece, gate_use) + contract_cols(up_piece, up_use)

    entry_grad = slot_reduce(entry_term, grad_slots.shape[0]).astype(jnp.bfloat16)
    grad_gate_out = grad_gate_w[None]
    grad_up_out = grad_up_w[None]
    grad_down_out = grad_down_w[None]
    entry_back = dispatch(entry_grad)
    padded_entry = jnp.concatenate([entry_back, jnp.zeros((1, model_width), jnp.bfloat16)], axis=0)
    route_entry = (
        padded_entry[destination].reshape(token_count, top_count, model_width).astype(jnp.float32)
    )
    grad_normal_h = jnp.sum(route_entry, axis=1) + contract_cols(grad_logits, w_router)
    grad_router_part = contract_rows(normal_h, grad_logits)
    grad_state_part, grad_moe_part = norm_backward(state_rows, inv_state, norm_moe, grad_normal_h)
    grad_state = upstream + grad_state_part
    grad_attn = grad_state.astype(jnp.bfloat16)
    grad_gathered = token_gather(to_columns(grad_attn))
    grad_out_part = contract_rows(gathered_heads, grad_gathered)
    grad_heads_part = contract_cols(grad_gathered, w_out)
    grad_mixed = heads_reduce(grad_heads_part[None])[0].astype(jnp.bfloat16)
    grad_query_seq, grad_key_seq, grad_value_seq = lax.map(
        attend_backward, (query_seq, key_seq, value_seq, grad_mixed.reshape(seq_shape), sums_log)
    )
    grad_normal_q = unrotate(
        grad_query_seq.reshape(head_shape) * HEAD_DIM ** (-0.5), cosine, sine_table
    ).reshape(group_tokens, local_width)
    grad_normal_k = unrotate(grad_key_seq.reshape(head_shape), cosine, sine_table).reshape(
        group_tokens, local_width
    )
    weighted_q = gain_query * grad_normal_q
    weighted_k = gain_key * grad_normal_k
    inner_q, inner_k = head_norms(
        jnp.sum(weighted_q * query_raw, axis=-1), jnp.sum(weighted_k * key_raw, axis=-1)
    )
    grad_query_raw = (
        inv_query * weighted_q - query_raw * inv_query**3 * inner_q[:, None] / model_width
    )
    grad_key_raw = inv_key * weighted_k - key_raw * inv_key**3 * inner_k[:, None] / model_width
    grad_qgain_part = jnp.sum(grad_normal_q * query_raw * inv_query, axis=0)
    grad_kgain_part = jnp.sum(grad_normal_k * key_raw * inv_key, axis=0)
    grad_stack = jnp.stack(
        [grad_query_raw, grad_key_raw, grad_value_seq.reshape(group_tokens, local_width)]
    ).astype(jnp.bfloat16)
    gathered_grads = heads_gather(grad_stack)
    grad_query_part = contract_rows(gathered_x, gathered_grads[0])
    grad_key_part = contract_rows(gathered_x, gathered_grads[1])
    grad_value_part = contract_rows(gathered_x, gathered_grads[2])
    grad_x_part = (
        contract_cols(gathered_grads[0], w_query)
        + contract_cols(gathered_grads[1], w_key)
        + contract_cols(gathered_grads[2], w_value)
    )
    grad_normal_x = to_blocks(token_reduce(grad_x_part))
    grad_input_part, grad_attn_gain = norm_backward(inputs, inv_input, norm_attn, grad_normal_x)
    grad_input = grad_state + grad_input_part
    grad_query, grad_key, grad_value, grad_out_proj = lax.psum(
        (grad_query_part, grad_key_part, grad_value_part, grad_out_part), "dp"
    )
    full_width = query_gain.shape[0]
    padded_qgain = lax.dynamic_update_slice_in_dim(
        jnp.zeros((full_width,), jnp.float32), grad_qgain_part, offset, 0
    )
    padded_kgain = lax.dynamic_update_slice_in_dim(
        jnp.zeros((full_width,), jnp.float32), grad_kgain_part, offset, 0
    )
    grad_norm_attn, grad_query_gain, grad_key_gain, grad_norm_moe, grad_router = lax.psum(
        (grad_attn_gain, padded_qgain, padded_kgain, grad_moe_part, grad_router_part),
        ("dp", "row", "col"),
    )
    return (
        block_out,
        grad_input,
        grad_norm_attn,
        grad_query,
        grad_key,
        grad_value,
        grad_query_gain,
        grad_key_gain,
        grad_out_proj,
        grad_norm_moe,
        grad_router,
        grad_gate_out,
        grad_up_out,
        grad_down_out,
    )


def solution(mesh):
    placed = (
        P(("dp", "row", "col"), None),
        P(("dp", "row", "col"), None),
        P(),
        P("col", "row"),
        P("col", "row"),
        P("col", "row"),
        P(),
        P(),
        P("row", "col"),
        P(),
        P(),
        P(("dp", "col"), None, "row"),
        P(("dp", "col"), None, "row"),
        P(("dp", "col"), "row", None),
        P(("dp", "row", "col"), None),
    )
    return jax.shard_map(
        per_device,
        mesh=mesh,
        in_specs=placed,
        out_specs=(
            P(("dp", "row", "col"), None),
            P(("dp", "row", "col"), None),
            P(),
            P("col", "row"),
            P("col", "row"),
            P("col", "row"),
            P(),
            P(),
            P("row", "col"),
            P(),
            P(),
            P(("dp", "col"), None, "row"),
            P(("dp", "col"), None, "row"),
            P(("dp", "col"), "row", None),
        ),
        check_vma=False,
    )
```

profile of v0, /device:TPU:6, one launch (start us, length us, event | category | flops | bytes accessed | tf_op | source)
XLA Modules:
  0.0 1946.6 jit_solution(1046364304056410755)
XLA Ops:
  10.6 10.6 all_to_all.124
  21.2 10.6 all-gather.7.cloned.1.call-done
  37.0 4.9 pad_maximum_fusion
  43.8 3.1 broadcast_multiply_fusion.2
  48.1 114.7 %reduce-scatter.7.cloned.1.call-done = f32[3,1024,256]{2,1,0:T(8,128)} async-done(((f32[3,1024,1024]{2,1,0:T(8,128)}), f32[3,1024,256]{2,1,0:T(8,128)}) %reduce-scatter.7.cloned.1.call-update) | async-done | bytes 3145744 | tf_op jit(solution)/shard_map/reduce_scatter | solution.py:156
  165.8 2.6 fusion.119
  173.9 15.5 all-reduce.8
  201.5 35.5 %all-gather.9.cloned.1.call-done = bf16[1,1024,1024]{1,2,0:T(8,128)(2,1)} async-done(((bf16[1,1024,256]{1,2,0:T(8,128)(2,1)}), bf16[1,1024,1024]{1,2,0:T(8,128)(2,1)}) %all-gather.9.cloned.1.call-update) | async-done | bytes 2097168 | tf_op jit(solution)/shard_map/all_gather | solution.py:160
  237.0 4.2 fusion.21
  241.7 4.5 reduce-window.6
  246.6 5.6 reduce-scatter.9.cloned.1.call-done
  252.2 4.5 all-to-all-start.1
  257.4 4.3 scatter_custom_fusion
  261.8 7.9 all-to-all-done.1
  273.3 10.9 gather_fusion
  284.2 7.3 all-to-all-start.2
  292.6 167.3 %all-to-all-done.2 = bf16[16,128,2048]{2,1,0:T(8,128)(2,1)} async-done(((bf16[16,128,2048]{2,1,0:T(8,128)(2,1)}), bf16[16,128,2048]{2,1,0:T(8,128)(2,1)}, u32[]{:S(2)}, u32[]{:S(2)}) %all-to-all-start.2) | async-done | bytes 8388640 | tf_op jit(solution)/shard_map/all_to_all | solution.py:168
  466.2 19.1 gather_fusion.2
  485.4 207.8 %all_to_all.125 = bf16[16,128,2048]{2,1,0:T(8,128)(2,1)} all-to-all(bf16[16,128,2048]{2,1,0:T(8,128)(2,1)} %bitcast.235), channel_id=1, replica_groups=mesh['dp'=4,'row'=2,'col'=4] {'dp','col'}, dimensions={0} | all-to-all | bytes 16777216 | tf_op jit(solution)/shard_map/all_to_all | solution.py:168
  693.3 16.9 fusion.13
  712.6 11.1 fusion.17
  723.6 23.9 %multiply_convert_fusion = (bf16[4096,512]{1,0:T(8,128)(2,1)}, bf16[4096,512]{1,0:T(8,128)(2,1)}, bf16[4096,512]{1,0:T(8,128)(2,1)}) fusion(f32[4096,512]{1,0:T(8,128)} %fusion.17, f32[4096,512]{1,0:T(8,128)} %fusion.13, bf16[4096,2048]{1,0:T(8,128)(2,1)} %all-gather.13.cloned.1.call-done, bf16[1,512,2048]{2,1,0:T(8,128)(2,1)S(1)} %copy-done), kind=kOutput, calls=%fused_computation.14 | convolution fusion | flops 8621391872 | bytes 48234496 | tf_op jit(solution)/shard_map/dot_general | solution.py:33
  747.5 17.8 fusion.15
  765.3 28.2 %convolution_add_fusion = f32[4096,2048]{1,0:T(8,128)} fusion(f32[4096,2048]{1,0:T(8,128)} %fusion.15, bf16[4096,512]{1,0:T(8,128)(2,1)} %get-tuple-element.172, bf16[1,2048,512]{2,1,0:T(8,128)(2,1)} %param.39), kind=kOutput, calls=%fused_computation.5 | convolution fusion | flops 8598323200 | bytes 73400320 | tf_op jit(solution)/shard_map/dot_general | solution.py:33
  793.6 24.8 %fusion.10 = f32[4096,2048]{1,0:T(8,128)} fusion(bf16[4096,512]{1,0:T(8,128)(2,1)} %get-tuple-element.174, bf16[1,512,2048]{2,1,0:T(8,128)(2,1)S(1)} %copy-done), kind=kOutput, calls=%fused_computation.47 | convolution fusion | flops 8589934592 | bytes 39845888 | tf_op jit(solution)/shard_map/dot_general | solution.py:282
  818.4 21.4 %reduce-scatter.13.cloned.1.call-done = f32[2048,2048]{1,0:T(8,128)} async-done(((f32[4096,2048]{1,0:T(8,128)}), f32[2048,2048]{1,0:T(8,128)}) %reduce-scatter.13.cloned.1.call-update) | async-done | bytes 16777232 | tf_op jit(solution)/shard_map/reduce_scatter | solution.py:176
  839.8 9.1 convert_element_type.149
  848.9 6.9 all-to-all-start.5
  855.8 32.8 %reduce-scatter.11.cloned.1.call-done = f32[2048,2048]{1,0:T(8,128)} async-done(((f32[4096,2048]{1,0:T(8,128)}), f32[2048,2048]{1,0:T(8,128)}) %reduce-scatter.11.cloned.1.call-update) | async-done | bytes 16777232 | tf_op jit(solution)/shard_map/reduce_scatter | solution.py:176
  888.6 9.0 convert_element_type.141
  897.6 127.0 %all-to-all-done.5 = bf16[16,128,2048]{2,1,0:T(8,128)(2,1)} async-done(((bf16[16,128,2048]{2,1,0:T(8,128)(2,1)}), bf16[16,128,2048]{2,1,0:T(8,128)(2,1)}, u32[]{:S(2)}, u32[]{:S(2)}) %all-to-all-start.5) | async-done | bytes 8388640 | tf_op jit(solution)/shard_map/all_to_all | solution.py:168
  1024.6 28.3 %all-to-all-start.3 = ((bf16[16,128,2048]{2,1,0:T(8,128)(2,1)}), bf16[16,128,2048]{2,1,0:T(8,128)(2,1)}, u32[]{:S(2)}, u32[]{:S(2)}) async-start(bf16[16,128,2048]{2,1,0:T(8,128)(2,1)} %bitcast.232), calls=%async_computation.6 | async-start | bytes 16777216 | tf_op jit(solution)/shard_map/all_to_all | solution.py:168
  1052.9 8.4 concatenate.87
  1061.3 13.7 gather_fusion.3
  1075.0 5.0 convert_reduce_fusion
  1080.0 139.3 %all-to-all-done.3 = bf16[16,128,2048]{2,1,0:T(8,128)(2,1)} async-done(((bf16[16,128,2048]{2,1,0:T(8,128)(2,1)}), bf16[16,128,2048]{2,1,0:T(8,128)(2,1)}, u32[]{:S(2)}, u32[]{:S(2)}) %all-to-all-start.3) | async-done | bytes 8388640 | tf_op jit(solution)/shard_map/all_to_all | solution.py:168
  1219.3 8.4 concatenate.85
  1227.7 13.4 gather_fusion.1
  1241.1 5.9 fusion.1
  1247.8 3.1 fusion.118
  1250.9 9.0 all_to_all.126
  1260.0 31.6 %all-gather.15.cloned.1.call-done = bf16[1024,512]{1,0:T(8,128)(2,1)} async-done(((bf16[512,512]{1,0:T(8,128)(2,1)}), bf16[1024,512]{1,0:T(8,128)(2,1)}) %all-gather.15.cloned.1.call-update) | async-done | bytes 1048592 | tf_op jit(solution)/shard_map/all_gather | solution.py:148
  1291.7 4.5 convolution_bitcast_fusion.3
  1302.4 46.6 %reduce-scatter.15.cloned.1.call-done = f32[1,1024,256]{2,1,0:T(8,128)} async-done(((f32[1,1024,1024]{2,1,0:T(8,128)}), f32[1,1024,256]{2,1,0:T(8,128)}) %reduce-scatter.15.cloned.1.call-update) | async-done | bytes 1048592 | tf_op jit(solution)/shard_map/reduce_scatter | solution.py:156
  1360.7 5.8 multiply_reduce_fusion
  1370.9 4.4 multiply_convert_fusion.3
  1391.1 3.1 reshape.698
  1394.3 2.7 fusion.76
  1397.0 15.4 all-reduce.7
  1412.4 3.1 fusion.71
  1417.0 70.2 %all-gather.17.cloned.1.call-done = bf16[3,1024,1024]{2,1,0:T(8,128)(2,1)} async-done(((bf16[3,1024,256]{2,1,0:T(8,128)(2,1)}), bf16[3,1024,1024]{2,1,0:T(8,128)(2,1)}) %all-gather.17.cloned.1.call-update) | async-done | bytes 6291472 | tf_op jit(solution)/shard_map/all_gather | solution.py:160
  1487.2 3.0 fusion.31
  1495.8 4.2 fusion.19
  1500.0 4.2 fusion.32
  1504.2 4.3 fusion.30
  1508.5 4.2 fusion.28
  1512.7 15.1 convolution_bitcast_fusion.1
  1527.8 13.9 convolution_bitcast_fusion.2
  1541.7 5.5 all-to-all-start.7
  1547.2 15.0 convolution_bitcast_fusion
  1565.1 41.3 %all-reduce.6 = (f32[2048]{0:T(1024)}, f32[2048]{0:T(1024)}, f32[2048]{0:T(1024)}, f32[2048]{0:T(1024)}) all-reduce(f32[2048]{0:T(1024)S(1)} %get-tuple-element.152, f32[2048]{0:T(1024)S(1)} %dynamic_update_slice.18, f32[2048]{0:T(1024)S(1)} %bitcast_dynamic-update-slice_fusion, ...), channel_id=1, replica_groups=mesh['dp'=4,'row'=2,'col'=4] {'dp','row','col'}, use_global_device_ids=true, to_apply=%region_37.38 | all-reduce | flops 8192 | bytes 65536 | tf_op jit(solution)/shard_map/psum | solution.py:382
  1607.9 28.0 %all-reduce.13.cloned.1.call-done = f32[2048,16]{0,1:T(8,128)} async-done(((f32[2048,16]{0,1:T(8,128)}), f32[2048,16]{0,1:T(8,128)}) %all-reduce.13.cloned.1.call-update) | async-done | bytes 131088 | tf_op jit(solution)/shard_map/psum | solution.py:382
  1635.9 295.6 %all-reduce.15.cloned.1.call-done = (f32[512,1024]{1,0:T(8,128)}, f32[512,1024]{1,0:T(8,128)}, f32[512,1024]{1,0:T(8,128)}, f32[1024,512]{1,0:T(8,128)}) async-done(((f32[512,1024]{1,0:T(8,128)}, f32[512,1024]{1,0:T(8,128)}, f32[512,1024]{1,0:T(8,128)}, f32[1024,512]{1,0:T(8,128)}), (f32[512,1024]{1,0:T(8,128)}, f32[512,1024]{1,0:T(8,128)}, f32[512,1024]{1,0:T(8,128)}, ...) | async-done | bytes 8388624 | tf_op jit(solution)/shard_map/psum | solution.py:372
  1931.4 3.3 copy.300
  (358 shorter events, 101.6 us)
Async XLA Ops:
  7.2 716.5 %copy-start = (bf16[1,512,2048]{2,1,0:T(8,128)(2,1)S(1)}, bf16[1,512,2048]{2,1,0:T(8,128)(2,1)}, u32[]{:S(2)}) copy-start(bf16[1,512,2048]{2,1,0:T(8,128)(2,1)} %param.40) | copy-start | bytes 6291460
  7.2 24.6 %copy-start.52 = (bf16[512,1024]{1,0:T(8,128)(2,1)S(1)}, bf16[512,1024]{1,0:T(8,128)(2,1)}, u32[]{:S(2)}) copy-start(bf16[512,1024]{1,0:T(8,128)(2,1)} %param.32) | copy-start | bytes 3145732
  7.2 24.6 %all-gather.7.cloned.1.call-start = ((), (), s32[]{:S(2)}) async-start(), calls=%async_computation.14 | async-start | bytes 1572864 | tf_op jit(solution)/shard_map/all_gather | solution.py:148
  9.3 11.9 copy-start.87
  21.2 141.6 %reduce-scatter.7.cloned.1.call-start = ((), (), s32[]{:S(2)}) async-start(), calls=%async_computation.15 | async-start | bytes 15728640 | tf_op jit(solution)/shard_map/reduce_scatter | solution.py:156
  41.9 195.1 %all-gather.9.cloned.1.call-start = ((), (), s32[]{:S(2)}) async-start(), calls=%async_computation.16 | async-start | bytes 2621440 | tf_op jit(solution)/shard_map/all_gather | solution.py:160
  43.6 152.6 %copy-start.22 = (pred[512,512]{0,1:T(8,128)(4,1)}, pred[512,512]{0,1:T(8,128)(4,1)S(1)}, u32[]{:S(2)}) copy-start(pred[512,512]{0,1:T(8,128)(4,1)S(1)} %iota_compare_fusion.1) | copy-start | bytes 786436
  171.7 20.7 %copy-start.8 = (f32[1024,2,128]{2,1,0:T(2,128)}, f32[1024,2,128]{2,1,0:T(2,128)S(1)}, u32[]{:S(2)}) copy-start(f32[1024,2,128]{2,1,0:T(2,128)S(1)} %squeeze.60) | copy-start | bytes 3145732
  199.1 37.9 %copy-start.95 = (bf16[1024,512]{1,0:T(8,128)(2,1)S(1)}, bf16[1024,512]{1,0:T(8,128)(2,1)}, u32[]{:S(2)}) copy-start(bf16[1024,512]{1,0:T(8,128)(2,1)} %param.35) | copy-start | bytes 3145732
  201.5 39.7 %copy-start.70 = (s32[128,8]{0,1:T(8,128)S(1)}, s32[128,8]{0,1:T(8,128)}, u32[]{:S(2)}) copy-start(s32[128,8]{0,1:T(8,128)} %param.41) | copy-start | bytes 12292
  201.5 50.7 %reduce-scatter.9.cloned.1.call-start = ((), (), s32[]{:S(2)}) async-start(), calls=%async_computation.17 | async-start | bytes 3145728 | tf_op jit(solution)/shard_map/reduce_scatter | solution.py:152
  241.2 29.8 %copy-start.12 = (bf16[128,2048]{1,0:T(8,128)(2,1)S(1)}, bf16[128,2048]{1,0:T(8,128)(2,1)}, u32[]{:S(2)}) copy-start(bf16[128,2048]{1,0:T(8,128)(2,1)} %param.27) | copy-start | bytes 1572868
  241.2 31.0 %copy-start.67 = (f32[2048]{0:T(1024)S(1)}, f32[2048]{0:T(1024)}, u32[]{:S(2)}) copy-start(f32[2048]{0:T(1024)} %param.36) | copy-start | bytes 24580
  252.2 17.5 all-to-all-start.1
  271.8 12.3 copy-start.89
  284.2 175.8 %all-to-all-start.2 = ((bf16[16,128,2048]{2,1,0:T(8,128)(2,1)}), bf16[16,128,2048]{2,1,0:T(8,128)(2,1)}, u32[]{:S(2)}, u32[]{:S(2)}) async-start(bf16[16,128,2048]{2,1,0:T(8,128)(2,1)} %bitcast.234), calls=%async_computation.4 | async-start | bytes 16777216 | tf_op jit(solution)/shard_map/all_to_all | solution.py:168
  291.4 401.8 %all-gather.11.cloned.1.call-start = ((), (), s32[]{:S(2)}) async-start(), calls=%async_computation.18 | async-start | bytes 25165824 | tf_op jit(solution)/shard_map/all_gather | solution.py:172
  292.6 170.3 %copy-start.17 = (f32[128,2048]{1,0:T(8,128)}, f32[128,2048]{1,0:T(8,128)S(1)}, u32[]{:S(2)}) copy-start(f32[128,2048]{1,0:T(8,128)S(1)} %convert_element_type.145) | copy-start | bytes 3145732
  460.0 263.7 %all-gather.13.cloned.1.call-start = ((), (), s32[]{:S(2)}) async-start(), calls=%async_computation.20 | async-start | bytes 25165824 | tf_op jit(solution)/shard_map/all_gather | solution.py:172
  693.2 146.6 %reduce-scatter.13.cloned.1.call-start = ((), (), s32[]{:S(2)}) async-start(), calls=%async_computation.21 | async-start | bytes 50331648 | tf_op jit(solution)/shard_map/reduce_scatter | solution.py:176
  693.3 18.4 copy-start.93
  693.3 19.3 copy-start.94
  793.5 95.0 %reduce-scatter.11.cloned.1.call-start = ((), (), s32[]{:S(2)}) async-start(), calls=%async_computation.19 | async-start | bytes 50331648 | tf_op jit(solution)/shard_map/reduce_scatter | solution.py:176
  848.9 175.7 %all-to-all-start.5 = ((bf16[16,128,2048]{2,1,0:T(8,128)(2,1)}), bf16[16,128,2048]{2,1,0:T(8,128)(2,1)}, u32[]{:S(2)}, u32[]{:S(2)}) async-start(bf16[16,128,2048]{2,1,0:T(8,128)(2,1)} %bitcast.233), calls=%async_computation.9 | async-start | bytes 16777216 | tf_op jit(solution)/shard_map/all_to_all | solution.py:168
  1024.6 28.3 %copy-start.82 = (s32[1024,1]{0,1:T(1,128)S(1)}, s32[1024,1]{0,1:T(1,128)}, u32[]{:S(2)}) copy-start(s32[1024,1]{0,1:T(1,128)} %get-tuple-element.198) | copy-start | bytes 12292
  1024.6 194.7 %all-to-all-start.3 = ((bf16[16,128,2048]{2,1,0:T(8,128)(2,1)}), bf16[16,128,2048]{2,1,0:T(8,128)(2,1)}, u32[]{:S(2)}, u32[]{:S(2)}) async-start(bf16[16,128,2048]{2,1,0:T(8,128)(2,1)} %bitcast.232), calls=%async_computation.6 | async-start | bytes 16777216 | tf_op jit(solution)/shard_map/all_to_all | solution.py:168
  1052.8 238.8 %all-gather.15.cloned.1.call-start = ((), (), s32[]{:S(2)}) async-start(), calls=%async_computation.22 | async-start | bytes 1572864 | tf_op jit(solution)/shard_map/all_gather | solution.py:148
  1227.7 13.4 copy-start.18
  1227.7 13.4 copy-start.56
  1241.1 6.1 copy-start.61
  1241.1 6.1 copy-start.84
  1241.1 6.1 copy-start.86
  1241.1 6.1 copy-start.7
  1241.1 6.1 copy-start.59
  1241.1 6.1 copy-start.68
  1241.1 6.1 copy-start.90
  1241.1 6.7 copy-start.92
  1247.8 43.8 %copy-start.96 = (bf16[1024,512]{1,0:T(8,128)(2,1)S(1)}, bf16[1024,512]{1,0:T(8,128)(2,1)}, u32[]{:S(2)}) copy-start(bf16[1024,512]{1,0:T(8,128)(2,1)} %param.35) | copy-start | bytes 3145732
  1260.0 89.1 %reduce-scatter.15.cloned.1.call-start = ((), (), s32[]{:S(2)}) async-start(), calls=%async_computation.23 | async-start | bytes 5242880 | tf_op jit(solution)/shard_map/reduce_scatter | solution.py:156
  1296.2 6.2 copy-start.73
  1296.2 6.2 copy-start.79
  1296.2 6.2 copy-start.75
  1296.2 6.2 copy-start.81
  1296.2 56.7 %copy-start.5 = (f32[2,512,512]{1,2,0:T(8,128)S(1)}, f32[2,512,512]{1,2,0:T(8,128)}, u32[]{:S(2)}) copy-start(f32[2,512,512]{1,2,0:T(8,128)} %copy-done.4) | copy-start | bytes 6291460
  1296.2 56.7 %copy-start.23 = (pred[512,512]{0,1:T(8,128)(4,1)S(1)}, pred[512,512]{0,1:T(8,128)(4,1)}, u32[]{:S(2)}) copy-start(pred[512,512]{0,1:T(8,128)(4,1)} %copy-done.22) | copy-start | bytes 786436
  1296.3 190.9 %all-gather.17.cloned.1.call-start = ((), (), s32[]{:S(2)}) async-start(), calls=%async_computation.24 | async-start | bytes 7864320 | tf_op jit(solution)/shard_map/all_gather | solution.py:160
  1300.6 54.8 %copy-start.19 = (f32[1024,2,128]{2,1,0:T(2,128)}, f32[1024,2,128]{2,1,0:T(2,128)S(1)}, u32[]{:S(2)}) copy-start(f32[1024,2,128]{2,1,0:T(2,128)S(1)} %mul.612) | copy-start | bytes 3145732
  1358.3 11.6 copy-start.24
  1391.1 21.3 %copy-start.40 = (f32[1,1024,256]{2,1,0:T(8,128)S(1)}, f32[1,1024,256]{2,1,0:T(8,128)}, u32[]{:S(2)}) copy-start(f32[1,1024,256]{2,1,0:T(8,128)} %mul.613) | copy-start | bytes 3145732
  1391.1 21.3 %copy-start.76 = (f32[1024]{0:T(1024)S(1)}, f32[1024]{0:T(1024)}, u32[]{:S(2)}) copy-start(f32[1024]{0:T(1024)} %get-tuple-element.202) | copy-start | bytes 12292
  1391.1 21.3 %copy-start.77 = (f32[1024]{0:T(1024)S(1)}, f32[1024]{0:T(1024)}, u32[]{:S(2)}) copy-start(f32[1024]{0:T(1024)} %get-tuple-element.222) | copy-start | bytes 12292
  1397.0 18.6 copy-start.50
  1415.5 71.6 %copy-start.98 = (bf16[512,1024]{1,0:T(8,128)(2,1)S(1)}, bf16[512,1024]{1,0:T(8,128)(2,1)}, u32[]{:S(2)}) copy-start(bf16[512,1024]{1,0:T(8,128)(2,1)} %param.31) | copy-start | bytes 3145732
  1416.9 73.3 %copy-start.100 = (bf16[512,1024]{1,0:T(8,128)(2,1)S(1)}, bf16[512,1024]{1,0:T(8,128)(2,1)}, u32[]{:S(2)}) copy-start(bf16[512,1024]{1,0:T(8,128)(2,1)} %param.30) | copy-start | bytes 3145732
  1416.9 124.7 %reduce-scatter.17.cloned.1.call-start = ((), (), s32[]{:S(2)}) async-start(), calls=%async_computation.25 | async-start | bytes 3145728 | tf_op jit(solution)/shard_map/reduce_scatter | solution.py:152
  1494.5 141.3 %all-reduce.13.cloned.1.call-start = ((), (), s32[]{:S(2)}) async-start(), calls=%async_computation.26 | async-start | bytes 262144 | tf_op jit(solution)/shard_map/psum | solution.py:382
  1495.5 436.0 %all-reduce.15.cloned.1.call-start = ((), (), s32[]{:S(2)}) async-start(), calls=%async_computation.27 | async-start | bytes 16777216 | tf_op jit(solution)/shard_map/psum | solution.py:372
  1512.7 15.1 copy-start.102
  1541.7 20.9 %all-to-all-start.7 = ((f32[4,128,512]{2,1,0:T(8,128)}), f32[4,128,512]{2,1,0:T(8,128)S(1)}, u32[]{:S(2)}, u32[]{:S(2)}) async-start(f32[4,128,512]{2,1,0:T(8,128)} %bitcast.261), calls=%async_computation.13 | async-start | bytes 2097152 | tf_op jit(solution)/shard_map/all_to_all | solution.py:144
  1547.2 17.7 copy-start.13
  1547.2 17.7 copy-start.69
  1547.2 17.7 copy-start.88
  1547.2 59.3 %copy-start.91 = (f32[128]{0:T(128)S(1)}, f32[128]{0:T(128)}, u32[]{:S(2)}) copy-start(f32[128]{0:T(128)} %get-tuple-element.204) | copy-start | bytes 1540
  1562.2 44.3 %copy-start.39 = (f32[128,2048]{1,0:T(8,128)S(1)}, f32[128,2048]{1,0:T(8,128)}, u32[]{:S(2)}) copy-start(f32[128,2048]{1,0:T(8,128)} %get-tuple-element.169) | copy-start | bytes 3145732
  (58 other events, 159.4 us)
Sparse Core Ops, SparseCore 0:
  21.3 10.4 all-gather.6
  42.0 120.7 reduce-scatter.6
  201.6 35.3 all-gather.8
  241.3 10.8 reduce-scatter.8
  460.1 51.3 all-gather.10
  693.3 30.0 all-gather.12
  793.6 46.0 reduce-scatter.12
  842.2 46.3 reduce-scatter.10
  1260.1 31.5 all-gather.14
  1296.4 52.6 reduce-scatter.14
  1417.0 70.0 all-gather.16
  1494.7 10.7 reduce-scatter.16
  1512.5 123.3 all-reduce.12
  1639.4 291.9 all-reduce.14
where the time goes:
time: 1960 us; the launch traced here: 1950 us
  waiting for transfers between devices  1130 us (58%)
  blocking collectives  300 us (15%)
  matrix products  226 us (12%)
  local copies, waits for them, and re-layouts  136 us (7%)
  other arithmetic  80.2 us (4%)
  starting transfers between devices  53.9 us (3%)
    all_to_all x3, waiting for transfers between devices, dispatch(): lax.all_to_all(payload, ('dp', 'col'), split_axis=0, concat_axis=0, tiled...  434 us
    psum x1, waiting for transfers between devices, per_device(): lax.psum((grad_query_part, grad_key_part, grad_value_part, grad_out_part)...  296 us
    all_to_all x1, blocking collectives, dispatch(): lax.all_to_all(payload, ('dp', 'col'), split_axis=0, concat_axis=0, tiled...  208 us
    reduce_scatter x2, waiting for transfers between devices, heads_reduce(): return lax.psum_scatter(payload, 'col', scatter_dimension=2, tiled=True)  161 us
    all_gather x2, waiting for transfers between devices, heads_gather(): return lax.all_gather(payload, 'col', axis=2, tiled=True)  106 us
    dot_general x8, matrix products, contract_cols(): lax.dot_general(left, right, (((1,), (1,)), ((), ())), preferred_element_...  81.9 us
    dot_general x8, matrix products, contract_rows(): lax.dot_general(left, right, (((0,), (0,)), ((), ())), preferred_element_...  61.6 us
    reduce_scatter x2, waiting for transfers between devices, slot_reduce(): lax.psum_scatter(term_fn(jnp.int32(0), count_rows * lax.axis_size('row'))...  54.1 us
  transfers between devices with their start and end apart: 19, of which 15 were waited for; matrix products, arithmetic and copies ran while one was open for 11% of the time, Pallas kernels for 0%

commit v1 on v0

v1 whole, which is shorter than its diff:
```python
import functools

import jax
import jax.numpy as jnp
from jax import lax
from jax.experimental import pallas as pl
from jax.experimental.pallas import tpu as pltpu
from jax.sharding import PartitionSpec as P

MESH = pl.DeviceIdType.MESH
ANYSPEC = pl.BlockSpec(memory_space=pl.ANY)

def place():
    return lax.axis_index("dp"), lax.axis_index("row"), lax.axis_index("col")

def greet(peers):
    barrier = pltpu.get_barrier_semaphore()
    for peer in peers:
        pl.semaphore_signal(barrier, inc=1, device_id=peer, device_id_type=MESH)
    pl.semaphore_wait(barrier, len(peers))

def gather_kernel(planes, parts, count, *refs):
    ins, outs = refs[:count], refs[count:2 * count]
    own_sem, send_sem, recv_sem = refs[2 * count:]
    z, r, c = place()
    first, second, diag = c ^ (1 + r), c ^ (2 - r), c ^ 3
    partner = (z, 1 - r, c)
    to_first, to_second = (z, r, first), (z, r, second)
    greet([to_first, to_second, partner] + [(z ^ k, r, c) for k in range(1, planes)])
    pieces = []
    for a in range(count):
        cut = parts if a == 0 else 1
        pieces += [(a, p, ins[a].shape[0], ins[a].shape[0] // cut) for p in range(cut)]

    def number(zz, rr, cc):
        return ((zz if planes > 1 else 0) * 2 + rr) * 4 + cc

    def place_of(i, which):
        a, p, depth, cut = pieces[i]
        return outs[a].at[pl.ds(pl.multiple_of(which * depth + p * cut, cut), cut)]

    sent = [[] for _ in pieces]

    def send(i, which, target, own=False):
        a, p, depth, cut = pieces[i]
        spot = place_of(i, which)
        copy = pltpu.make_async_remote_copy(
            src_ref=ins[a].at[pl.ds(p * cut, cut)] if own else spot, dst_ref=spot,
            send_sem=send_sem.at[i, len(sent[i])], recv_sem=recv_sem.at[i, which],
            device_id=target, device_id_type=MESH)
        copy.start()
        sent[i].append(copy)

    def await_block(i, which):
        spot = place_of(i, which)
        pltpu.make_async_remote_copy(
            src_ref=spot, dst_ref=spot, send_sem=send_sem.at[i, 0], recv_sem=recv_sem.at[i, which],
            device_id=partner, device_id_type=MESH).wait_recv()

    mine = number(z, r, c)
    keeps = []
    every = range(len(pieces))
    for i in every:
        for target in [to_first, to_second] + [(z ^ k, r, c) for k in range(1, planes)] + [partner]:
            send(i, mine, target, True)
    for a in range(count):
        keep = pltpu.make_async_copy(ins[a], outs[a].at[pl.ds(pl.multiple_of(mine * ins[a].shape[0], ins[a].shape[0]), ins[a].shape[0])], own_sem.at[a])
        keep.start()
        keeps.append(keep)

    def forward(which, targets):
        for i in every:
            await_block(i, which)
            for target in targets:
                send(i, which, target)

    for step in range(planes + 2):
        if 0 < step < planes:
            forward(number(z ^ step, r, c), [to_first, to_second, partner])
        if 0 <= step - 1 < planes:
            forward(number(z ^ (step - 1), r, first), [to_second, partner])
            forward(number(z ^ (step - 1), r, second), [partner])
        if 0 <= step - 2 < planes:
            forward(number(z ^ (step - 2), r, diag), [partner])
    for k in range(planes):
        for j in range(4):
            for i in every:
                await_block(i, number(z ^ k, 1 - r, c ^ j))
    for keep in keeps:
        keep.wait()
    for copies in sent:
        for copy in copies:
            copy.wait_send()

def gather(arrays, planes, collective_id, parts=1):
    count = len(arrays)
    blocks = planes * 8
    sends = (3 + planes - 1) + (planes - 1) * 3 + planes * 4
    pieces = count - 1 + parts
    return pl.pallas_call(
        functools.partial(gather_kernel, planes, parts, count),
        out_shape=[jax.ShapeDtypeStruct((blocks * a.shape[0],) + a.shape[1:], a.dtype) for a in arrays],
        in_specs=[ANYSPEC] * count, out_specs=[ANYSPEC] * count,
        scratch_shapes=[pltpu.SemaphoreType.DMA((count,)), pltpu.SemaphoreType.DMA((pieces, sends)), pltpu.SemaphoreType.DMA((pieces, blocks))],
        compiler_params=pltpu.CompilerParams(collective_id=collective_id, has_side_effects=True),
    )(*arrays)

def reduce_kernel(planes, count, *refs):
    parts, outs = refs[:count], refs[count:2 * count]
    held, fromp, relay, near, far = (refs[(2 + i) * count:(3 + i) * count] for i in range(5))
    load_sem, pair_send, pair_recv, send_sem, relay_recv, near_recv, far_recv = refs[7 * count:]
    z, r, c = place()
    first, second, diag = c ^ (1 + r), c ^ (2 - r), c ^ 3
    partner = (z, 1 - r, c)
    to_first, to_second = (z, r, first), (z, r, second)
    greet([to_first, to_second, partner] + [(z ^ k, r, c) for k in range(1, planes)])
    depth = outs[0].shape[0]
    every = range(count)

    def rows(a, zz, rr, cc):
        which = ((zz if planes > 1 else 0) * 2 + rr) * 4 + cc
        return parts[a].at[pl.ds(pl.multiple_of(which * depth, depth), depth)]

    columns, partner_columns = [c, first, second, diag], [c, second, first, diag]
    loads, pairs = {}, {}
    for k in reversed(range(planes)):
        for j in (3, 2, 1, 0):
            for a in every:
                load = pltpu.make_async_copy(rows(a, z ^ k, r, columns[j]), held[a].at[k, j], load_sem.at[a, k, j])
                load.start()
                pair = pltpu.make_async_remote_copy(
                    src_ref=rows(a, z ^ k, 1 - r, partner_columns[j]), dst_ref=fromp[a].at[k, j],
                    send_sem=pair_send.at[a, k, j], recv_sem=pair_recv.at[a, k, j], device_id=partner, device_id_type=MESH)
                pair.start()
                loads[a, k, j], pairs[a, k, j] = load, pair
    step_rows = 32

    def add(target, sources):
        def body(i, _):
            at = pl.ds(pl.multiple_of(i * step_rows, step_rows), step_rows)
            total = sources[0][at].astype(jnp.float32)
            for source in sources[1:]:
                total = total + source[at].astype(jnp.float32)
            target[at] = total.astype(target.dtype)
            return 0
        lax.fori_loop(0, depth // step_rows, body, 0)

    sent = [[] for _ in every]

    def send(a, source, target, recv, device):
        copy = pltpu.make_async_remote_copy(
            src_ref=source, dst_ref=target, send_sem=send_sem.at[a, len(sent[a])], recv_sem=recv,
            device_id=device, device_id_type=MESH)
        copy.start()
        sent[a].append(copy)

    def await_in(a, target, recv):
        pltpu.make_async_remote_copy(
            src_ref=target, dst_ref=target, send_sem=send_sem.at[a, 0], recv_sem=recv,
            device_id=partner, device_id_type=MESH).wait_recv()

    def ready(a, k, j):
        loads[a, k, j].wait()
        pairs[a, k, j].wait_recv()

    def to_relay(k):
        for j in (3, 2):
            for a in every:
                ready(a, k, j)
                mine = held[a].at[k, j]
                add(mine, [mine, fromp[a].at[k, j]])
                if j == 3:
                    send(a, mine, relay[a].at[k], relay_recv.at[a, k], to_second)
                else:
                    send(a, mine, near[a].at[k, 1], near_recv.at[a, k, 1], to_second)

    def pass_on(k):
        for a in every:
            ready(a, k, 1)
            await_in(a, relay[a].at[k], relay_recv.at[a, k])
            mine = held[a].at[k, 1]
            add(mine, [mine, fromp[a].at[k, 1], relay[a].at[k]])
            send(a, mine, near[a].at[k, 0], near_recv.at[a, k, 0], to_first)

    def collect(k):
        for a in every:
            ready(a, k, 0)
            await_in(a, near[a].at[k, 0], near_recv.at[a, k, 0])
            await_in(a, near[a].at[k, 1], near_recv.at[a, k, 1])
            mine = held[a].at[k, 0]
            terms = [mine, fromp[a].at[k, 0], near[a].at[k, 0], near[a].at[k, 1]]
            if k > 0:
                add(mine, terms)
                send(a, mine, far[a].at[k - 1], far_recv.at[a, k - 1], (z ^ k, r, c))
            else:
                for i in range(planes - 1):
                    await_in(a, far[a].at[i], far_recv.at[a, i])
                add(outs[a], terms + [far[a].at[i] for i in range(planes - 1)])

    order = list(reversed(range(planes)))
    for step in range(planes + 2):
        if step < planes:
            to_relay(order[step])
        if 0 <= step - 1 < planes:
            pass_on(order[step - 1])
        if 0 <= step - 2 < planes:
            collect(order[step - 2])
    for copies in sent:
        for copy in copies:
            copy.wait_send()
    for pair in pairs.values():
        pair.wait_send()


def reduce_scatter(partials, planes, collective_id):
    count, blocks = len(partials), planes * 8
    shapes = [((p.shape[0] // blocks, p.shape[1]), p.dtype) for p in partials]
    sends, far = planes * 4 - 1, max(planes - 1, 1)
    scratch = [pltpu.VMEM(lead + shape, kind) for lead in ((planes, 4), (planes, 4), (planes,), (planes, 2), (far,)) for shape, kind in shapes]
    dma = pltpu.SemaphoreType.DMA
    return pl.pallas_call(
        functools.partial(reduce_kernel, planes, count),
        out_shape=[jax.ShapeDtypeStruct(shape, jnp.float32) for shape, _ in shapes],
        in_specs=[ANYSPEC] * count, out_specs=[pl.BlockSpec(memory_space=pltpu.VMEM)] * count,
        scratch_shapes=scratch + [
            dma((count, planes, 4)), dma((count, planes, 4)), dma((count, planes, 4)), dma((count, sends)),
            dma((count, planes)), dma((count, planes, 2)), dma((count, far))],
        compiler_params=pltpu.CompilerParams(collective_id=collective_id, has_side_effects=True, vmem_limit_bytes=48 * 2**20),
    )(*partials)


def exchange_kernel(wq_ref, wk_ref, wv_ref, wo_ref, proj_ref, out_ref, own_sem, send_sem, recv_sem):
    z, r, c = place()
    width = proj_ref.shape[1] // 3
    depth = wq_ref.shape[0]
    out_rows, out_width = out_ref.shape[0], wo_ref.shape[1]
    greet([(z, r, c ^ j) for j in range(1, 4)])

    def source(a, target):
        if a < 3:
            return (wq_ref, wk_ref, wv_ref)[a].at[:, pl.ds(pl.multiple_of(target * width, width), width)]
        return wo_ref.at[pl.ds(pl.multiple_of(target * out_rows, out_rows), out_rows), :]

    def spot(a, origin):
        if a < 3:
            return proj_ref.at[pl.ds(pl.multiple_of(origin * depth, depth), depth), pl.ds(a * width, width)]
        return out_ref.at[:, pl.ds(pl.multiple_of(origin * out_width, out_width), out_width)]

    waits = []
    for a in range(4):
        keep = pltpu.make_async_copy(source(a, c), spot(a, c), own_sem.at[a])
        keep.start()
        waits.append(keep.wait)
        for j in range(1, 4):
            copy = pltpu.make_async_remote_copy(
                src_ref=source(a, c ^ j), dst_ref=spot(a, c), send_sem=send_sem.at[a, j - 1],
                recv_sem=recv_sem.at[a, j - 1], device_id=(z, r, c ^ j), device_id_type=MESH)
            copy.start()
            waits.append(copy.wait_send)
    for a in range(4):
        for j in range(1, 4):
            arrived = spot(a, c ^ j)
            pltpu.make_async_remote_copy(
                src_ref=arrived, dst_ref=arrived, send_sem=send_sem.at[a, j - 1], recv_sem=recv_sem.at[a, j - 1],
                device_id=(z, r, c ^ j), device_id_type=MESH).wait_recv()
    for wait in waits:
        wait()


def exchange_weights(w_query, w_key, w_value, w_out, collective_id):
    depth, half = w_query.shape
    kind = w_query.dtype
    width, out_rows, out_width = half // 4, w_out.shape[0] // 4, w_out.shape[1] * 4
    return pl.pallas_call(
        exchange_kernel,
        out_shape=[jax.ShapeDtypeStruct((depth * 4, 3 * width), kind), jax.ShapeDtypeStruct((out_rows, out_width), kind)],
        in_specs=[ANYSPEC] * 4, out_specs=[ANYSPEC] * 2,
        scratch_shapes=[pltpu.SemaphoreType.DMA((4,)), pltpu.SemaphoreType.DMA((4, 3)), pltpu.SemaphoreType.DMA((4, 3))],
        compiler_params=pltpu.CompilerParams(collective_id=collective_id, has_side_effects=True),
    )(w_query, w_key, w_value, w_out)


def total_kernel(value_ref, out_ref, slots, send_sem, recv_sem):
    z, r, c = place()
    peers = [(z, r ^ (j >> 2), c ^ (j & 3)) for j in range(1, 8)]
    greet(peers)
    copies = []
    for j, peer in enumerate(peers):
        copy = pltpu.make_async_remote_copy(
            src_ref=value_ref, dst_ref=slots.at[j], send_sem=send_sem.at[j], recv_sem=recv_sem.at[j],
            device_id=peer, device_id_type=MESH)
        copy.start()
        copies.append(copy)
    for copy in copies:
        copy.wait()
    here = r * 4 + c
    total = jnp.zeros(value_ref.shape, jnp.float32)
    for who in range(8):
        which = here ^ who
        term = jnp.where(which == 0, value_ref[...], slots[jnp.maximum(which - 1, 0)])
        total = total + term
    out_ref[...] = total


def group_total(value, collective_id):
    return pl.pallas_call(
        total_kernel,
        out_shape=jax.ShapeDtypeStruct(value.shape, jnp.float32),
        in_specs=[pl.BlockSpec(memory_space=pltpu.VMEM)], out_specs=pl.BlockSpec(memory_space=pltpu.VMEM),
        scratch_shapes=[pltpu.VMEM((7,) + value.shape, jnp.float32), pltpu.SemaphoreType.DMA((7,)), pltpu.SemaphoreType.DMA((7,))],
        compiler_params=pltpu.CompilerParams(collective_id=collective_id, has_side_effects=True),
    )(value)


HEAD_DIM = 128
SEQ_LEN = 1024
EPSILON = 1e-05
THETA = 10000.0
MASKED = -1e30
GROUP = ("row", "col")
EVERYONE = ("dp", "row", "col")


def on_links():
    return lax.axis_size("dp") == 4 and lax.axis_size("col") == 4 and lax.axis_size("row") == 2


def gather_tokens(arrays, everyone, collective_id, parts):
    if on_links():
        return gather(arrays, 4 if everyone else 1, collective_id, parts)
    axes = EVERYONE if everyone else GROUP
    return [lax.all_gather(a, axes, axis=0, tiled=True) for a in arrays]


def scatter_sums(arrays, everyone, collective_id):
    if on_links():
        return reduce_scatter(arrays, 4 if everyone else 1, collective_id)
    axes = EVERYONE if everyone else GROUP
    return [lax.psum_scatter(a, axes, scatter_dimension=0, tiled=True).astype(jnp.float32) for a in arrays]


def to_heads(w_query, w_key, w_value, w_out):
    if on_links():
        return exchange_weights(w_query, w_key, w_value, w_out, 1)
    pieces = [lax.all_to_all(w, "col", split_axis=1, concat_axis=0, tiled=True) for w in (w_query, w_key, w_value)]
    return jnp.concatenate(pieces, axis=1), lax.all_to_all(w_out, "col", split_axis=0, concat_axis=1, tiled=True)


def sum_over_heads(first_part, second_part, collective_id):
    if on_links():
        stacked = jnp.concatenate([first_part, second_part]).reshape(-1, 128)
        total = group_total(stacked, collective_id).reshape(2, -1)
        return total[0], total[1]
    return lax.psum((first_part, second_part), GROUP)


def inverse_rms(values):
    return lax.rsqrt(jnp.mean(values * values, axis=-1, keepdims=True) + EPSILON)


def norm_backward(values, inv_scale, gain_row, upstream):
    weighted = gain_row * upstream
    inner_sum = jnp.sum(weighted * values, axis=-1, keepdims=True)
    grad_values = inv_scale * weighted - values * inv_scale**3 * inner_sum / values.shape[-1]
    return (grad_values, jnp.sum(upstream * values * inv_scale, axis=0))


def contract(left, right):
    return jnp.dot(left, right, preferred_element_type=jnp.float32)


def contract_rows(left, right):
    return lax.dot_general(
        left, right, (((0,), (0,)), ((), ())), preferred_element_type=jnp.float32
    )


def contract_cols(left, right):
    return lax.dot_general(
        left, right, (((1,), (1,)), ((), ())), preferred_element_type=jnp.float32
    )


def turn_tables(total_rows, seq_length, head_width):
    positions = (jnp.arange(total_rows) % seq_length).astype(jnp.float32)
    inverse = THETA ** (-jnp.arange(0, head_width, 2, dtype=jnp.float32) / head_width)
    angles = positions[:, None] * inverse[None, :]
    angles = jnp.concatenate([angles, angles], axis=-1)
    return (jnp.cos(angles)[:, None, :], jnp.sin(angles)[:, None, :])


def rotate(values, cosine, sine_table):
    middle = values.shape[-1] // 2
    turned = jnp.concatenate([-values[..., middle:], values[..., :middle]], axis=-1)
    return values * cosine + turned * sine_table


def unrotate(upstream, cosine, sine_table):
    middle = upstream.shape[-1] // 2
    turned_part = upstream * sine_table
    return upstream * cosine + jnp.concatenate(
        [turned_part[..., middle:], -turned_part[..., :middle]], axis=-1
    )


def attend_forward(queries, key_rows, value_rows):
    length = queries.shape[0]
    block_rows = min(512, length)
    outputs = []
    sums_log = []
    for first_row in range(0, length, block_rows):
        finish = first_row + block_rows
        scores = jnp.einsum(
            "qhd,khd->hqk",
            queries[first_row:finish],
            key_rows[:finish],
            preferred_element_type=jnp.float32,
        )
        causal = (first_row + jnp.arange(block_rows))[:, None] >= jnp.arange(finish)[None, :]
        scores = jnp.where(causal[None], scores, MASKED)
        highest = jnp.max(scores, axis=-1, keepdims=True)
        weights = jnp.exp(scores - highest)
        totals = jnp.sum(weights, axis=-1, keepdims=True)
        weights = (weights / totals).astype(jnp.bfloat16)
        outputs.append(
            jnp.einsum(
                "hqk,khd->qhd", weights, value_rows[:finish], preferred_element_type=jnp.float32
            )
        )
        sums_log.append((highest + jnp.log(totals))[..., 0])
    return (jnp.concatenate(outputs, axis=0), jnp.concatenate(sums_log, axis=1))


def attend_backward(queries, key_rows, value_rows, grad_out, sums_log):
    length = queries.shape[0]
    block_rows = min(512, length)
    grad_queries = []
    grad_keys = jnp.zeros(key_rows.shape, jnp.float32)
    grad_values = jnp.zeros(value_rows.shape, jnp.float32)
    for first_row in range(0, length, block_rows):
        finish = first_row + block_rows
        scores = jnp.einsum(
            "qhd,khd->hqk",
            queries[first_row:finish],
            key_rows[:finish],
            preferred_element_type=jnp.float32,
        )
        causal = (first_row + jnp.arange(block_rows))[:, None] >= jnp.arange(finish)[None, :]
        scores = jnp.where(causal[None], scores, MASKED)
        weights = jnp.exp(scores - sums_log[:, first_row:finish, None])
        grad_weights = jnp.einsum(
            "qhd,khd->hqk",
            grad_out[first_row:finish],
            value_rows[:finish],
            preferred_element_type=jnp.float32,
        )
        centre = jnp.sum(weights * grad_weights, axis=-1, keepdims=True)
        grad_scores = (weights * (grad_weights - centre)).astype(jnp.bfloat16)
        grad_queries.append(
            jnp.einsum(
                "hqk,khd->qhd", grad_scores, key_rows[:finish], preferred_element_type=jnp.float32
            )
        )
        grad_keys = grad_keys.at[:finish].add(
            jnp.einsum(
                "hqk,qhd->khd",
                grad_scores,
                queries[first_row:finish],
                preferred_element_type=jnp.float32,
            )
        )
        grad_values = grad_values.at[:finish].add(
            jnp.einsum(
                "hqk,qhd->khd",
                weights.astype(jnp.bfloat16),
                grad_out[first_row:finish],
                preferred_element_type=jnp.float32,
            )
        )
    return (jnp.concatenate(grad_queries, axis=0), grad_keys, grad_values)


def by_sequence(step, pieces, sequences):
    if sequences == 1:
        return tuple(out[None] for out in step(*[p[0] for p in pieces]))
    return lax.map(lambda each: step(*each), tuple(pieces))


def expert_rows(normal_h, side, cotangent, gate_use, up_use, down_use, expert_count):
    (all_cotangent,) = gather_tokens([cotangent], True, 3, 2)
    rows_h, rows_side = gather_tokens([normal_h, side], True, 6, 2)
    expert = lax.axis_index("dp") * lax.axis_size("col") + lax.axis_index("col")
    lane = jnp.arange(side.shape[1])
    own_share = jnp.sum(
        jnp.where((lane == expert) | (lane == expert + expert_count), rows_side.astype(jnp.float32), 0.0),
        axis=1,
        keepdims=True,
    )
    back_rows = contract_cols(all_cotangent, down_use)
    gate_rows = contract(rows_h, gate_use)
    up_rows = contract(rows_h, up_use)
    sigmoid_gate = jax.nn.sigmoid(gate_rows)
    silu_gate = gate_rows * sigmoid_gate
    active = silu_gate * up_rows
    route_grad = jnp.sum(active * back_rows, axis=1, keepdims=True)
    active_share = (own_share * active).astype(jnp.bfloat16)
    grad_active = own_share * back_rows
    grad_gate_rows = (
        grad_active * up_rows * sigmoid_gate * (1.0 + gate_rows * (1.0 - sigmoid_gate))
    ).astype(jnp.bfloat16)
    grad_up_rows = (grad_active * silu_gate).astype(jnp.bfloat16)
    entry_part = (contract_cols(grad_gate_rows, gate_use) + contract_cols(grad_up_rows, up_use)).astype(jnp.bfloat16)
    grad_side = jnp.where(jnp.arange(128 if expert_count <= 128 else expert_count)[None, :] == expert, route_grad, 0.0).astype(jnp.bfloat16)
    entry_rows, grad_probs_all = scatter_sums([entry_part, grad_side], True, 7)
    out_part = contract(active_share, down_use).astype(jnp.bfloat16)
    (mixture,) = scatter_sums([out_part], True, 8)
    grad_down_w = contract_rows(active_share, all_cotangent)
    grad_gate_w = contract_rows(rows_h, grad_gate_rows)
    grad_up_w = contract_rows(rows_h, grad_up_rows)
    return entry_rows, grad_probs_all, mixture, grad_gate_w, grad_up_w, grad_down_w


def per_device(
    hidden_in,
    cotangent,
    norm_attn,
    w_query,
    w_key,
    w_value,
    query_gain,
    key_gain,
    w_out,
    norm_moe,
    w_router,
    w_gate,
    w_up,
    w_down,
    routes,
):
    inputs = hidden_in.astype(jnp.float32)
    upstream = cotangent.astype(jnp.float32)
    token_count, top_count = routes.shape
    model_width = inputs.shape[1]
    expert_count = w_router.shape[1]

    inv_input = inverse_rms(inputs)
    normal_x = (inputs * inv_input * norm_attn).astype(jnp.bfloat16)
    w_proj, w_out_own = to_heads(w_query, w_key, w_value, w_out)
    (gathered_x,) = gather_tokens([normal_x], False, 2, 2)
    group_tokens = gathered_x.shape[0]
    raw = contract(gathered_x, w_proj)
    local_width = w_proj.shape[1] // 3
    query_raw = raw[:, :local_width]
    key_raw = raw[:, local_width : 2 * local_width]
    value_heads = raw[:, 2 * local_width :].astype(jnp.bfloat16)
    head_count = local_width // HEAD_DIM
    query_square, key_square = sum_over_heads(
        jnp.sum(query_raw * query_raw, axis=-1), jnp.sum(key_raw * key_raw, axis=-1), 4
    )
    inv_query = lax.rsqrt(query_square / model_width + EPSILON)[:, None]
    inv_key = lax.rsqrt(key_square / model_width + EPSILON)[:, None]
    offset = (lax.axis_index("row") * lax.axis_size("col") + lax.axis_index("col")) * local_width
    gain_query = lax.dynamic_slice_in_dim(query_gain, offset, local_width)
    gain_key = lax.dynamic_slice_in_dim(key_gain, offset, local_width)
    cosine, sine_table = turn_tables(group_tokens, SEQ_LEN, HEAD_DIM)
    head_shape = (group_tokens, head_count, HEAD_DIM)
    sequences = group_tokens // SEQ_LEN
    seq_shape = (sequences, SEQ_LEN, head_count, HEAD_DIM)
    query_heads = (
        rotate((query_raw * inv_query * gain_query).reshape(head_shape), cosine, sine_table)
        * HEAD_DIM ** (-0.5)
    ).astype(jnp.bfloat16)
    key_heads = rotate(
        (key_raw * inv_key * gain_key).reshape(head_shape), cosine, sine_table
    ).astype(jnp.bfloat16)
    query_seq = query_heads.reshape(seq_shape)
    key_seq = key_heads.reshape(seq_shape)
    value_seq = value_heads.reshape(seq_shape)
    mixed, sums_log = by_sequence(attend_forward, (query_seq, key_seq, value_seq), sequences)
    mixed_heads = mixed.reshape(group_tokens, local_width).astype(jnp.bfloat16)
    attn_part = contract(mixed_heads, w_out_own).astype(jnp.bfloat16)
    (attn_rows,) = scatter_sums([attn_part], False, 5)
    state_rows = inputs + attn_rows

    inv_state = inverse_rms(state_rows)
    normal_h = (state_rows * inv_state * norm_moe).astype(jnp.bfloat16)
    logits = contract(normal_h, w_router)
    shifted = jnp.exp(logits - jnp.max(logits, axis=-1, keepdims=True))
    probabilities = shifted / jnp.sum(shifted, axis=-1, keepdims=True)
    selected = jnp.sum(
        (routes[:, :, None] == jnp.arange(expert_count)[None, None, :]).astype(jnp.float32), axis=1
    )
    shares = probabilities * selected
    share_high = shares.astype(jnp.bfloat16)
    share_low = (shares - share_high.astype(jnp.float32)).astype(jnp.bfloat16)
    side_width = max(2 * expert_count, 128)
    side = jnp.concatenate(
        [
            share_high,
            share_low,
            jnp.zeros((token_count, side_width - 2 * expert_count), jnp.bfloat16),
        ],
        axis=1,
    )

    chunks = max(1, lax.axis_size(EVERYONE) // 32)
    if chunks == 1:
        entry_rows, grad_probs_all, mixture, *expert_grads = expert_rows(
            normal_h, side, cotangent, w_gate[0], w_up[0], w_down[0], expert_count
        )
    else:

        def piece_step(sums, piece):
            entry, probs, mixed_rows, *grads = expert_rows(*piece, w_gate[0], w_up[0], w_down[0], expert_count)
            return [s + g for s, g in zip(sums, grads)], (entry, probs, mixed_rows)

        cut = [a.reshape((chunks, token_count // chunks) + a.shape[1:]) for a in (normal_h, side, cotangent)]
        empty = [jnp.zeros(w.shape[1:], jnp.float32) for w in (w_gate, w_up, w_down)]
        expert_grads, rows = lax.scan(piece_step, empty, cut)
        entry_rows, grad_probs_all, mixture = [r.reshape((token_count,) + r.shape[2:]) for r in rows]
    grad_gate_w, grad_up_w, grad_down_w = expert_grads
    block_out = (state_rows + mixture).astype(jnp.bfloat16)

    grad_probs = selected * grad_probs_all[:, :expert_count]
    grad_logits = (
        probabilities * (grad_probs - jnp.sum(probabilities * grad_probs, axis=-1, keepdims=True))
    ).astype(jnp.bfloat16)
    grad_normal_h = entry_rows + contract_cols(grad_logits, w_router)
    grad_router_part = contract_rows(normal_h, grad_logits)
    grad_state_part, grad_moe_part = norm_backward(state_rows, inv_state, norm_moe, grad_normal_h)
    grad_state = upstream + grad_state_part
    grad_attn = grad_state.astype(jnp.bfloat16)
    (grad_gathered,) = gather_tokens([grad_attn], False, 9, 2)
    grad_out_own = contract_rows(mixed_heads, grad_gathered).astype(jnp.bfloat16)
    grad_mixed = contract_cols(grad_gathered, w_out_own).astype(jnp.bfloat16)
    grad_query_seq, grad_key_seq, grad_value_seq = by_sequence(
        attend_backward,
        (query_seq, key_seq, value_seq, grad_mixed.reshape(seq_shape), sums_log),
        sequences,
    )
    grad_normal_q = unrotate(
        grad_query_seq.reshape(head_shape) * HEAD_DIM ** (-0.5), cosine, sine_table
    ).reshape(group_tokens, local_width)
    grad_normal_k = unrotate(grad_key_seq.reshape(head_shape), cosine, sine_table).reshape(
        group_tokens, local_width
    )
    weighted_q = gain_query * grad_normal_q
    weighted_k = gain_key * grad_normal_k
    inner_q, inner_k = sum_over_heads(
        jnp.sum(weighted_q * query_raw, axis=-1), jnp.sum(weighted_k * key_raw, axis=-1), 10
    )
    grad_query_raw = (
        inv_query * weighted_q - query_raw * inv_query**3 * inner_q[:, None] / model_width
    )
    grad_key_raw = inv_key * weighted_k - key_raw * inv_key**3 * inner_k[:, None] / model_width
    grad_qgain_part = jnp.sum(grad_normal_q * query_raw * inv_query, axis=0)
    grad_kgain_part = jnp.sum(grad_normal_k * key_raw * inv_key, axis=0)
    grad_raw = jnp.concatenate(
        [grad_query_raw, grad_key_raw, grad_value_seq.reshape(group_tokens, local_width)], axis=1
    ).astype(jnp.bfloat16)
    grad_x_part = contract_cols(grad_raw, w_proj).astype(jnp.bfloat16)
    (grad_normal_x,) = scatter_sums([grad_x_part], False, 11)
    grad_proj_own = contract_rows(gathered_x, grad_raw).astype(jnp.bfloat16)
    grad_input_part, grad_attn_gain = norm_backward(inputs, inv_input, norm_attn, grad_normal_x)
    grad_input = grad_state + grad_input_part
    grad_query, grad_key, grad_value, grad_out_proj = weight_sums(grad_proj_own, grad_out_own)
    full_width = query_gain.shape[0]
    padded_qgain = lax.dynamic_update_slice_in_dim(
        jnp.zeros((full_width,), jnp.float32), grad_qgain_part, offset, 0
    )
    padded_kgain = lax.dynamic_update_slice_in_dim(
        jnp.zeros((full_width,), jnp.float32), grad_kgain_part, offset, 0
    )
    grad_norm_attn, grad_query_gain, grad_key_gain, grad_norm_moe, grad_router = lax.psum(
        (grad_attn_gain, padded_qgain, padded_kgain, grad_moe_part, grad_router_part),
        ("dp", "row", "col"),
    )
    return (
        block_out,
        grad_input,
        grad_norm_attn,
        grad_query,
        grad_key,
        grad_value,
        grad_query_gain,
        grad_key_gain,
        grad_out_proj,
        grad_norm_moe,
        grad_router,
        grad_gate_w[None],
        grad_up_w[None],
        grad_down_w[None],
    )


def weight_sums(grad_proj_own, grad_out_own):
    width = grad_proj_own.shape[1] // 3
    blocks = [
        lax.all_to_all(grad_proj_own[:, a * width : (a + 1) * width], "col", split_axis=0, concat_axis=1, tiled=True)
        for a in range(3)
    ]
    out_block = lax.all_to_all(grad_out_own, "col", split_axis=1, concat_axis=0, tiled=True)
    return [total.astype(jnp.float32) for total in lax.psum((*blocks, out_block), "dp")]


def solution(mesh):
    placed = (
        P(("dp", "row", "col"), None),
        P(("dp", "row", "col"), None),
        P(),
        P("col", "row"),
        P("col", "row"),
        P("col", "row"),
        P(),
        P(),
        P("row", "col"),
        P(),
        P(),
        P(("dp", "col"), None, "row"),
        P(("dp", "col"), None, "row"),
        P(("dp", "col"), "row", None),
        P(("dp", "row", "col"), None),
    )
    return jax.shard_map(
        per_device,
        mesh=mesh,
        in_specs=placed,
        out_specs=(
            P(("dp", "row", "col"), None),
            P(("dp", "row", "col"), None),
            P(),
            P("col", "row"),
            P("col", "row"),
            P("col", "row"),
            P(),
            P(),
            P("row", "col"),
            P(),
            P(),
            P(("dp", "col"), None, "row"),
            P(("dp", "col"), None, "row"),
            P(("dp", "col"), "row", None),
        ),
        check_vma=False,
    )
```

time: 1960 us -> 1060 us (0.54)
  waiting for transfers between devices: 1130 us -> 168 us
  Pallas kernels: 0 us -> 508 us
  blocking collectives: 300 us -> 77.6 us
  local copies, waits for them, and re-layouts: 136 us -> 27 us
  starting transfers between devices: 53.9 us -> 11.3 us
  other arithmetic: 80.2 us -> 47.8 us
  matrix products: 226 us -> 196 us
    pallas_call x0 -> x11, Pallas kernels: none -> 508 us  [the longest x4 232 us: reduce_scatter(): pl.pallas_call(functools.partial(reduce_kernel, planes, count), out_shape...]
    all_to_all x5 -> x2, waiting for transfers between devices: 442 us -> 13.7 us  [the longest x1 8.34 us: weight_sums(): lax.all_to_all(grad_out_own, 'col', split_axis=1, concat_axis=0, tiled=True)]
    psum x1, waiting for transfers between devices: 296 us -> 34.8 us  [weight_sums(): lax.psum((*blocks, out_block), 'dp')]
    reduce_scatter x6 -> x0, waiting for transfers between devices: 221 us -> none  [the longest x2 161 us: heads_reduce(): return lax.psum_scatter(payload, 'col', scatter_dimension=2, tiled=True)]
    all_to_all x3 -> x2, blocking collectives: 227 us -> 32.3 us  [weight_sums(): lax.all_to_all(grad_proj_own[:, a * width:(a + 1) * width], 'col', split_...]
    all_gather x6 -> x0, waiting for transfers between devices: 148 us -> none  [the longest x2 106 us: heads_gather(): return lax.all_gather(payload, 'col', axis=2, tiled=True)]
    psum x1, waiting for transfers between devices: 28 us -> 119 us  [per_device(): lax.psum((grad_attn_gain, padded_qgain, padded_kgain, grad_moe_part, grad...]
    gather x4 -> x0, local copies, waits for them, and re-layouts: 57.1 us -> none  [the longest x1 19.1 us: per_device(): grad_slots = dispatch(padded_grad[source])]
  transfers between devices with their start and end apart: 19 -> 4, of which waited for: 15 -> 4; matrix products, arithmetic and copies ran while one was open for 11% -> 7% of each run, Pallas kernels for 0% -> 2%
where the time goes in v1:
time: 1060 us; the launch traced here: 1050 us
  Pallas kernels  508 us (48%)
  matrix products  196 us (18%)
  waiting for transfers between devices  168 us (16%)
  blocking collectives  77.6 us (7%)
  other arithmetic  47.8 us (5%)
  local copies, waits for them, and re-layouts  27 us (3%)
  between operations  15.5 us (1%)
  starting transfers between devices  11.3 us (1%)
    pallas_call x4, Pallas kernels, reduce_scatter(): pl.pallas_call(functools.partial(reduce_kernel, planes, count), out_shape...  232 us
    pallas_call x4, Pallas kernels, gather(): pl.pallas_call(functools.partial(gather_kernel, planes, parts, count), ou...  215 us
    psum x1, waiting for transfers between devices, per_device(): lax.psum((grad_attn_gain, padded_qgain, padded_kgain, grad_moe_part, grad...  119 us
    dot_general x6, matrix products, contract_cols(): lax.dot_general(left, right, (((1,), (1,)), ((), ())), preferred_element_...  72.4 us
    dot_general x6, matrix products, contract(): return jnp.dot(left, right, preferred_element_type=jnp.float32)  54.2 us
    dot_general x6, matrix products, contract_rows(): lax.dot_general(left, right, (((0,), (0,)), ((), ())), preferred_element_...  53.4 us
    pallas_call x1, Pallas kernels, exchange_weights(): pl.pallas_call(exchange_kernel, out_shape=[jax.ShapeDtypeStruct((depth *...  49.7 us
    psum x1, blocking collectives, per_device(): lax.psum((grad_attn_gain, padded_qgain, padded_kgain, grad_moe_part, grad...  45.3 us
  transfers between devices with their start and end apart: 4, of which 4 were waited for; matrix products, arithmetic and copies ran while one was open for 7% of the time, Pallas kernels for 2%

profile of v1, /device:TPU:6, one launch (start us, length us, event | category | flops | bytes accessed | tf_op | source)
XLA Modules:
  0.0 1051.6 jit_solution(6549105097892141392)
XLA Ops:
  7.3 1.4 fusion.35
  9.3 2.0 fusion.37.refs_0_
  11.3 22.1 %shard_map.264 = bf16[1024,2048]{1,0:T(8,128)(2,1)} custom-call(bf16[128,2048]{1,0:T(8,128)(2,1)} %fusion.37.refs_0_), custom_call_target="tpu_custom_call" | custom-call | tf_op jit(solution)/shard_map/pallas_call | solution.py:100
  33.4 49.7 %shard_map.265 = (bf16[2048,768]{1,0:T(8,128)(2,1)}, bf16[256,2048]{1,0:T(8,128)(2,1)}) custom-call(bf16[512,1024]{1,0:T(8,128)(2,1)} %wq_ref.1, bf16[512,1024]{1,0:T(8,128)(2,1)} %wk_ref.1, bf16[512,1024]{1,0:T(8,128)(2,1)} %wv_ref.1, bf16[1024,512]{1,0:T(8,128)(2,1)} %wo_ref.1), custom_call_target="tpu_custom_call" | custom-call | tf_op jit(solution)/shard_map/pallas_call | solution.py:274
  83.1 7.9 fusion.85
  91.0 1.7 copy-done.6
  93.6 6.1 shard_map.266
  99.7 1.3 multiply_multiply_fusion.3
  101.7 1.7 slice.207
  103.4 1.9 slice.216
  108.2 3.6 broadcast_multiply_fusion.2
  111.8 1.6 multiply_multiply_fusion.1
  113.4 1.6 copy.117
  115.0 2.5 copy.120
  117.5 2.4 slice_negate_fusion.1
  126.5 1.5 fusion.32
  128.8 1.3 convolution_convert_fusion.1.refs_0_
  130.2 22.3 %shard_map.267 = f32[128,2048]{1,0:T(8,128)S(1)} custom-call(bf16[1024,2048]{1,0:T(8,128)(2,1)S(1)} %convolution_convert_fusion.1.refs_0_), custom_call_target="tpu_custom_call" | custom-call | tf_op jit(solution)/shard_map/pallas_call | solution.py:221
  154.2 83.9 %shard_map.270 = bf16[4096,2048]{1,0:T(8,128)(2,1)} custom-call(bf16[128,2048]{1,0:T(8,128)(2,1)} %refs_0_.1), custom_call_target="tpu_custom_call" | custom-call | tf_op jit(solution)/shard_map/pallas_call | solution.py:100
  239.3 86.3 %shard_map.268 = (bf16[4096,2048]{1,0:T(8,128)(2,1)}, bf16[4096,128]{1,0:T(8,128)(2,1)}) custom-call(bf16[128,2048]{1,0:T(8,128)(2,1)} %copy-done.17, bf16[128,128]{1,0:T(8,128)(2,1)} %maximum_maximum_fusion.refs_1_), custom_call_target="tpu_custom_call" | custom-call | tf_op jit(solution)/shard_map/pallas_call | solution.py:100
  325.6 15.4 %fusion.9 = f32[4096,512]{0,1:T(8,128)} fusion(bf16[4096,2048]{1,0:T(8,128)(2,1)} %get-tuple-element.87, bf16[1,2048,512]{2,1,0:T(8,128)(2,1)} %param.39), kind=kOutput, calls=%fused_computation.35 | convolution fusion | flops 8589934592 | bytes 27262976 | tf_op jit(solution)/shard_map/dot_general | solution.py:369
  341.0 14.6 %fusion.13 = f32[4096,512]{0,1:T(8,128)} fusion(bf16[4096,2048]{1,0:T(8,128)(2,1)} %get-tuple-element.87, bf16[1,2048,512]{2,1,0:T(8,128)(2,1)S(1)} %copy-done.77), kind=kOutput, calls=%fused_computation.39 | convolution fusion | flops 8589934592 | bytes 27262976 | tf_op jit(solution)/shard_map/dot_general | solution.py:369
  356.0 24.1 %multiply_reduce_fusion = (bf16[4096]{0:T(1024)(128)(2,1)S(1)}, bf16[4096,512]{0,1:T(8,128)(2,1)}, bf16[4096,512]{0,1:T(8,128)(2,1)}, bf16[4096,512]{0,1:T(8,128)(2,1)}) fusion(f32[4096,512]{0,1:T(8,128)} %fusion.9, f32[4096,512]{0,1:T(8,128)} %fusion.13, f32[4096]{0:T(1024)S(1)} %select_reduce_fusion.1, bf16[4096,2048]{1,0:T(8,128)(2,1)} %shard_map.270, ...), kind=kOutput, calls=%fused_computation.2 | convolution fusion | flops 8629776384 | bytes 48259072 | tf_op jit(solution)/shard_map/dot_general | solution.py:379
  380.1 14.6 %convolution_convert_fusion.refs_0_ = bf16[4096,2048]{1,0:T(8,128)(2,1)} fusion(bf16[4096,512]{0,1:T(8,128)(2,1)} %get-tuple-element.117, bf16[1,512,2048]{2,1,0:T(8,128)(2,1)S(1)} %copy-done), kind=kOutput, calls=%fused_computation.1 | convolution fusion | flops 8598323200 | bytes 23068672 | tf_op jit(solution)/shard_map/dot_general | solution.py:369
  394.8 92.8 %shard_map.269 = f32[128,2048]{1,0:T(8,128)S(1)} custom-call(bf16[4096,2048]{1,0:T(8,128)(2,1)} %convolution_convert_fusion.refs_0_), custom_call_target="tpu_custom_call" | custom-call | tf_op jit(solution)/shard_map/pallas_call | solution.py:221
  487.7 15.7 %fusion.11 = f32[4096,2048]{1,0:T(8,128)} fusion(bf16[4096,512]{0,1:T(8,128)(2,1)S(1)} %copy-done.81, bf16[1,2048,512]{2,1,0:T(8,128)(2,1)S(1)} %copy-done.78), kind=kOutput, calls=%fused_computation.37 | convolution fusion | flops 8589934592 | bytes 39845888 | tf_op jit(solution)/shard_map/dot_general | solution.py:379
  504.0 22.8 %add_convert_fusion.refs_0_ = bf16[4096,2048]{1,0:T(8,128)(2,1)} fusion(f32[4096,2048]{1,0:T(8,128)} %fusion.11, bf16[4096,512]{0,1:T(8,128)(2,1)} %get-tuple-element.118, bf16[1,2048,512]{2,1,0:T(8,128)(2,1)} %param.39), kind=kOutput, calls=%fused_computation | convolution fusion | flops 8606711808 | bytes 56623104 | tf_op jit(solution)/shard_map/dot_general | solution.py:379
  526.8 93.7 %shard_map.271 = (f32[128,2048]{1,0:T(8,128)S(1)}, f32[128,128]{1,0:T(8,128)S(1)}) custom-call(bf16[4096,2048]{1,0:T(8,128)(2,1)} %add_convert_fusion.refs_0_, bf16[4096,128]{1,0:T(8,128)(2,1)S(1)} %select_convert_fusion.refs_1_), custom_call_target="tpu_custom_call" | custom-call | tf_op jit(solution)/shard_map/pallas_call | solution.py:221
  621.5 1.8 fusion.80
  623.3 22.6 %shard_map.272 = bf16[1024,2048]{1,0:T(8,128)(2,1)} custom-call(bf16[128,2048]{1,0:T(8,128)(2,1)} %get-tuple-element.111.refs_0_), custom_call_target="tpu_custom_call" | custom-call | tf_op jit(solution)/shard_map/pallas_call | solution.py:100
  645.9 3.6 convolution_convert_fusion.5
  649.6 1.5 convolution_bitcast_fusion.5
  653.8 1.2 convolution_bitcast_fusion.4
  655.0 2.0 copy.135
  658.0 4.0 multiply_reduce_fusion.1
  662.0 2.2 fusion.28
  664.2 1.4 multiply_convert_fusion.3
  669.0 1.3 maximum_add_fusion
  670.3 1.6 copy.142
  673.1 3.2 fusion.52
  676.9 6.2 shard_map.273
  683.9 2.6 subtract_convert_fusion.1
  687.5 3.8 convolution_convert_fusion.3
  692.5 16.5 %all_to_all.76 = bf16[4,512,256]{2,1,0:T(8,128)(2,1)S(1)} all-to-all(bf16[4,512,256]{2,1,0:T(8,128)(2,1)S(1)} %bitcast.162), channel_id=1, replica_groups=mesh['dp'=4,'row'=2,'col'=4] {'col'}, dimensions={0} | all-to-all | bytes 2097152 | tf_op jit(solution)/shard_map/all_to_all | solution.py:699
  709.0 15.8 %all_to_all.77 = bf16[4,512,256]{2,1,0:T(8,128)(2,1)S(1)} all-to-all(bf16[4,512,256]{2,1,0:T(8,128)(2,1)S(1)} %bitcast.161), channel_id=1, replica_groups=mesh['dp'=4,'row'=2,'col'=4] {'col'}, dimensions={0} | all-to-all | bytes 2097152 | tf_op jit(solution)/shard_map/all_to_all | solution.py:699
  724.8 5.5 all-to-all-start
  730.3 3.6 convolution_convert_fusion.4
  734.9 5.4 all-to-all-done
  740.4 5.7 all-to-all-start.3
  749.4 8.3 all-to-all-done.3
  758.8 16.0 %convolution_bitcast_fusion = f32[1,512,2048]{2,1,0:T(8,128)} fusion(bf16[4096,512]{0,1:T(8,128)(2,1)} %get-tuple-element.117, bf16[4096,2048]{1,0:T(8,128)(2,1)} %shard_map.270), kind=kOutput, calls=%fused_computation.18 | convolution fusion | flops 8589934592 | bytes 25165824 | tf_op jit(solution)/shard_map/dot_general | solution.py:373
  774.8 15.2 %convolution_bitcast_fusion.2 = f32[1,2048,512]{2,1,0:T(8,128)} fusion(bf16[4096,2048]{1,0:T(8,128)(2,1)} %get-tuple-element.87, bf16[4096,512]{0,1:T(8,128)(2,1)} %get-tuple-element.116), kind=kOutput, calls=%fused_computation.20 | convolution fusion | flops 8589934592 | bytes 25165824 | tf_op jit(solution)/shard_map/dot_general | solution.py:373
  790.0 13.9 %convolution_bitcast_fusion.1 = f32[1,2048,512]{2,1,0:T(8,128)} fusion(bf16[4096,2048]{1,0:T(8,128)(2,1)S(1)} %bitcast.181, bf16[4096,512]{0,1:T(8,128)(2,1)} %get-tuple-element.118), kind=kOutput, calls=%fused_computation.19 | convolution fusion | flops 8589934592 | bytes 25165824 | tf_op jit(solution)/shard_map/dot_general | solution.py:373
  804.0 5.7 convolution_convert_fusion.2.refs_0_
  809.7 22.7 %shard_map.274 = f32[128,2048]{1,0:T(8,128)S(1)} custom-call(bf16[1024,2048]{1,0:T(8,128)(2,1)S(1)} %convolution_convert_fusion.2.refs_0_), custom_call_target="tpu_custom_call" | custom-call | tf_op jit(solution)/shard_map/pallas_call | solution.py:221
  832.8 1.4 fusion.41
  834.7 45.3 %all-reduce.2 = (f32[2048]{0:T(1024)}, f32[2048]{0:T(1024)}, f32[2048]{0:T(1024)}, f32[2048]{0:T(1024)}) all-reduce(f32[2048]{0:T(1024)S(1)} %get-tuple-element.100, f32[2048]{0:T(1024)S(1)} %dynamic_update_slice.6, f32[2048]{0:T(1024)S(1)} %dynamic_update_slice.7, ...), channel_id=1, replica_groups=mesh['dp'=4,'row'=2,'col'=4] {'dp','row','col'}, use_global_device_ids=true, to_apply=%region_21.22 | all-reduce | flops 8192 | bytes 65536 | tf_op jit(solution)/shard_map/psum | solution.py:674
  879.9 34.8 %all-reduce.9.cloned.1.call-done = (bf16[512,1024]{1,0:T(8,128)(2,1)}, bf16[512,1024]{1,0:T(8,128)(2,1)}, bf16[512,1024]{1,0:T(8,128)(2,1)}, bf16[1024,512]{1,0:T(8,128)(2,1)}) async-done(((bf16[512,1024]{1,0:T(8,128)(2,1)}, bf16[512,1024]{1,0:T(8,128)(2,1)}, bf16[512,1024]{1,0:T(8,128)(2,1)}, bf16[1024,512]{1,0:T(8,128)(2,1)}), (bf16[512,1024]{1,0:T(8,128)(2,1)}, bf16[512,1024]{1,0:T(8,128)(2,1)}, ...) | async-done | bytes 4194320 | tf_op jit(solution)/shard_map/psum | solution.py:703
  914.7 2.9 convert_element_type.152
  917.7 2.9 convert_element_type.153
  920.6 1.6 convert_element_type.154
  922.2 1.6 convert_element_type.156
  923.8 119.3 %all-reduce.7.cloned.1.call-done = f32[2048,16]{0,1:T(8,128)} async-done(((f32[2048,16]{0,1:T(8,128)}), f32[2048,16]{0,1:T(8,128)}) %all-reduce.7.cloned.1.call-update) | async-done | bytes 131088 | tf_op jit(solution)/shard_map/psum | solution.py:674
  1043.0 1.6 copy.175
  (239 shorter events, 34.9 us)
Async XLA Ops:
  7.2 348.8 %copy-start = (bf16[1,512,2048]{2,1,0:T(8,128)(2,1)S(1)}, bf16[1,512,2048]{2,1,0:T(8,128)(2,1)}, u32[]{:S(2)}) copy-start(bf16[1,512,2048]{2,1,0:T(8,128)(2,1)} %param.40) | copy-start | bytes 6291460
  7.3 115.2 %copy-start.15 = (pred[512,512]{0,1:T(8,128)(4,1)}, pred[512,512]{0,1:T(8,128)(4,1)S(1)}, u32[]{:S(2)}) copy-start(pred[512,512]{0,1:T(8,128)(4,1)S(1)} %iota_compare_fusion.1) | copy-start | bytes 786436
  9.3 73.8 %copy-start.70 = (f32[128]{0:T(128)}, f32[128]{0:T(128)S(1)}, u32[]{:S(2)}) copy-start(f32[128]{0:T(128)S(1)} %get-tuple-element.152) | copy-start | bytes 1540
  83.1 23.6 %copy-start.74 = (s32[128,8]{0,1:T(8,128)S(1)}, s32[128,8]{0,1:T(8,128)}, u32[]{:S(2)}) copy-start(s32[128,8]{0,1:T(8,128)} %param.41) | copy-start | bytes 12292
  101.7 11.7 %copy-start.59 = (f32[1024]{0:T(1024)}, f32[1024]{0:T(1024)S(1)}, u32[]{:S(2)}) copy-start(f32[1024]{0:T(1024)S(1)} %get-tuple-element.149) | copy-start | bytes 12292
  101.7 11.7 %copy-start.61 = (f32[1024]{0:T(1024)}, f32[1024]{0:T(1024)S(1)}, u32[]{:S(2)}) copy-start(f32[1024]{0:T(1024)S(1)} %get-tuple-element.150) | copy-start | bytes 12292
  106.0 7.4 copy-start.66
  106.8 6.7 copy-start.68
  106.9 5.0 copy-start.7
  130.1 22.3 %copy-start.13 = (bf16[128,2048]{1,0:T(8,128)(2,1)S(1)}, bf16[128,2048]{1,0:T(8,128)(2,1)}, u32[]{:S(2)}) copy-start(bf16[128,2048]{1,0:T(8,128)(2,1)} %param.27) | copy-start | bytes 1572868
  130.1 23.5 %copy-start.55 = (f32[2048]{0:T(1024)S(1)}, f32[2048]{0:T(1024)}, u32[]{:S(2)}) copy-start(f32[2048]{0:T(1024)} %param.36) | copy-start | bytes 24580
  130.2 23.7 %copy-start.53 = (bf16[2048,16]{0,1:T(8,128)(2,1)S(1)}, bf16[2048,16]{0,1:T(8,128)(2,1)}, u32[]{:S(2)}) copy-start(bf16[2048,16]{0,1:T(8,128)(2,1)} %param.37) | copy-start | bytes 196612
  153.3 84.9 %copy-start.72 = (f32[128]{0:T(128)}, f32[128]{0:T(128)S(1)}, u32[]{:S(2)}) copy-start(f32[128]{0:T(128)S(1)} %get-tuple-element.154) | copy-start | bytes 1540
  153.8 84.3 %copy-start.17 = (bf16[128,2048]{1,0:T(8,128)(2,1)}, bf16[128,2048]{1,0:T(8,128)(2,1)S(1)}, u32[]{:S(2)}) copy-start(bf16[128,2048]{1,0:T(8,128)(2,1)S(1)} %multiply_convert_fusion.5.refs_0_) | copy-start | bytes 1572868
  325.5 15.5 %copy-start.77 = (bf16[1,2048,512]{2,1,0:T(8,128)(2,1)S(1)}, bf16[1,2048,512]{2,1,0:T(8,128)(2,1)}, u32[]{:S(2)}) copy-start(bf16[1,2048,512]{2,1,0:T(8,128)(2,1)} %param.38) | copy-start | bytes 6291460
  341.0 14.6 %copy-start.45 = (bf16[4096,128]{1,0:T(8,128)(2,1)S(1)}, bf16[4096,128]{1,0:T(8,128)(2,1)}, u32[]{:S(2)}) copy-start(bf16[4096,128]{1,0:T(8,128)(2,1)} %get-tuple-element.86) | copy-start | bytes 3145732
  394.8 92.8 %copy-start.78 = (bf16[1,2048,512]{2,1,0:T(8,128)(2,1)S(1)}, bf16[1,2048,512]{2,1,0:T(8,128)(2,1)}, u32[]{:S(2)}) copy-start(bf16[1,2048,512]{2,1,0:T(8,128)(2,1)} %param.38) | copy-start | bytes 6291460
  394.8 92.9 %copy-start.81 = (bf16[4096,512]{0,1:T(8,128)(2,1)S(1)}, bf16[4096,512]{0,1:T(8,128)(2,1)}, u32[]{:S(2)}) copy-start(bf16[4096,512]{0,1:T(8,128)(2,1)} %get-tuple-element.116) | copy-start | bytes 12582916
  526.8 94.1 %copy-start.9 = (f32[128,2048]{1,0:T(8,128)S(1)}, f32[128,2048]{1,0:T(8,128)}, u32[]{:S(2)}) copy-start(f32[128,2048]{1,0:T(8,128)} %copy-done.8) | copy-start | bytes 3145732
  526.8 94.1 %copy-start.54 = (bf16[2048,16]{0,1:T(8,128)(2,1)S(1)}, bf16[2048,16]{0,1:T(8,128)(2,1)}, u32[]{:S(2)}) copy-start(bf16[2048,16]{0,1:T(8,128)(2,1)} %param.37) | copy-start | bytes 196612
  526.8 94.1 %copy-start.56 = (f32[2048]{0:T(1024)S(1)}, f32[2048]{0:T(1024)}, u32[]{:S(2)}) copy-start(f32[2048]{0:T(1024)} %param.36) | copy-start | bytes 24580
  526.8 94.1 %copy-start.73 = (f32[128]{0:T(128)S(1)}, f32[128]{0:T(128)}, u32[]{:S(2)}) copy-start(f32[128]{0:T(128)} %copy-done.72) | copy-start | bytes 1540
  526.8 94.6 %copy-start.34 = (bf16[128,2048]{1,0:T(8,128)(2,1)S(1)}, bf16[128,2048]{1,0:T(8,128)(2,1)}, u32[]{:S(2)}) copy-start(bf16[128,2048]{1,0:T(8,128)(2,1)} %refs_0_.1) | copy-start | bytes 1572868
  526.8 94.6 %copy-start.76 = (f32[128]{0:T(128)S(1)}, f32[128]{0:T(128)}, u32[]{:S(2)}) copy-start(f32[128]{0:T(128)} %get-tuple-element.153) | copy-start | bytes 1540
  621.5 24.4 %copy-start.47 = (bf16[256,2048]{1,0:T(8,128)(2,1)S(1)}, bf16[256,2048]{1,0:T(8,128)(2,1)}, u32[]{:S(2)}) copy-start(bf16[256,2048]{1,0:T(8,128)(2,1)} %get-tuple-element.85) | copy-start | bytes 3145732
  645.9 3.7 copy-start.5
  645.9 3.7 copy-start.16
  645.9 5.2 copy-start.44
  652.6 4.4 copy-start.37
  652.6 5.4 copy-start.12
  652.6 5.4 copy-start.36
  652.6 5.4 copy-start.63
  658.0 4.0 copy-start.3
  658.0 4.0 copy-start.52
  668.9 4.1 copy-start.25
  669.0 4.1 copy-start.38
  669.0 4.1 copy-start.60
  669.0 4.1 copy-start.62
  669.0 4.1 copy-start.67
  669.0 4.1 copy-start.69
  671.9 12.0 %copy-start.64 = (f32[1024]{0:T(1024)S(1)}, f32[1024]{0:T(1024)}, u32[]{:S(2)}) copy-start(f32[1024]{0:T(1024)} %get-tuple-element.145) | copy-start | bytes 12292
  671.9 12.0 %copy-start.65 = (f32[1024]{0:T(1024)S(1)}, f32[1024]{0:T(1024)}, u32[]{:S(2)}) copy-start(f32[1024]{0:T(1024)} %get-tuple-element.146) | copy-start | bytes 12292
  676.3 11.2 %copy-start.79 = (bf16[1024,2,128]{0,2,1:T(8,128)(2,1)S(1)}, bf16[1024,2,128]{0,2,1:T(8,128)(2,1)}, u32[]{:S(2)}) copy-start(bf16[1024,2,128]{0,2,1:T(8,128)(2,1)} %fusion.28) | copy-start | bytes 1572868
  683.1 4.5 copy-start.32
  724.8 15.6 %all-to-all-start = ((bf16[4,512,256]{2,1,0:T(8,128)(2,1)}), bf16[4,512,256]{2,1,0:T(8,128)(2,1)S(1)}, u32[]{:S(2)}, u32[]{:S(2)}) async-start(bf16[4,512,256]{2,1,0:T(8,128)(2,1)} %bitcast.160), calls=%async_computation | async-start | bytes 2097152 | tf_op jit(solution)/shard_map/all_to_all | solution.py:699
  740.4 17.4 %all-to-all-start.3 = ((bf16[256,4,512]{2,0,1:T(8,128)(2,1)}), bf16[256,4,512]{2,0,1:T(8,128)(2,1)}, u32[]{:S(2)}, u32[]{:S(2)}) async-start(bf16[256,4,512]{2,0,1:T(8,128)(2,1)} %bitcast.156), calls=%async_computation.3 | async-start | bytes 2097152 | tf_op jit(solution)/shard_map/all_to_all | solution.py:702
  746.1 168.6 %all-reduce.9.cloned.1.call-start = ((), (), s32[]{:S(2)}) async-start(), calls=%async_computation.5 | async-start | bytes 8388608 | tf_op jit(solution)/shard_map/psum | solution.py:703
  747.2 10.6 %copy-start.18 = (bf16[128,2048]{1,0:T(8,128)(2,1)S(1)}, bf16[128,2048]{1,0:T(8,128)(2,1)}, u32[]{:S(2)}) copy-start(bf16[128,2048]{1,0:T(8,128)(2,1)} %copy-done.17) | copy-start | bytes 1572868
  757.8 285.3 %all-reduce.7.cloned.1.call-start = ((), (), s32[]{:S(2)}) async-start(), calls=%async_computation.4 | async-start | bytes 262144 | tf_op jit(solution)/shard_map/psum | solution.py:674
  758.7 31.2 %slice-start = ((s8[16777216]{0:T(1024)(128)(4,1)}), s8[4194304]{0:T(1024)(128)(4,1)S(1)}, s32[]{:S(2)}) async-start(s8[16777216]{0:T(1024)(128)(4,1)} %bitcast.180), calls=%async_computation.6 | async-start | bytes 8388608
  758.8 31.2 %slice-start.1 = ((s8[16777216]{0:T(1024)(128)(4,1)}), s8[4194304]{0:T(1024)(128)(4,1)S(1)}, s32[]{:S(2)}) async-start(s8[16777216]{0:T(1024)(128)(4,1)} %bitcast.180), calls=%async_computation.7 | async-start | bytes 8388608
  774.8 15.2 %slice-start.2 = ((s8[16777216]{0:T(1024)(128)(4,1)}), s8[4194304]{0:T(1024)(128)(4,1)S(1)}, s32[]{:S(2)}) async-start(s8[16777216]{0:T(1024)(128)(4,1)} %bitcast.180), calls=%async_computation.8 | async-start | bytes 8388608
  774.8 15.2 %slice-start.3 = ((s8[16777216]{0:T(1024)(128)(4,1)}), s8[4194304]{0:T(1024)(128)(4,1)S(1)}, s32[]{:S(2)}) async-start(s8[16777216]{0:T(1024)(128)(4,1)} %bitcast.180), calls=%async_computation.9 | async-start | bytes 8388608
  790.0 14.0 %copy-start.49 = (bf16[1024,256]{0,1:T(8,128)(2,1)S(1)}, bf16[1024,256]{0,1:T(8,128)(2,1)}, u32[]{:S(2)}) copy-start(bf16[1024,256]{0,1:T(8,128)(2,1)} %copy-done.48) | copy-start | bytes 1572868
  790.0 14.0 %copy-start.51 = (bf16[1024,256]{0,1:T(8,128)(2,1)S(1)}, bf16[1024,256]{0,1:T(8,128)(2,1)}, u32[]{:S(2)}) copy-start(bf16[1024,256]{0,1:T(8,128)(2,1)} %copy-done.50) | copy-start | bytes 1572868
  790.0 13.9 %copy-start.80 = (bf16[1024,2,128]{0,2,1:T(8,128)(2,1)S(1)}, bf16[1024,2,128]{0,2,1:T(8,128)(2,1)}, u32[]{:S(2)}) copy-start(bf16[1024,2,128]{0,2,1:T(8,128)(2,1)} %fusion.28) | copy-start | bytes 1572868
  809.6 22.8 %copy-start.14 = (bf16[128,2048]{1,0:T(8,128)(2,1)S(1)}, bf16[128,2048]{1,0:T(8,128)(2,1)}, u32[]{:S(2)}) copy-start(bf16[128,2048]{1,0:T(8,128)(2,1)} %param.27) | copy-start | bytes 1572868
  809.6 22.8 %copy-start.57 = (f32[2048]{0:T(1024)S(1)}, f32[2048]{0:T(1024)}, u32[]{:S(2)}) copy-start(f32[2048]{0:T(1024)} %param.29) | copy-start | bytes 24580
  809.7 22.8 %copy-start.71 = (f32[128]{0:T(128)S(1)}, f32[128]{0:T(128)}, u32[]{:S(2)}) copy-start(f32[128]{0:T(128)} %copy-done.70) | copy-start | bytes 1540
  809.7 23.1 %copy-start.31 = (f32[128,2048]{1,0:T(8,128)S(1)}, f32[128,2048]{1,0:T(8,128)}, u32[]{:S(2)}) copy-start(f32[128,2048]{1,0:T(8,128)} %get-tuple-element.112) | copy-start | bytes 3145732
  809.7 23.1 %copy-start.75 = (f32[128]{0:T(128)S(1)}, f32[128]{0:T(128)}, u32[]{:S(2)}) copy-start(f32[128]{0:T(128)} %get-tuple-element.151) | copy-start | bytes 1540
  914.7 5.9 copy-start.42
  914.7 7.5 copy-start.41
  917.7 127.0 %copy-start.1 = (bf16[1,512,2048]{2,1,0:T(8,128)(2,1)S(1)}, bf16[1,512,2048]{2,1,0:T(8,128)(2,1)}, u32[]{:S(2)}) copy-start(bf16[1,512,2048]{2,1,0:T(8,128)(2,1)} %param.40) | copy-start | bytes 6291460
  (26 other events, 51.7 us)
Sparse Core Ops, SparseCore 0:
  757.9 156.7 all-reduce.8
  921.7 121.2 all-reduce.6

commit v2 on v1

--- a/solution.py
+++ b/solution.py
@@ -105,35 +105,43 @@
         compiler_params=pltpu.CompilerParams(collective_id=collective_id, has_side_effects=True),
     )(*arrays)
 
-def reduce_kernel(planes, count, *refs):
-    parts, outs = refs[:count], refs[count:2 * count]
-    held, fromp, relay, near, far = (refs[(2 + i) * count:(3 + i) * count] for i in range(5))
-    load_sem, pair_send, pair_recv, send_sem, relay_recv, near_recv, far_recv = refs[7 * count:]
+def reduce_steps(planes, parts, outs, buffers, semaphores, filler):
+    held, fromp, relay, near, far = buffers
+    load_sem, pair_send, pair_recv, send_sem, relay_recv, near_recv, far_recv = semaphores
     z, r, c = place()
     first, second, diag = c ^ (1 + r), c ^ (2 - r), c ^ 3
     partner = (z, 1 - r, c)
     to_first, to_second = (z, r, first), (z, r, second)
     greet([to_first, to_second, partner] + [(z ^ k, r, c) for k in range(1, planes)])
     depth = outs[0].shape[0]
-    every = range(count)
-
-    def rows(a, zz, rr, cc):
-        which = ((zz if planes > 1 else 0) * 2 + rr) * 4 + cc
+    every = range(len(parts))
+
+    def rows(a, k, rr, cc):
+        which = (((z ^ k) if planes > 1 else 0) * 2 + rr) * 4 + cc
         return parts[a].at[pl.ds(pl.multiple_of(which * depth, depth), depth)]
 
     columns, partner_columns = [c, first, second, diag], [c, second, first, diag]
-    loads, pairs = {}, {}
-    for k in reversed(range(planes)):
+
+    def remote(source, target, send, recv, device):
+        return pltpu.make_async_remote_copy(
+            src_ref=source, dst_ref=target, send_sem=send, recv_sem=recv, device_id=device, device_id_type=MESH)
+
+    def load(a, k, j):
+        return pltpu.make_async_copy(rows(a, k, r, columns[j]), held[a].at[k, j], load_sem.at[a, k, j])
+
+    def pair(a, k, j):
+        return remote(rows(a, k, 1 - r, partner_columns[j]), fromp[a].at[k, j], pair_send.at[a, k, j], pair_recv.at[a, k, j], partner)
+
+    def begin(i, _):
+        k = planes - 1 - i
         for j in (3, 2, 1, 0):
             for a in every:
-                load = pltpu.make_async_copy(rows(a, z ^ k, r, columns[j]), held[a].at[k, j], load_sem.at[a, k, j])
-                load.start()
-                pair = pltpu.make_async_remote_copy(
-                    src_ref=rows(a, z ^ k, 1 - r, partner_columns[j]), dst_ref=fromp[a].at[k, j],
-                    send_sem=pair_send.at[a, k, j], recv_sem=pair_recv.at[a, k, j], device_id=partner, device_id_type=MESH)
-                pair.start()
-                loads[a, k, j], pairs[a, k, j] = load, pair
-    step_rows = 32
+                load(a, k, j).start()
+                pair(a, k, j).start()
+        return 0
+
+    lax.fori_loop(0, planes, begin, 0)
+    step_rows = min(32, depth)
 
     def add(target, sources):
         def body(i, _):
@@ -145,86 +153,113 @@
             return 0
         lax.fori_loop(0, depth // step_rows, body, 0)
 
-    sent = [[] for _ in every]
-
-    def send(a, source, target, recv, device):
-        copy = pltpu.make_async_remote_copy(
-            src_ref=source, dst_ref=target, send_sem=send_sem.at[a, len(sent[a])], recv_sem=recv,
-            device_id=device, device_id_type=MESH)
-        copy.start()
-        sent[a].append(copy)
-
-    def await_in(a, target, recv):
-        pltpu.make_async_remote_copy(
-            src_ref=target, dst_ref=target, send_sem=send_sem.at[a, 0], recv_sem=recv,
-            device_id=partner, device_id_type=MESH).wait_recv()
-
     def ready(a, k, j):
-        loads[a, k, j].wait()
-        pairs[a, k, j].wait_recv()
+        load(a, k, j).wait()
+        pair(a, k, j).wait_recv()
+
+    def to_diag(a, k):
+        return remote(held[a].at[k, 3], relay[a].at[k], send_sem.at[a, k, 0], relay_recv.at[a, k], to_second)
+
+    def to_near(a, k, which):
+        source, device = (held[a].at[k, 2], to_second) if which else (held[a].at[k, 1], to_first)
+        return remote(source, near[a].at[k, which], send_sem.at[a, k, 1 + which], near_recv.at[a, k, which], device)
+
+    def to_far(a, k):
+        slot = jnp.maximum(k - 1, 0)
+        return remote(held[a].at[k, 0], far[a].at[slot], send_sem.at[a, k, 3], far_recv.at[a, slot], (z ^ k, r, c))
 
     def to_relay(k):
-        for j in (3, 2):
-            for a in every:
-                ready(a, k, j)
-                mine = held[a].at[k, j]
-                add(mine, [mine, fromp[a].at[k, j]])
-                if j == 3:
-                    send(a, mine, relay[a].at[k], relay_recv.at[a, k], to_second)
-                else:
-                    send(a, mine, near[a].at[k, 1], near_recv.at[a, k, 1], to_second)
+        for a in every:
+            ready(a, k, 3)
+            add(held[a].at[k, 3], [held[a].at[k, 3], fromp[a].at[k, 3]])
+            to_diag(a, k).start()
+        for a in every:
+            ready(a, k, 2)
+            add(held[a].at[k, 2], [held[a].at[k, 2], fromp[a].at[k, 2]])
+            to_near(a, k, 1).start()
 
     def pass_on(k):
         for a in every:
             ready(a, k, 1)
-            await_in(a, relay[a].at[k], relay_recv.at[a, k])
-            mine = held[a].at[k, 1]
-            add(mine, [mine, fromp[a].at[k, 1], relay[a].at[k]])
-            send(a, mine, near[a].at[k, 0], near_recv.at[a, k, 0], to_first)
+            to_diag(a, k).wait_recv()
+            add(held[a].at[k, 1], [held[a].at[k, 1], fromp[a].at[k, 1], relay[a].at[k]])
+            to_near(a, k, 0).start()
 
     def collect(k):
         for a in every:
             ready(a, k, 0)
-            await_in(a, near[a].at[k, 0], near_recv.at[a, k, 0])
-            await_in(a, near[a].at[k, 1], near_recv.at[a, k, 1])
-            mine = held[a].at[k, 0]
-            terms = [mine, fromp[a].at[k, 0], near[a].at[k, 0], near[a].at[k, 1]]
-            if k > 0:
-                add(mine, terms)
-                send(a, mine, far[a].at[k - 1], far_recv.at[a, k - 1], (z ^ k, r, c))
-            else:
-                for i in range(planes - 1):
-                    await_in(a, far[a].at[i], far_recv.at[a, i])
+            to_near(a, k, 0).wait_recv()
+            to_near(a, k, 1).wait_recv()
+            terms = [held[a].at[k, 0], fromp[a].at[k, 0], near[a].at[k, 0], near[a].at[k, 1]]
+
+            @pl.when(k > 0)
+            def _():
+                add(held[a].at[k, 0], terms)
+                to_far(a, k).start()
+
+            @pl.when(k == 0)
+            def _():
+                for i in range(1, planes):
+                    to_far(a, i).wait_recv()
                 add(outs[a], terms + [far[a].at[i] for i in range(planes - 1)])
 
-    order = list(reversed(range(planes)))
-    for step in range(planes + 2):
-        if step < planes:
-            to_relay(order[step])
-        if 0 <= step - 1 < planes:
-            pass_on(order[step - 1])
-        if 0 <= step - 2 < planes:
-            collect(order[step - 2])
-    for copies in sent:
-        for copy in copies:
-            copy.wait_send()
-    for pair in pairs.values():
-        pair.wait_send()
+    def step_body(step, _):
+        @pl.when(step < planes)
+        def _():
+            to_relay(planes - 1 - step)
+
+        @pl.when(jnp.logical_and(step >= 1, step < planes + 1))
+        def _():
+            pass_on(planes - step)
+
+        @pl.when(step >= 2)
+        def _():
+            collect(planes + 1 - step)
+        if filler is not None:
+            filler(step)
+        return 0
+
+    lax.fori_loop(0, planes + 2, step_body, 0)
+
+    def drain(k, _):
+        for a in every:
+            for j in range(4):
+                pair(a, k, j).wait_send()
+            to_diag(a, k).wait_send()
+            to_near(a, k, 0).wait_send()
+            to_near(a, k, 1).wait_send()
+
+            @pl.when(k > 0)
+            def _():
+                to_far(a, k).wait_send()
+        return 0
+
+    lax.fori_loop(0, planes, drain, 0)
+
+
+def reduce_scratch(partials, planes):
+    shapes = [((p.shape[0] // (planes * 8), p.shape[1]), p.dtype) for p in partials]
+    count, far = len(partials), max(planes - 1, 1)
+    dma = pltpu.SemaphoreType.DMA
+    buffers = [pltpu.VMEM(lead + shape, kind) for lead in ((planes, 4), (planes, 4), (planes,), (planes, 2), (far,)) for shape, kind in shapes]
+    return shapes, buffers, [
+        dma((count, planes, 4)), dma((count, planes, 4)), dma((count, planes, 4)), dma((count, planes, 4)),
+        dma((count, planes)), dma((count, planes, 2)), dma((count, far))]
+
+
+def reduce_kernel(planes, count, *refs):
+    buffers = [refs[(2 + i) * count:(3 + i) * count] for i in range(5)]
+    reduce_steps(planes, refs[:count], refs[count:2 * count], buffers, refs[7 * count:], None)
 
 
 def reduce_scatter(partials, planes, collective_id):
-    count, blocks = len(partials), planes * 8
-    shapes = [((p.shape[0] // blocks, p.shape[1]), p.dtype) for p in partials]
-    sends, far = planes * 4 - 1, max(planes - 1, 1)
-    scratch = [pltpu.VMEM(lead + shape, kind) for lead in ((planes, 4), (planes, 4), (planes,), (planes, 2), (far,)) for shape, kind in shapes]
-    dma = pltpu.SemaphoreType.DMA
+    count = len(partials)
+    shapes, buffers, semaphores = reduce_scratch(partials, planes)
     return pl.pallas_call(
         functools.partial(reduce_kernel, planes, count),
         out_shape=[jax.ShapeDtypeStruct(shape, jnp.float32) for shape, _ in shapes],
         in_specs=[ANYSPEC] * count, out_specs=[pl.BlockSpec(memory_space=pltpu.VMEM)] * count,
-        scratch_shapes=scratch + [
-            dma((count, planes, 4)), dma((count, planes, 4)), dma((count, planes, 4)), dma((count, sends)),
-            dma((count, planes)), dma((count, planes, 2)), dma((count, far))],
+        scratch_shapes=buffers + semaphores,
         compiler_params=pltpu.CompilerParams(collective_id=collective_id, has_side_effects=True, vmem_limit_bytes=48 * 2**20),
     )(*partials)
 
@@ -310,6 +345,490 @@
         scratch_shapes=[pltpu.VMEM((7,) + value.shape, jnp.float32), pltpu.SemaphoreType.DMA((7,)), pltpu.SemaphoreType.DMA((7,))],
         compiler_params=pltpu.CompilerParams(collective_id=collective_id, has_side_effects=True),
     )(value)
+
+
+def finish_kernel(planes, proj_ref, outp_ref, small_ref, proj_out, outp_out, small_out, proj_own, outp_own, proj_in, outp_in,
+                  slices, far_slices, own_sem, swap_send, swap_recv, down_send, down_recv, up_send, up_recv,
+                  slice_send, slice_recv, far_send, far_recv, whole_send, whole_recv):
+    z, r, c = place()
+    here = r * 4 + c
+    group = [(z, r ^ (j >> 2), c ^ (j & 3)) for j in range(1, 8)]
+    greet(group + [(z ^ k, r, c) for k in range(1, planes)])
+    width = proj_ref.shape[1] // 3
+    depth, out_width = proj_ref.shape[0] // 4, outp_ref.shape[1] // 4
+    out_rows, step = outp_ref.shape[0], proj_ref.shape[0] // 16
+    chunks = 16
+
+    def remote(source, target, send, recv, device):
+        return pltpu.make_async_remote_copy(
+            src_ref=source, dst_ref=target, send_sem=send, recv_sem=recv, device_id=device, device_id_type=MESH)
+
+    def piece(i, target):
+        if i < 12:
+            a, m = i // 4, i % 4
+            return proj_ref.at[pl.ds(pl.multiple_of(target * depth + m * step, step), step), pl.ds(a * width, width)]
+        return outp_ref.at[:, pl.ds(pl.multiple_of(target * out_width, out_width), out_width)]
+
+    def spot(i, origin):
+        a, m = i // 4, i % 4
+        return proj_own.at[a, pl.ds(m * step, step), pl.ds(pl.multiple_of(origin * width, width), width)]
+
+    def rows(proj, outp, i):
+        if i < 12:
+            return proj.at[i // 4, pl.ds((i % 4) * step, step), :]
+        return outp.at[pl.ds((i - 12) * out_rows, out_rows), :]
+
+    small_copies = []
+    for j in range(1, 8):
+        copy = remote(small_ref.at[here ^ j], slices.at[here], slice_send.at[j], slice_recv.at[here], group[j - 1])
+        copy.start()
+        small_copies.append(copy)
+
+    order = [0, 1, 2, 3, 12, 13, 4, 5, 6, 7, 14, 15, 8, 9, 10, 11]
+    swaps = []
+    for i in order:
+        if i < 12:
+            keep = pltpu.make_async_copy(piece(i, c), spot(i, c), own_sem.at[i])
+            keep.start()
+            for j in range(1, 4):
+                copy = remote(piece(i, c ^ j), spot(i, c), swap_send.at[i, j - 1], swap_recv.at[i, j - 1], (z, r, c ^ j))
+                copy.start()
+                swaps.append(copy)
+        else:
+            @pl.when(c == i - 12)
+            def _():
+                pltpu.make_async_copy(piece(i, c), rows(proj_own, outp_own, i), own_sem.at[i]).start()
+                for j in range(1, 4):
+                    remote(piece(i, c ^ j), rows(proj_own, outp_own, i), swap_send.at[i, j - 1], swap_recv.at[i, 0], (z, r, c ^ j)).start()
+
+    def local_ready(i):
+        target = rows(proj_own, outp_own, i)
+        if i < 12:
+            pltpu.make_async_copy(piece(i, c), spot(i, c), own_sem.at[i]).wait()
+            for j in range(1, 4):
+                arrived = spot(i, c ^ j)
+                remote(arrived, arrived, swap_send.at[i, j - 1], swap_recv.at[i, j - 1], (z, r, c ^ j)).wait_recv()
+        else:
+            @pl.when(c == i - 12)
+            def _():
+                pltpu.make_async_copy(piece(i, c), target, own_sem.at[i]).wait()
+
+            @pl.when(c != i - 12)
+            def _():
+                remote(target, target, swap_send.at[i, 0], swap_recv.at[i, 0], (z, r, c ^ 1)).wait_recv()
+
+    def combine(target, first, second, count):
+        def body(s, _):
+            at = pl.ds(pl.multiple_of(s * 32, 32), 32)
+            total = first[at].astype(jnp.float32) + second[at].astype(jnp.float32)
+            target[at] = total.astype(target.dtype)
+            return 0
+        lax.fori_loop(0, count // 32, body, 0)
+
+    def seat(i):
+        root_low = i % 2 == 0
+        spot_from_root = z if root_low else planes - 1 - z
+        up = (jnp.minimum(z + 1, planes - 1) if root_low else jnp.maximum(z - 1, 0), r, c)
+        down = (jnp.maximum(z - 1, 0) if root_low else jnp.minimum(z + 1, planes - 1), r, c)
+        return spot_from_root, up, down
+
+    def count_of(i):
+        return step if i < 12 else out_rows
+
+    def to_root(i, p):
+        _, up, down = seat(i)
+        own, arriving, result = rows(proj_own, outp_own, i), rows(proj_in, outp_in, i), rows(proj_out, outp_out, i)
+        local_ready(i)
+        if p < planes - 1:
+            remote(arriving, arriving, down_send.at[i], down_recv.at[i], up).wait_recv()
+        if p == 0:
+            combine(result, own, arriving, count_of(i))
+            remote(result, result, up_send.at[i], up_recv.at[i], up).start()
+        else:
+            if p < planes - 1:
+                combine(own, own, arriving, count_of(i))
+            remote(own, arriving, down_send.at[i], down_recv.at[i], down).start()
+
+    def from_root(i, p):
+        _, up, down = seat(i)
+        result = rows(proj_out, outp_out, i)
+        remote(result, result, up_send.at[i], up_recv.at[i], down).wait_recv()
+        if p < planes - 1:
+            remote(result, result, up_send.at[i], up_recv.at[i], up).start()
+
+    def small_group():
+        for j in range(1, 8):
+            arrived = slices.at[here ^ j]
+            remote(arrived, arrived, slice_send.at[0], slice_recv.at[here ^ j], group[j - 1]).wait_recv()
+        slices[here] = small_ref[here]
+        total = slices[0]
+        for j in range(1, 8):
+            total = total + slices[j]
+        far_slices[z] = total
+        for k in range(1, planes):
+            copy = remote(far_slices.at[z], far_slices.at[z], far_send.at[k - 1], far_recv.at[z], (z ^ k, r, c))
+            copy.start()
+            small_copies.append(copy)
+
+    def small_far():
+        for k in range(1, planes):
+            arrived = far_slices.at[z ^ k]
+            remote(arrived, arrived, far_send.at[k - 1], far_recv.at[z ^ k], (z ^ k, r, c)).wait_recv()
+        total = far_slices[0]
+        for k in range(1, planes):
+            total = total + far_slices[k]
+        small_out[here] = total
+        for j in range(1, 8):
+            copy = remote(small_out.at[here], small_out.at[here], whole_send.at[j], whole_recv.at[here], group[j - 1])
+            copy.start()
+            small_copies.append(copy)
+
+    lag = 2
+    hops = 2 * planes - 1
+    for s in range(chunks + (hops - 1) * lag):
+        for h in range(hops):
+            if 0 <= s - h * lag < chunks:
+                i = order[s - h * lag]
+                p = planes - 1 - h if h < planes else h - planes + 1
+
+                @pl.when(seat(i)[0] == p)
+                def _(i=i, p=p, h=h):
+                    if h < planes:
+                        to_root(i, p)
+                    else:
+                        from_root(i, p)
+        if s == 2:
+            small_group()
+        if s == 12:
+            small_far()
+    for j in range(1, 8):
+        arrived = small_out.at[here ^ j]
+        remote(arrived, arrived, whole_send.at[0], whole_recv.at[here ^ j], group[j - 1]).wait_recv()
+    for copy in small_copies + swaps:
+        copy.wait_send()
+    for i in range(12, 16):
+        @pl.when(c == i - 12)
+        def _():
+            for j in range(1, 4):
+                remote(piece(i, c ^ j), rows(proj_own, outp_own, i), swap_send.at[i, j - 1], swap_recv.at[i, 0], (z, r, c ^ j)).wait_send()
+    for i in range(chunks):
+        p, up, down = seat(i)
+        own, arriving, result = rows(proj_own, outp_own, i), rows(proj_in, outp_in, i), rows(proj_out, outp_out, i)
+
+        @pl.when(p > 0)
+        def _():
+            remote(own, arriving, down_send.at[i], down_recv.at[i], down).wait_send()
+
+        @pl.when(p < planes - 1)
+        def _():
+            remote(result, result, up_send.at[i], up_recv.at[i], up).wait_send()
+
+
+def finish(grad_proj_own, grad_out_own, small, planes, collective_id):
+    depth, width = grad_proj_own.shape[0] // 4, grad_proj_own.shape[1] // 3
+    out_rows, out_width = grad_out_own.shape[0], grad_out_own.shape[1] // 4
+    kind = grad_proj_own.dtype
+    proj, outp = (3, depth, 4 * width), (4 * out_rows, out_width)
+    vmem = pl.BlockSpec(memory_space=pltpu.VMEM)
+    dma = pltpu.SemaphoreType.DMA
+    return pl.pallas_call(
+        functools.partial(finish_kernel, planes),
+        out_shape=[jax.ShapeDtypeStruct(proj, kind), jax.ShapeDtypeStruct(outp, kind), jax.ShapeDtypeStruct(small.shape, small.dtype)],
+        in_specs=[ANYSPEC, ANYSPEC, vmem], out_specs=[vmem, vmem, vmem],
+        scratch_shapes=[
+            pltpu.VMEM(proj, kind), pltpu.VMEM(outp, kind), pltpu.VMEM(proj, kind), pltpu.VMEM(outp, kind),
+            pltpu.VMEM(small.shape, jnp.float32), pltpu.VMEM((planes,) + small.shape[1:], jnp.float32),
+            dma((16,)), dma((16, 3)), dma((16, 3)), dma((16,)), dma((16,)), dma((16,)), dma((16,)),
+            dma((8,)), dma((8,)), dma((planes,)), dma((planes,)), dma((8,)), dma((8,))],
+        compiler_params=pltpu.CompilerParams(collective_id=collective_id, has_side_effects=True, vmem_limit_bytes=40 * 2**20),
+    )(grad_proj_own, grad_out_own, small)
+
+
+def expert_kernel(planes, experts, own_h, own_side, cot, w_gate, w_up, w_down,
+                  all_h, all_side, entry_out, route_out, active_out, grad_gate_out, grad_up_out,
+                  gate_use, up_use, down_use, rows_h, rows_c, rows_side, back_rows,
+                  gate_rows, up_rows, active_rows, grad_gate, grad_up, entry_stage, route_stage,
+                  weight_sem, own_sem, send_sem, recv_sem, cot_sem, load_sem, store_sem):
+    z, r, c = place()
+    first, second, diag = c ^ (1 + r), c ^ (2 - r), c ^ 3
+    partner = (z, 1 - r, c)
+    to_first, to_second = (z, r, first), (z, r, second)
+    count = own_h.shape[0]
+    group = 4 * count
+    expert = z * 4 + c
+    half = count // 2
+    pieces = [(own_h, all_h, 0, half), (own_h, all_h, half, half), (own_side, all_side, 0, count)]
+
+    weights = [(w_gate, gate_use), (w_up, up_use), (w_down, down_use)]
+    for i, (source, target) in enumerate(weights):
+        pltpu.make_async_copy(source, target, weight_sem.at[i]).start()
+
+    def number(zz, rr, cc):
+        return (zz * 2 + rr) * 4 + cc
+
+    def spot(i, which):
+        _, target, start, size = pieces[i]
+        return target.at[pl.ds(pl.multiple_of(which * count + start, size), size)]
+
+    def copy_of(i, source, which, k, slot, device):
+        return pltpu.make_async_remote_copy(
+            src_ref=source, dst_ref=spot(i, which), send_sem=send_sem.at[i, k, slot], recv_sem=recv_sem.at[i, which],
+            device_id=device, device_id_type=MESH)
+
+    def own_piece(i):
+        source, _, start, size = pieces[i]
+        return source.at[pl.ds(start, size)]
+
+    def await_block(i, which):
+        copy_of(i, spot(i, which), which, 0, 0, partner).wait_recv()
+
+    def forward(which, k, targets):
+        for i in range(3):
+            await_block(i, which)
+            for slot, device in targets:
+                copy_of(i, spot(i, which), which, k, slot, device).start()
+
+    greet([to_first, to_second, partner] + [(z ^ k, r, c) for k in range(1, planes)])
+    mine = number(z, r, c)
+    for i in range(3):
+        for slot, device in ((0, to_first), (1, to_second)):
+            copy_of(i, own_piece(i), mine, 0, slot, device).start()
+        for k in range(1, planes):
+            copy_of(i, own_piece(i), mine, k, 7, (z ^ k, r, c)).start()
+        copy_of(i, own_piece(i), mine, 0, 2, partner).start()
+    keeps = [pltpu.make_async_copy(own_piece(i), spot(i, mine), own_sem.at[i]) for i in range(3)]
+    for keep in keeps:
+        keep.start()
+
+    def base_of(k, rr):
+        return pl.multiple_of(number(z ^ k, rr, 0) * count, group)
+
+    def dot(left, right):
+        return jnp.dot(left, right, preferred_element_type=jnp.float32)
+
+    def dot_turned(left, right):
+        return lax.dot_general(left, right, (((1,), (1,)), ((), ())), preferred_element_type=jnp.float32)
+
+    def cot_copy(g):
+        rr = jnp.where(g % 2 == 0, r, 1 - r)
+        return pltpu.make_async_copy(cot.at[pl.ds(base_of(g // 2, rr), group)], rows_c.at[g % 2], cot_sem.at[g % 2])
+
+    cot_copy(0).start()
+    for i, (source, target) in enumerate(weights):
+        pltpu.make_async_copy(source, target, weight_sem.at[i]).wait()
+
+    def back_body(g, _):
+        @pl.when(g + 1 < 2 * planes)
+        def _():
+            cot_copy(g + 1).start()
+
+        cot_copy(g).wait()
+        back_rows[g] = dot_turned(rows_c[g % 2], down_use[...])
+        return 0
+
+    lax.fori_loop(0, 2 * planes, back_body, 0)
+    for keep in keeps:
+        keep.wait()
+
+    def stores(k, rr, slot):
+        at = pl.ds(base_of(k, rr), group)
+        return [
+            pltpu.make_async_copy(source.at[slot], target.at[at], store_sem.at[slot, i])
+            for i, (source, target) in enumerate((
+                (entry_stage, entry_out), (route_stage, route_out), (active_rows, active_out),
+                (grad_gate, grad_gate_out), (grad_up, grad_up_out)))]
+
+    def compute(k, rr, slot):
+        at = pl.ds(base_of(k, rr), group)
+        loads = [pltpu.make_async_copy(all_h.at[at], rows_h, load_sem.at[0]),
+                 pltpu.make_async_copy(all_side.at[at], rows_side, load_sem.at[1])]
+        for load in loads:
+            load.start()
+        for load in loads:
+            load.wait()
+        gate_rows[...] = dot(rows_h[...], gate_use[...])
+        up_rows[...] = dot(rows_h[...], up_use[...])
+
+        @pl.when(k > 0)
+        def _():
+            for store in stores(k, rr, slot):
+                store.wait()
+
+        part = 64
+        lane = lax.broadcasted_iota(jnp.int32, (part, rows_side.shape[1]), 1)
+
+        @pl.loop(0, group // part)
+        def _(t):
+            at = pl.ds(pl.multiple_of(t * part, part), part)
+            mask = (lane == expert) | (lane == expert + experts)
+            share = jnp.sum(jnp.where(mask, rows_side[at, :].astype(jnp.float32), 0.0), axis=1, keepdims=True)
+            gate, up, back = gate_rows[at, :], up_rows[at, :], back_rows[2 * k + slot, at, :]
+            squash = jax.nn.sigmoid(gate)
+            silu = gate * squash
+            active = silu * up
+            route = jnp.sum(active * back, axis=1, keepdims=True)
+            route_stage[slot, at, :] = jnp.where(lane == expert, route, 0.0).astype(jnp.bfloat16)
+            active_rows[slot, at, :] = (share * active).astype(jnp.bfloat16)
+            grad_active = share * back
+            grad_gate[slot, at, :] = (grad_active * up * squash * (1.0 + gate * (1.0 - squash))).astype(jnp.bfloat16)
+            grad_up[slot, at, :] = (grad_active * silu).astype(jnp.bfloat16)
+
+        entry = dot_turned(grad_gate[slot], gate_use[...]) + dot_turned(grad_up[slot], up_use[...])
+        entry_stage[slot] = entry.astype(jnp.bfloat16)
+        for store in stores(k, rr, slot):
+            store.start()
+
+    def step_body(step, _):
+        @pl.when(jnp.logical_and(step > 0, step < planes))
+        def _():
+            forward(number(z ^ step, r, c), step, ((0, to_first), (1, to_second), (2, partner)))
+
+        @pl.when(jnp.logical_and(step >= 1, step < planes + 1))
+        def _():
+            k = step - 1
+            forward(number(z ^ k, r, first), k, ((3, to_second), (4, partner)))
+            forward(number(z ^ k, r, second), k, ((5, partner),))
+
+        @pl.when(jnp.logical_and(step >= 2, step < planes + 2))
+        def _():
+            k = step - 2
+            forward(number(z ^ k, r, diag), k, ((6, partner),))
+            compute(k, r, 0)
+
+        @pl.when(jnp.logical_and(step >= 3, step < planes + 3))
+        def _():
+            k = step - 3
+            for j in range(4):
+                for i in range(3):
+                    await_block(i, number(z ^ k, 1 - r, c ^ j))
+            compute(k, 1 - r, 1)
+        return 0
+
+    lax.fori_loop(0, planes + 3, step_body, 0)
+    for slot, rr in ((0, r), (1, 1 - r)):
+        for store in stores(planes - 1, rr, slot):
+            store.wait()
+
+    def drain(k, _):
+        for i in range(3):
+            for slot in range(7):
+                copy_of(i, spot(i, mine), mine, k, slot, partner).wait_send()
+
+            @pl.when(k > 0)
+            def _():
+                copy_of(i, spot(i, mine), mine, k, 7, partner).wait_send()
+        return 0
+
+    lax.fori_loop(0, planes, drain, 0)
+
+
+def expert_rows_on_links(normal_h, side, all_cotangent, w_gate, w_up, w_down, experts, collective_id):
+    planes = lax.axis_size("dp")
+    count, width = normal_h.shape
+    hidden = w_gate.shape[1]
+    total, group, low, wide = planes * 8 * count, 4 * count, jnp.bfloat16, jnp.float32
+    sides = side.shape[1]
+    vmem, dma = pltpu.VMEM, pltpu.SemaphoreType.DMA
+    outs = [jax.ShapeDtypeStruct((total, n), low) for n in (width, sides, width, sides, hidden, hidden, hidden)]
+    return pl.pallas_call(
+        functools.partial(expert_kernel, planes, experts),
+        out_shape=outs, in_specs=[ANYSPEC] * 6, out_specs=[ANYSPEC] * 7,
+        scratch_shapes=[
+            vmem((width, hidden), low), vmem((width, hidden), low), vmem((hidden, width), low),
+            vmem((group, width), low), vmem((2, group, width), low), vmem((group, sides), low), vmem((2 * planes, group, hidden), wide),
+            vmem((group, hidden), wide), vmem((group, hidden), wide),
+            vmem((2, group, hidden), low), vmem((2, group, hidden), low), vmem((2, group, hidden), low),
+            vmem((2, group, width), low), vmem((2, group, sides), low),
+            dma((3,)), dma((3,)), dma((3, planes, 8)), dma((3, planes * 8)), dma((2,)), dma((2,)), dma((2, 5))],
+        compiler_params=pltpu.CompilerParams(collective_id=collective_id, has_side_effects=True, vmem_limit_bytes=60 * 2**20),
+    )(normal_h, side, all_cotangent, w_gate, w_up, w_down)
+
+
+def entry_kernel(planes, entry_part, route_part, all_h, cot, active, grad_gate, grad_up, w_down,
+                 entry_out, route_out, mixed_out, acc_gate, acc_up, acc_down, *scratch):
+    buffers = [scratch[2 * i:2 * i + 2] for i in range(5)]
+    semaphores = scratch[10:17]
+    down_use, rows_h, rows_c, rows_x, mixed_stage, down_sem, load_sem, store_sem = scratch[17:]
+    group = rows_h.shape[1]
+    groups = all_h.shape[0] // group
+
+    def loads(g):
+        slot = g % 2
+        at = pl.ds(pl.multiple_of(g * group, group), group)
+        pairs = [(all_h, rows_h.at[slot]), (cot, rows_c.at[slot])] + [
+            (source, rows_x.at[slot, i]) for i, source in enumerate((active, grad_gate, grad_up))]
+        return [pltpu.make_async_copy(source.at[at], target, load_sem.at[slot, i]) for i, (source, target) in enumerate(pairs)]
+
+    def store(g):
+        at = pl.ds(pl.multiple_of(g * group, group), group)
+        return pltpu.make_async_copy(mixed_stage, mixed_out.at[at], store_sem.at[0])
+
+    def turned(left, right):
+        return lax.dot_general(left, right, (((0,), (0,)), ((), ())), preferred_element_type=jnp.float32)
+
+    down = pltpu.make_async_copy(w_down, down_use, down_sem.at[0])
+    down.start()
+    for load in loads(0):
+        load.start()
+    for acc in (acc_gate, acc_up, acc_down):
+        @pl.loop(0, acc.shape[0] // 32)
+        def _(t, acc=acc):
+            acc[pl.ds(pl.multiple_of(t * 32, 32), 32), :] = jnp.zeros((32, acc.shape[1]), jnp.float32)
+    down.wait()
+
+    def one(g):
+        @pl.when(g + 1 < groups)
+        def _():
+            for load in loads(g + 1):
+                load.start()
+
+        for load in loads(g):
+            load.wait()
+        slot = g % 2
+        acc_gate[...] += turned(rows_h[slot], rows_x[slot, 1])
+        acc_up[...] += turned(rows_h[slot], rows_x[slot, 2])
+        acc_down[...] += turned(rows_x[slot, 0], rows_c[slot])
+
+        @pl.when(g > 0)
+        def _():
+            store(g - 1).wait()
+
+        mixed_stage[...] = jnp.dot(rows_x[slot, 0], down_use[...], preferred_element_type=jnp.float32).astype(jnp.bfloat16)
+        store(g).start()
+
+    steps = planes + 2
+    per_step = -(-groups // (steps - 2))
+
+    def filler(step):
+        def body(i, _):
+            @pl.when(step * per_step + i < groups)
+            def _():
+                one(step * per_step + i)
+            return 0
+        lax.fori_loop(0, per_step, body, 0)
+
+    reduce_steps(planes, (entry_part, route_part), (entry_out, route_out), buffers, semaphores, filler)
+    store(groups - 1).wait()
+
+
+def entry_sums(entry_part, route_part, all_h, cot, active, grad_gate, grad_up, w_down, collective_id):
+    planes = lax.axis_size("dp")
+    partials = [entry_part, route_part]
+    shapes, buffers, semaphores = reduce_scratch(partials, planes)
+    (count, width), hidden, group = shapes[0][0], w_down.shape[0], 256
+    low, wide, vmem, dma = jnp.bfloat16, jnp.float32, pltpu.VMEM, pltpu.SemaphoreType.DMA
+    kept = pl.BlockSpec(memory_space=pltpu.VMEM)
+    return pl.pallas_call(
+        functools.partial(entry_kernel, planes),
+        out_shape=[jax.ShapeDtypeStruct(shape, wide) for shape, _ in shapes] + [
+            jax.ShapeDtypeStruct(entry_part.shape, low), jax.ShapeDtypeStruct((width, hidden), wide),
+            jax.ShapeDtypeStruct((width, hidden), wide), jax.ShapeDtypeStruct((hidden, width), wide)],
+        in_specs=[ANYSPEC] * 8, out_specs=[kept, kept, ANYSPEC, kept, kept, kept],
+        scratch_shapes=buffers + semaphores + [
+            vmem((hidden, width), low), vmem((2, group, width), low), vmem((2, group, width), low), vmem((2, 3, group, hidden), low),
+            vmem((group, width), low), dma((1,)), dma((2, 5)), dma((1,))],
+        compiler_params=pltpu.CompilerParams(collective_id=collective_id, has_side_effects=True, vmem_limit_bytes=60 * 2**20),
+    )(entry_part, route_part, all_h, cot, active, grad_gate, grad_up, w_down)
 
 
 HEAD_DIM = 128
@@ -487,7 +1006,16 @@
 
 
 def expert_rows(normal_h, side, cotangent, gate_use, up_use, down_use, expert_count):
-    (all_cotangent,) = gather_tokens([cotangent], True, 3, 2)
+    all_cotangent = lax.all_gather(cotangent, EVERYONE, axis=0, tiled=True)
+    if on_links():
+        rows_h, _, entry_part, grad_side, active_share, grad_gate_rows, grad_up_rows = expert_rows_on_links(
+            normal_h, side, all_cotangent, gate_use, up_use, down_use, expert_count, 6
+        )
+        entry_rows, grad_probs_all, out_part, *grads = entry_sums(
+            entry_part, grad_side, rows_h, all_cotangent, active_share, grad_gate_rows, grad_up_rows, down_use, 7
+        )
+        (mixture,) = scatter_sums([out_part], True, 8)
+        return (entry_rows, grad_probs_all, mixture, *grads)
     rows_h, rows_side = gather_tokens([normal_h, side], True, 6, 2)
     expert = lax.axis_index("dp") * lax.axis_size("col") + lax.axis_index("col")
     lane = jnp.arange(side.shape[1])
@@ -663,7 +1191,6 @@
     grad_proj_own = contract_rows(gathered_x, grad_raw).astype(jnp.bfloat16)
     grad_input_part, grad_attn_gain = norm_backward(inputs, inv_input, norm_attn, grad_normal_x)
     grad_input = grad_state + grad_input_part
-    grad_query, grad_key, grad_value, grad_out_proj = weight_sums(grad_proj_own, grad_out_own)
     full_width = query_gain.shape[0]
     padded_qgain = lax.dynamic_update_slice_in_dim(
         jnp.zeros((full_width,), jnp.float32), grad_qgain_part, offset, 0
@@ -671,10 +1198,9 @@
     padded_kgain = lax.dynamic_update_slice_in_dim(
         jnp.zeros((full_width,), jnp.float32), grad_kgain_part, offset, 0
     )
-    grad_norm_attn, grad_query_gain, grad_key_gain, grad_norm_moe, grad_router = lax.psum(
-        (grad_attn_gain, padded_qgain, padded_kgain, grad_moe_part, grad_router_part),
-        ("dp", "row", "col"),
-    )
+    small = (grad_attn_gain, padded_qgain, padded_kgain, grad_moe_part, grad_router_part)
+    grad_query, grad_key, grad_value, grad_out_proj, small = last_sums(grad_proj_own, grad_out_own, small)
+    grad_norm_attn, grad_query_gain, grad_key_gain, grad_norm_moe, grad_router = small
     return (
         block_out,
         grad_input,
@@ -693,14 +1219,22 @@
     )
 
 
-def weight_sums(grad_proj_own, grad_out_own):
+def last_sums(grad_proj_own, grad_out_own, small):
+    if on_links():
+        flat = jnp.concatenate([part.reshape(-1) for part in small])
+        proj, outp, total = finish(grad_proj_own, grad_out_own, flat.reshape(8, -1, 128), lax.axis_size("dp"), 12)
+        total, sums, start = total.reshape(-1), [], 0
+        for part in small:
+            sums.append(total[start : start + part.size].reshape(part.shape))
+            start += part.size
+        return (*(proj[a].astype(jnp.float32) for a in range(3)), outp.astype(jnp.float32), sums)
     width = grad_proj_own.shape[1] // 3
     blocks = [
         lax.all_to_all(grad_proj_own[:, a * width : (a + 1) * width], "col", split_axis=0, concat_axis=1, tiled=True)
         for a in range(3)
     ]
     out_block = lax.all_to_all(grad_out_own, "col", split_axis=1, concat_axis=0, tiled=True)
-    return [total.astype(jnp.float32) for total in lax.psum((*blocks, out_block), "dp")]
+    return (*(total.astype(jnp.float32) for total in lax.psum((*blocks, out_block), "dp")), lax.psum(small, EVERYONE))
 
 
 def solution(mesh):

time: 1060 us -> 782 us (0.74)
  waiting for transfers between devices: 168 us -> 0.68 us
  matrix products: 196 us -> 38 us
  Pallas kernels: 508 us -> 635 us
  blocking collectives: 77.6 us -> 0 us
  local copies, waits for them, and re-layouts: 27 us -> 40.3 us
  starting transfers between devices: 11.3 us -> 0.04 us
    pallas_call x0 -> x3, Pallas kernels: none -> 365 us  [the longest x1 131 us: finish(): pl.pallas_call(functools.partial(finish_kernel, planes), out_shape=[jax.S...]
    pallas_call x4 -> x2, Pallas kernels: 215 us -> 47.4 us  [gather(): pl.pallas_call(functools.partial(gather_kernel, planes, parts, count), ou...]
    psum x2 -> x0, waiting for transfers between devices: 154 us -> none  [the longest x1 119 us: per_device(): lax.psum((grad_attn_gain, padded_qgain, padded_kgain, grad_moe_part, grad...]
    pallas_call x4 -> x3, Pallas kernels: 232 us -> 134 us  [reduce_scatter(): pl.pallas_call(functools.partial(reduce_kernel, planes, count), out_shape...]
    dot_general x6 -> x3, matrix products: 72.4 us -> 7.69 us  [contract_cols(): lax.dot_general(left, right, (((1,), (1,)), ((), ())), preferred_element_...]
    dot_general x6 -> x3, matrix products: 53.4 us -> 7.48 us  [contract_rows(): lax.dot_general(left, right, (((0,), (0,)), ((), ())), preferred_element_...]
    psum x1 -> x0, blocking collectives: 45.3 us -> none  [per_device(): lax.psum((grad_attn_gain, padded_qgain, padded_kgain, grad_moe_part, grad...]
    dot_general x6 -> x3, matrix products: 54.2 us -> 8.94 us  [contract(): return jnp.dot(left, right, preferred_element_type=jnp.float32)]
  transfers between devices with their start and end apart: 4 -> 1, of which waited for: 4 -> 0; matrix products, arithmetic and copies ran while one was open for 7% -> 6% of each run, Pallas kernels for 2% -> 17%
where the time goes in v2:
time: 782 us; the launch traced here: 772 us
  Pallas kernels  635 us (81%)
  other arithmetic  42.3 us (5%)
  local copies, waits for them, and re-layouts  40.3 us (5%)
  matrix products  38 us (5%)
  between operations  15.6 us (2%)
    pallas_call x3, Pallas kernels, reduce_scatter(): pl.pallas_call(functools.partial(reduce_kernel, planes, count), out_shape...  134 us
    pallas_call x1, Pallas kernels, finish(): pl.pallas_call(functools.partial(finish_kernel, planes), out_shape=[jax.S...  131 us
    pallas_call x1, Pallas kernels, expert_rows_on_links(): pl.pallas_call(functools.partial(expert_kernel, planes, experts), out_sha...  127 us
    pallas_call x1, Pallas kernels, entry_sums(): pl.pallas_call(functools.partial(entry_kernel, planes), out_shape=[jax.Sh...  107 us
    pallas_call x1, Pallas kernels, exchange_weights(): pl.pallas_call(exchange_kernel, out_shape=[jax.ShapeDtypeStruct((depth *...  74.4 us
    pallas_call x2, Pallas kernels, gather(): pl.pallas_call(functools.partial(gather_kernel, planes, parts, count), ou...  47.4 us
    unnamed x160, local copies, waits for them, and re-layouts  20.7 us
  transfers between devices with their start and end apart: 1, of which 0 were waited for; matrix products, arithmetic and copies ran while one was open for 6% of the time, Pallas kernels for 17%

profile of v2, /device:TPU:6, one launch (start us, length us, event | category | flops | bytes accessed | tf_op | source)
XLA Modules:
  0.0 771.6 jit_solution(17404331885127270099)
XLA Ops:
  7.9 1.2 fusion.24
  10.2 2.0 fusion.26.refs_0_
  12.2 25.9 %shard_map.264 = bf16[1024,2048]{1,0:T(8,128)(2,1)} custom-call(bf16[128,2048]{1,0:T(8,128)(2,1)} %fusion.26.refs_0_), custom_call_target="tpu_custom_call" | custom-call | tf_op jit(solution)/shard_map/pallas_call | solution.py:100
  38.1 74.4 %shard_map.265 = (bf16[2048,768]{1,0:T(8,128)(2,1)}, bf16[256,2048]{1,0:T(8,128)(2,1)}) custom-call(bf16[512,1024]{1,0:T(8,128)(2,1)} %wq_ref.1, bf16[512,1024]{1,0:T(8,128)(2,1)} %wk_ref.1, bf16[512,1024]{1,0:T(8,128)(2,1)} %wv_ref.1, bf16[1024,512]{1,0:T(8,128)(2,1)} %wo_ref.1), custom_call_target="tpu_custom_call" | custom-call | tf_op jit(solution)/shard_map/pallas_call | solution.py:309
  112.5 6.2 fusion.74
  118.8 0.9 slice.240
  120.6 6.6 shard_map.266
  129.4 1.6 multiply_multiply_fusion.1
  131.0 1.6 copy.110
  132.5 1.6 copy.113
  134.4 2.9 broadcast_multiply_fusion.2
  140.2 0.9 select_reduce_fusion
  141.1 1.1 fusion
  143.6 1.5 fusion.21
  146.0 1.3 convolution_convert_fusion.refs_0_
  147.3 22.8 %shard_map.267 = f32[128,2048]{1,0:T(8,128)S(1)} custom-call(bf16[1024,2048]{1,0:T(8,128)(2,1)S(1)} %convolution_convert_fusion.refs_0_), custom_call_target="tpu_custom_call" | custom-call | tf_op jit(solution)/shard_map/pallas_call | solution.py:258
  171.8 1.4 fusion.75
  174.1 1.3 convert_reduce_fusion
  175.3 1.4 copy.119
  176.8 2.1 copy.129
  178.8 2.0 copy.128
  181.0 0.8 fusion.57
  181.8 1.3 log_add_fusion.1
  183.1 1.3 log_add_fusion
  185.0 0.9 multiply_convert_fusion.4
  186.7 126.8 %shard_map.268 = (bf16[4096,2048]{1,0:T(8,128)(2,1)}, bf16[4096,128]{1,0:T(8,128)(2,1)}, bf16[4096,2048]{1,0:T(8,128)(2,1)}, bf16[4096,128]{1,0:T(8,128)(2,1)}, ...) custom-call(bf16[128,2048]{1,0:T(8,128)(2,1)} %copy-done.12, ...), custom_call_target="tpu_custom_call" | custom-call | tf_op jit(solution)/shard_map/pallas_call | solution.py:733
  313.5 107.2 %shard_map.269 = (f32[128,2048]{1,0:T(8,128)}, f32[128,128]{1,0:T(8,128)}, bf16[4096,2048]{1,0:T(8,128)(2,1)}, f32[2048,512]{1,0:T(8,128)}, f32[2048,512]{1,0:T(8,128)}, /*index=5*/f32[512,2048]{1,0:T(8,128)}) custom-call(bf16[4096,2048]{1,0:T(8,128)(2,1)} %get-tuple-element.97.entry_part, bf16[4096,128]{1,0:T(8,128)(2,1)} %get-tuple-element.98.route_part, ...), custom_call_target="tpu_custom_call" | custom-call | tf_op jit(solution)/shard_map/pallas_call | solution.py:821
  420.8 1.0 multiply_reduce_fusion.10
  421.8 1.0 multiply_convert_fusion.3
  422.8 89.3 %shard_map.270 = f32[128,2048]{1,0:T(8,128)S(1)} custom-call(bf16[4096,2048]{1,0:T(8,128)(2,1)} %get-tuple-element.103.refs_0_), custom_call_target="tpu_custom_call" | custom-call | tf_op jit(solution)/shard_map/pallas_call | solution.py:258
  513.2 1.8 fusion.69
  514.9 21.6 %shard_map.271 = bf16[1024,2048]{1,0:T(8,128)(2,1)} custom-call(bf16[128,2048]{1,0:T(8,128)(2,1)} %get-tuple-element.167.refs_0_), custom_call_target="tpu_custom_call" | custom-call | tf_op jit(solution)/shard_map/pallas_call | solution.py:100
  536.5 3.5 convolution_convert_fusion.4
  542.8 1.5 convolution_bitcast_fusion.2
  544.3 1.3 fusion.77
  545.6 1.3 convolution_convert_fusion.3.outp_ref
  546.9 0.9 copy-done.4
  548.0 1.7 multiply_reduce_fusion
  549.7 1.4 multiply_convert_fusion
  552.3 1.1 fusion.70
  553.4 1.0 broadcast_multiply_fusion
  555.4 1.4 maximum_add_fusion
  556.8 1.6 copy.135
  558.4 1.3 pad_maximum_fusion.1
  559.8 3.5 fusion.41
  563.8 6.7 shard_map.272
  571.2 3.7 fusion.17
  575.6 1.3 copy-done.75
  576.9 3.7 convolution_convert_fusion.1.refs_0_
  580.6 4.9 convolution_convert_fusion.2.proj_ref
  585.5 22.3 %shard_map.273 = f32[128,2048]{1,0:T(8,128)S(1)} custom-call(bf16[1024,2048]{1,0:T(8,128)(2,1)S(1)} %convolution_convert_fusion.1.refs_0_), custom_call_target="tpu_custom_call" | custom-call | tf_op jit(solution)/shard_map/pallas_call | solution.py:258
  609.1 1.9 copy-done.2
  610.9 131.3 %shard_map.274 = (bf16[3,512,1024]{2,1,0:T(8,128)(2,1)S(1)}, bf16[1024,512]{1,0:T(8,128)(2,1)S(1)}, f32[8,40,128]{2,1,0:T(8,128)S(1)}) custom-call(bf16[2048,768]{1,0:T(8,128)(2,1)S(1)} %copy-done.2, bf16[256,2048]{1,0:T(8,128)(2,1)S(1)} %convolution_convert_fusion.3.outp_ref, f32[8,40,128]{2,1,0:T(8,128)S(1)} %bitcast.113), custom_call_target="tpu_custom_call" | custom-call | tf_op jit(solution)/shard_map/pallas_call | solution.py:534
  742.3 2.9 bitcast_convert_fusion
  745.2 1.4 slice.229
  746.7 2.3 slice.252
  749.0 2.2 copy.138
  751.2 1.6 convert_element_type.140
  753.4 1.5 fusion.30
  754.9 2.1 copy.163
  757.0 1.6 copy-done.29
  758.6 2.1 copy.164
  760.7 1.6 copy-done.28
  762.3 2.0 copy.165
  (201 shorter events, 24.0 us)
Async XLA Ops:
  7.2 164.6 %copy-start = (bf16[2048,16]{0,1:T(8,128)(2,1)S(1)}, bf16[2048,16]{0,1:T(8,128)(2,1)}, u32[]{:S(2)}) copy-start(bf16[2048,16]{0,1:T(8,128)(2,1)} %param.37) | copy-start | bytes 196612
  7.2 179.5 %all-gather.2.cloned.1.call-start = ((), (), s32[]{:S(2)}) async-start(), calls=%async_computation | async-start | bytes 17301504 | tf_op jit(solution)/shard_map/all_gather | solution.py:1009
  118.7 12.3 %copy-start.5 = (f32[1024,768]{0,1:T(8,128)}, f32[1024,768]{0,1:T(8,128)S(1)}, u32[]{:S(2)}) copy-start(f32[1024,768]{0,1:T(8,128)S(1)} %get-tuple-element.212) | copy-start | bytes 9437188
  118.7 23.4 %copy-start.40 = (bf16[512,256]{0,1:T(8,128)(2,1)}, bf16[512,256]{0,1:T(8,128)(2,1)S(1)}, u32[]{:S(2)}) copy-start(bf16[512,256]{0,1:T(8,128)(2,1)S(1)} %slice.231) | copy-start | bytes 786436
  127.9 3.0 copy-start.62
  128.7 2.3 copy-start.64
  129.4 1.6 copy-start.51
  129.4 1.6 copy-start.53
  137.7 5.3 copy-start.7
  139.2 1.9 copy-start.14
  139.2 1.9 copy-start.23
  139.7 2.5 copy-start.56
  140.1 2.0 copy-start.58
  141.1 2.0 copy-start.3
  141.1 2.0 copy-start.57
  142.2 1.4 copy-start.36
  143.6 2.4 copy-start.43
  147.3 22.8 %copy-start.9 = (bf16[128,2048]{1,0:T(8,128)(2,1)S(1)}, bf16[128,2048]{1,0:T(8,128)(2,1)}, u32[]{:S(2)}) copy-start(bf16[128,2048]{1,0:T(8,128)(2,1)} %param.27) | copy-start | bytes 1572868
  147.3 23.6 %copy-start.47 = (f32[2048]{0:T(1024)S(1)}, f32[2048]{0:T(1024)}, u32[]{:S(2)}) copy-start(f32[2048]{0:T(1024)} %param.36) | copy-start | bytes 24580
  170.1 14.3 %copy-start.49 = (f32[16,128]{1,0:T(8,128)S(1)}, f32[16,128]{1,0:T(8,128)}, u32[]{:S(2)}) copy-start(f32[16,128]{1,0:T(8,128)} %shard_map.266) | copy-start | bytes 24580
  170.9 2.4 copy-start.71
  181.8 3.2 copy-start.67
  313.5 107.2 %copy-start.39 = (f32[128,16]{1,0:T(8,128)S(1)}, f32[128,16]{1,0:T(8,128)}, u32[]{:S(2)}) copy-start(f32[128,16]{1,0:T(8,128)} %copy.119) | copy-start | bytes 24580
  313.5 107.2 %copy-start.66 = (f32[128]{0:T(128)S(1)}, f32[128]{0:T(128)}, u32[]{:S(2)}) copy-start(f32[128]{0:T(128)} %get-tuple-element.217) | copy-start | bytes 1540
  313.5 107.2 %copy-start.68 = (f32[128]{0:T(128)S(1)}, f32[128]{0:T(128)}, u32[]{:S(2)}) copy-start(f32[128]{0:T(128)} %copy-done.67) | copy-start | bytes 1540
  422.8 89.4 %copy-start.45 = (bf16[128,16]{1,0:T(8,128)(2,1)}, bf16[128,16]{1,0:T(8,128)(2,1)S(1)}, u32[]{:S(2)}) copy-start(bf16[128,16]{1,0:T(8,128)(2,1)S(1)} %multiply_convert_fusion.3) | copy-start | bytes 12292
  422.8 89.4 %copy-start.42 = (f32[128,2048]{1,0:T(8,128)S(1)}, f32[128,2048]{1,0:T(8,128)}, u32[]{:S(2)}) copy-start(f32[128,2048]{1,0:T(8,128)} %get-tuple-element.104) | copy-start | bytes 3145732
  422.8 89.4 %copy-start.72 = (f32[128]{0:T(128)S(1)}, f32[128]{0:T(128)}, u32[]{:S(2)}) copy-start(f32[128]{0:T(128)} %copy-done.71) | copy-start | bytes 1540
  514.9 21.6 %copy-start.44 = (bf16[256,2048]{1,0:T(8,128)(2,1)S(1)}, bf16[256,2048]{1,0:T(8,128)(2,1)}, u32[]{:S(2)}) copy-start(bf16[256,2048]{1,0:T(8,128)(2,1)} %get-tuple-element.96) | copy-start | bytes 3145732
  536.5 3.6 copy-start.41
  536.5 3.6 copy-start.50
  541.9 2.3 copy-start.13
  541.9 2.3 copy-start.46
  542.3 9.7 %copy-start.18 = (f32[2,128,512]{2,1,0:T(8,128)}, f32[2,128,512]{2,1,0:T(8,128)S(1)}, u32[]{:S(2)}) copy-start(f32[2,128,512]{2,1,0:T(8,128)S(1)} %fusion.50) | copy-start | bytes 1572868
  542.3 3.3 copy-start.27
  542.3 3.3 copy-start.34
  545.6 2.2 copy-start.4
  545.6 2.3 copy-start.8
  545.6 2.5 copy-start.37
  545.6 2.4 copy-start.55
  552.0 2.4 copy-start.20
  556.8 2.9 copy-start.19
  556.8 2.9 copy-start.52
  556.8 2.9 copy-start.54
  556.8 2.9 copy-start.63
  556.8 3.0 copy-start.65
  571.2 3.8 copy-start.6
  571.2 3.8 copy-start.32
  571.2 3.8 copy-start.60
  571.2 3.8 copy-start.61
  575.0 1.9 copy-start.75
  576.9 3.7 copy-start.26
  585.5 22.3 %copy-start.10 = (bf16[128,2048]{1,0:T(8,128)(2,1)S(1)}, bf16[128,2048]{1,0:T(8,128)(2,1)}, u32[]{:S(2)}) copy-start(bf16[128,2048]{1,0:T(8,128)(2,1)} %param.27) | copy-start | bytes 1572868
  585.5 22.3 %copy-start.48 = (f32[2048]{0:T(1024)S(1)}, f32[2048]{0:T(1024)}, u32[]{:S(2)}) copy-start(f32[2048]{0:T(1024)} %param.29) | copy-start | bytes 24580
  585.5 22.3 %copy-start.70 = (f32[128]{0:T(128)S(1)}, f32[128]{0:T(128)}, u32[]{:S(2)}) copy-start(f32[128]{0:T(128)} %copy-done.69) | copy-start | bytes 1540
  585.5 22.6 %copy-start.31 = (f32[2048,16]{1,0:T(8,128)S(1)}, f32[2048,16]{1,0:T(8,128)}, u32[]{:S(2)}) copy-start(f32[2048,16]{1,0:T(8,128)} %fusion.77) | copy-start | bytes 393220
  609.0 1.9 copy-start.2
  746.7 6.7 copy-start.11
  746.7 6.7 copy-start.73
  751.2 2.2 copy-start.25
  751.2 3.7 copy-start.30
  754.9 3.7 copy-start.29
  758.6 3.7 copy-start.28
  758.6 5.7 copy-start.1
  (13 other events, 13.2 us)
Sparse Core Ops, SparseCore 0:
  10.9 144.2 all-gather.1

commit v3 on v2

--- a/solution.py
+++ b/solution.py
@@ -105,14 +105,13 @@
         compiler_params=pltpu.CompilerParams(collective_id=collective_id, has_side_effects=True),
     )(*arrays)
 
-def reduce_steps(planes, parts, outs, buffers, semaphores, filler):
+def reducer(planes, parts, outs, buffers, semaphores):
     held, fromp, relay, near, far = buffers
     load_sem, pair_send, pair_recv, send_sem, relay_recv, near_recv, far_recv = semaphores
     z, r, c = place()
     first, second, diag = c ^ (1 + r), c ^ (2 - r), c ^ 3
     partner = (z, 1 - r, c)
     to_first, to_second = (z, r, first), (z, r, second)
-    greet([to_first, to_second, partner] + [(z ^ k, r, c) for k in range(1, planes)])
     depth = outs[0].shape[0]
     every = range(len(parts))
 
@@ -140,7 +139,6 @@
                 pair(a, k, j).start()
         return 0
 
-    lax.fori_loop(0, planes, begin, 0)
     step_rows = min(32, depth)
 
     def add(target, sources):
@@ -203,24 +201,6 @@
                     to_far(a, i).wait_recv()
                 add(outs[a], terms + [far[a].at[i] for i in range(planes - 1)])
 
-    def step_body(step, _):
-        @pl.when(step < planes)
-        def _():
-            to_relay(planes - 1 - step)
-
-        @pl.when(jnp.logical_and(step >= 1, step < planes + 1))
-        def _():
-            pass_on(planes - step)
-
-        @pl.when(step >= 2)
-        def _():
-            collect(planes + 1 - step)
-        if filler is not None:
-            filler(step)
-        return 0
-
-    lax.fori_loop(0, planes + 2, step_body, 0)
-
     def drain(k, _):
         for a in every:
             for j in range(4):
@@ -234,6 +214,32 @@
                 to_far(a, k).wait_send()
         return 0
 
+    return begin, to_relay, pass_on, collect, drain
+
+
+def reduce_steps(planes, parts, outs, buffers, semaphores, filler):
+    z, r, c = place()
+    greet([(z, r, c ^ 1), (z, r, c ^ 2), (z, 1 - r, c)] + [(z ^ k, r, c) for k in range(1, planes)])
+    begin, to_relay, pass_on, collect, drain = reducer(planes, parts, outs, buffers, semaphores)
+    lax.fori_loop(0, planes, begin, 0)
+
+    def step_body(step, _):
+        @pl.when(step < planes)
+        def _():
+            to_relay(planes - 1 - step)
+
+        @pl.when(jnp.logical_and(step >= 1, step < planes + 1))
+        def _():
+            pass_on(planes - step)
+
+        @pl.when(step >= 2)
+        def _():
+            collect(planes + 1 - step)
+        if filler is not None:
+            filler(step)
+        return 0
+
+    lax.fori_loop(0, planes + 2, step_body, 0)
     lax.fori_loop(0, planes, drain, 0)
 
 
@@ -347,9 +353,12 @@
     )(value)
 
 
-def finish_kernel(planes, proj_ref, outp_ref, small_ref, proj_out, outp_out, small_out, proj_own, outp_own, proj_in, outp_in,
-                  slices, far_slices, own_sem, swap_send, swap_recv, down_send, down_recv, up_send, up_recv,
-                  slice_send, slice_recv, far_send, far_recv, whole_send, whole_recv):
+def finish_kernel(planes, proj_ref, outp_ref, small_ref, scaled_ref, mixed_part, entry_part,
+                  proj_out, outp_out, small_out, mixed_out, entry_out, *scratch):
+    (proj_own, outp_own, proj_in, outp_in, small_own, slices, far_slices, own_sem, swap_send, swap_recv, down_send, down_recv,
+     up_send, up_recv, slice_send, slice_recv, far_send, far_recv, whole_send, whole_recv) = scratch[:20]
+    wide = reducer(planes, (mixed_part,), (mixed_out,), [(ref,) for ref in scratch[20:25]], scratch[25:32])
+    near = reducer(1, (entry_part,), (entry_out,), [(ref,) for ref in scratch[32:37]], scratch[37:44])
     z, r, c = place()
     here = r * 4 + c
     group = [(z, r ^ (j >> 2), c ^ (j & 3)) for j in range(1, 8)]
@@ -379,14 +388,23 @@
         return outp.at[pl.ds((i - 12) * out_rows, out_rows), :]
 
     small_copies = []
-    for j in range(1, 8):
-        copy = remote(small_ref.at[here ^ j], slices.at[here], slice_send.at[j], slice_recv.at[here], group[j - 1])
-        copy.start()
-        small_copies.append(copy)
+
+    def small_begin():
+        lanes = small_ref.shape[2]
+        small_own[...] = small_ref[...]
+        for j in range(entry_out.shape[1] // lanes):
+            at = pl.ds(j * lanes, lanes)
+            part = jnp.sum(entry_out[:, at] * scaled_ref[:, at], axis=0, keepdims=True)
+            small_own[j // small_ref.shape[1], pl.ds(j % small_ref.shape[1], 1), :] = part
+        for j in range(1, 8):
+            copy = remote(small_own.at[here ^ j], slices.at[here], slice_send.at[j], slice_recv.at[here], group[j - 1])
+            copy.start()
+            small_copies.append(copy)
 
     order = [0, 1, 2, 3, 12, 13, 4, 5, 6, 7, 14, 15, 8, 9, 10, 11]
     swaps = []
-    for i in order:
+
+    def issue(i):
         if i < 12:
             keep = pltpu.make_async_copy(piece(i, c), spot(i, c), own_sem.at[i])
             keep.start()
@@ -401,6 +419,12 @@
                 for j in range(1, 4):
                     remote(piece(i, c ^ j), rows(proj_own, outp_own, i), swap_send.at[i, j - 1], swap_recv.at[i, 0], (z, r, c ^ j)).start()
 
+    ahead = 4
+    for i in order[:ahead]:
+        issue(i)
+    near[0](0, 0)
+    lax.fori_loop(0, planes, wide[0], 0)
+
     def local_ready(i):
         target = rows(proj_own, outp_own, i)
         if i < 12:
@@ -460,7 +484,7 @@
         for j in range(1, 8):
             arrived = slices.at[here ^ j]
             remote(arrived, arrived, slice_send.at[0], slice_recv.at[here ^ j], group[j - 1]).wait_recv()
-        slices[here] = small_ref[here]
+        slices[here] = small_own[here]
         total = slices[0]
         for j in range(1, 8):
             total = total + slices[j]
@@ -485,7 +509,21 @@
 
     lag = 2
     hops = 2 * planes - 1
+    top = planes - 1
+    actions = {0: [lambda: near[1](0)], 3: [lambda: near[2](0)], 6: [lambda: near[3](0), small_begin], 10: [small_group], 16: [small_far]}
+    for turn in range(planes + 2):
+        todo = []
+        if turn < planes:
+            todo.append(lambda k=top - turn: wide[1](k))
+        if 0 <= turn - 1 < planes:
+            todo.append(lambda k=top - turn + 1: wide[2](k))
+        if 0 <= turn - 2 < planes:
+            todo.append(lambda k=top - turn + 2: wide[3](k))
+        for n, action in enumerate(todo):
+            actions.setdefault(2 + 4 * turn + n, []).append(action)
     for s in range(chunks + (hops - 1) * lag):
+        if s + ahead < chunks:
+            issue(order[s + ahead])
         for h in range(hops):
             if 0 <= s - h * lag < chunks:
                 i = order[s - h * lag]
@@ -497,13 +535,13 @@
                         to_root(i, p)
                     else:
                         from_root(i, p)
-        if s == 2:
-            small_group()
-        if s == 12:
-            small_far()
+        for action in actions.get(s, ()):
+            action()
     for j in range(1, 8):
         arrived = small_out.at[here ^ j]
         remote(arrived, arrived, whole_send.at[0], whole_recv.at[here ^ j], group[j - 1]).wait_recv()
+    near[4](0, 0)
+    lax.fori_loop(0, planes, wide[4], 0)
     for copy in small_copies + swaps:
         copy.wait_send()
     for i in range(12, 16):
@@ -524,24 +562,28 @@
             remote(result, result, up_send.at[i], up_recv.at[i], up).wait_send()
 
 
-def finish(grad_proj_own, grad_out_own, small, planes, collective_id):
+def finish(grad_proj_own, grad_out_own, small, scaled, mixed_part, entry_part, planes, collective_id):
     depth, width = grad_proj_own.shape[0] // 4, grad_proj_own.shape[1] // 3
     out_rows, out_width = grad_out_own.shape[0], grad_out_own.shape[1] // 4
     kind = grad_proj_own.dtype
     proj, outp = (3, depth, 4 * width), (4 * out_rows, out_width)
     vmem = pl.BlockSpec(memory_space=pltpu.VMEM)
     dma = pltpu.SemaphoreType.DMA
+    [(mixed_shape, _)], mixed_buffers, mixed_semaphores = reduce_scratch([mixed_part], planes)
+    [(entry_shape, _)], entry_buffers, entry_semaphores = reduce_scratch([entry_part], 1)
     return pl.pallas_call(
         functools.partial(finish_kernel, planes),
-        out_shape=[jax.ShapeDtypeStruct(proj, kind), jax.ShapeDtypeStruct(outp, kind), jax.ShapeDtypeStruct(small.shape, small.dtype)],
-        in_specs=[ANYSPEC, ANYSPEC, vmem], out_specs=[vmem, vmem, vmem],
+        out_shape=[jax.ShapeDtypeStruct(proj, kind), jax.ShapeDtypeStruct(outp, kind), jax.ShapeDtypeStruct(small.shape, small.dtype),
+                   jax.ShapeDtypeStruct(mixed_shape, jnp.float32), jax.ShapeDtypeStruct(entry_shape, jnp.float32)],
+        in_specs=[ANYSPEC, ANYSPEC, vmem, vmem, ANYSPEC, ANYSPEC], out_specs=[vmem] * 5,
         scratch_shapes=[
             pltpu.VMEM(proj, kind), pltpu.VMEM(outp, kind), pltpu.VMEM(proj, kind), pltpu.VMEM(outp, kind),
-            pltpu.VMEM(small.shape, jnp.float32), pltpu.VMEM((planes,) + small.shape[1:], jnp.float32),
+            pltpu.VMEM(small.shape, jnp.float32), pltpu.VMEM(small.shape, jnp.float32), pltpu.VMEM((planes,) + small.shape[1:], jnp.float32),
             dma((16,)), dma((16, 3)), dma((16, 3)), dma((16,)), dma((16,)), dma((16,)), dma((16,)),
-            dma((8,)), dma((8,)), dma((planes,)), dma((planes,)), dma((8,)), dma((8,))],
-        compiler_params=pltpu.CompilerParams(collective_id=collective_id, has_side_effects=True, vmem_limit_bytes=40 * 2**20),
-    )(grad_proj_own, grad_out_own, small)
+            dma((8,)), dma((8,)), dma((planes,)), dma((planes,)), dma((8,)), dma((8,))]
+        + mixed_buffers + mixed_semaphores + entry_buffers + entry_semaphores,
+        compiler_params=pltpu.CompilerParams(collective_id=collective_id, has_side_effects=True, vmem_limit_bytes=58 * 2**20),
+    )(grad_proj_own, grad_out_own, small, scaled, mixed_part, entry_part)
 
 
 def expert_kernel(planes, experts, own_h, own_side, cot, w_gate, w_up, w_down,
@@ -654,7 +696,7 @@
             for store in stores(k, rr, slot):
                 store.wait()
 
-        part = 64
+        part = 128
         lane = lax.broadcasted_iota(jnp.int32, (part, rows_side.shape[1]), 1)
 
         @pl.loop(0, group // part)
@@ -673,6 +715,7 @@
             grad_gate[slot, at, :] = (grad_active * up * squash * (1.0 + gate * (1.0 - squash))).astype(jnp.bfloat16)
             grad_up[slot, at, :] = (grad_active * silu).astype(jnp.bfloat16)
 
+    def finish_rows(k, rr, slot):
         entry = dot_turned(grad_gate[slot], gate_use[...]) + dot_turned(grad_up[slot], up_use[...])
         entry_stage[slot] = entry.astype(jnp.bfloat16)
         for store in stores(k, rr, slot):
@@ -682,18 +725,6 @@
         @pl.when(jnp.logical_and(step > 0, step < planes))
         def _():
             forward(number(z ^ step, r, c), step, ((0, to_first), (1, to_second), (2, partner)))
-
-        @pl.when(jnp.logical_and(step >= 1, step < planes + 1))
-        def _():
-            k = step - 1
-            forward(number(z ^ k, r, first), k, ((3, to_second), (4, partner)))
-            forward(number(z ^ k, r, second), k, ((5, partner),))
-
-        @pl.when(jnp.logical_and(step >= 2, step < planes + 2))
-        def _():
-            k = step - 2
-            forward(number(z ^ k, r, diag), k, ((6, partner),))
-            compute(k, r, 0)
 
         @pl.when(jnp.logical_and(step >= 3, step < planes + 3))
         def _():
@@ -702,6 +733,24 @@
                 for i in range(3):
                     await_block(i, number(z ^ k, 1 - r, c ^ j))
             compute(k, 1 - r, 1)
+
+        @pl.when(jnp.logical_and(step >= 1, step < planes + 1))
+        def _():
+            k = step - 1
+            forward(number(z ^ k, r, first), k, ((3, to_second), (4, partner)))
+            forward(number(z ^ k, r, second), k, ((5, partner),))
+
+        @pl.when(jnp.logical_and(step >= 3, step < planes + 3))
+        def _():
+            finish_rows(step - 3, 1 - r, 1)
+            finish_rows(step - 3, r, 0)
+
+        @pl.when(jnp.logical_and(step >= 2, step < planes + 2))
+        def _():
+            k = step - 2
+            forward(number(z ^ k, r, diag), k, ((6, partner),))
+            compute(k, r, 0)
+
         return 0
 
     lax.fori_loop(0, planes + 3, step_body, 0)
@@ -831,6 +880,190 @@
     )(entry_part, route_part, all_h, cot, active, grad_gate, grad_up, w_down)
 
 
+def dot_plain(left, right):
+    return jnp.dot(left, right, preferred_element_type=jnp.float32)
+
+
+def dot_cols(left, right):
+    return lax.dot_general(left, right, (((1,), (1,)), ((), ())), preferred_element_type=jnp.float32)
+
+
+def dot_rows(left, right):
+    return lax.dot_general(left, right, (((0,), (0,)), ((), ())), preferred_element_type=jnp.float32)
+
+
+def group_peers():
+    z, r, c = place()
+    return r * 4 + c, [(z, r ^ (j >> 2), c ^ (j & 3)) for j in range(1, 8)]
+
+
+def group_sums(own, slots, send_sem, recv_sem):
+    here, peers = group_peers()
+    copies = []
+    for j, peer in enumerate(peers):
+        copy = pltpu.make_async_remote_copy(
+            src_ref=own, dst_ref=slots.at[j], send_sem=send_sem.at[j], recv_sem=recv_sem.at[j],
+            device_id=peer, device_id_type=MESH)
+        copy.start()
+        copies.append(copy)
+    for copy in copies:
+        copy.wait()
+    total = jnp.zeros(own.shape, jnp.float32)
+    for who in range(8):
+        which = here ^ who
+        total = total + jnp.where(which == 0, own[...], slots[jnp.maximum(which - 1, 0)])
+    return total
+
+
+def row_of_tokens(values):
+    folded = values[:, :128]
+    for start in range(128, values.shape[1], 128):
+        folded = folded + values[:, start:start + 128]
+    return jnp.sum(folded.T, axis=0, keepdims=True)
+
+
+def column_of(row):
+    return jnp.broadcast_to(row, (128, row.shape[1])).T
+
+
+BLOCK = 256
+
+
+def block_weights(queries, keys, first, finish):
+    scores = dot_cols(queries[first:finish], keys[:finish])
+    at_query = lax.broadcasted_iota(jnp.int32, scores.shape, 0) + first
+    at_key = lax.broadcasted_iota(jnp.int32, scores.shape, 1)
+    scores = jnp.where(at_query >= at_key, scores, MASKED)
+    weights = jnp.exp(scores - jnp.max(scores, axis=1, keepdims=True))
+    return weights / jnp.sum(weights, axis=1, keepdims=True)
+
+
+def forward_kernel(width, x_ref, proj_ref, gains, cosine, sine, w_out_ref,
+                   part_out, query_out, key_out, value_out, raw_out, scale_out, mixed_out,
+                   sums, slots, send_sem, recv_sem):
+    greet(group_peers()[1])
+    local = value_out.shape[1]
+    raw = dot_plain(x_ref[...], proj_ref[...])
+    raw_out[...] = raw[:, :2 * local]
+    value_out[...] = raw[:, 2 * local:].astype(jnp.bfloat16)
+    sums[...] = jnp.zeros(sums.shape, jnp.float32)
+    for i in range(2):
+        half = raw_out[:, pl.ds(i * local, local)]
+        sums[pl.ds(i, 1), :] = row_of_tokens(half * half)
+    total = group_sums(sums, slots, send_sem, recv_sem)
+    for i, (target, factor) in enumerate(((query_out, 128 ** (-0.5)), (key_out, 1.0))):
+        scale = lax.rsqrt(column_of(total[i:i + 1]) / width + EPSILON)
+        scale_out[:, pl.ds(i * 128, 128)] = scale
+        for start in range(0, local, 128):
+            lanes = pl.ds(start, 128)
+            normal = raw_out[:, pl.ds(i * local + start, 128)] * scale * gains[pl.ds(i, 1), lanes]
+            turned = normal * cosine[...] + pltpu.roll(normal, 64, 1) * sine[...]
+            target[:, lanes] = (turned * factor).astype(jnp.bfloat16)
+    tokens = x_ref.shape[0]
+    for start in range(0, local, 128):
+        lanes = pl.ds(start, 128)
+        queries, keys, values = query_out[:, lanes], key_out[:, lanes], value_out[:, lanes]
+        for first in range(0, tokens, BLOCK):
+            weights = block_weights(queries, keys, first, first + BLOCK).astype(jnp.bfloat16)
+            mixed = dot_plain(weights, values[:first + BLOCK])
+            mixed_out[pl.ds(first, BLOCK), lanes] = mixed.astype(jnp.bfloat16)
+    part_out[...] = dot_plain(mixed_out[...], w_out_ref[...]).astype(jnp.bfloat16)
+
+
+def attention_forward(gathered_x, w_proj, gains, cosine, sine, w_out_own, collective_id):
+    tokens, width = gathered_x.shape
+    local = w_proj.shape[1] // 3
+    low, wide = jnp.bfloat16, jnp.float32
+    shape, vmem = jax.ShapeDtypeStruct, pl.BlockSpec(memory_space=pltpu.VMEM)
+    dma = pltpu.SemaphoreType.DMA
+    return pl.pallas_call(
+        functools.partial(forward_kernel, width),
+        out_shape=[shape((tokens, width), low), shape((tokens, local), low), shape((tokens, local), low), shape((tokens, local), low),
+                   shape((tokens, 2 * local), wide), shape((tokens, 256), wide), shape((tokens, local), low)],
+        in_specs=[vmem] * 6, out_specs=[vmem] * 7,
+        scratch_shapes=[pltpu.VMEM((8, tokens), wide), pltpu.VMEM((7, 8, tokens), wide), dma((7,)), dma((7,))],
+        compiler_params=pltpu.CompilerParams(collective_id=collective_id, has_side_effects=True, vmem_limit_bytes=56 * 2**20),
+    )(gathered_x, w_proj, gains, cosine, sine, w_out_own)
+
+
+def backward_kernel(width, grad_ref, w_out_ref, x_hbm, proj_hbm, query_ref, key_ref, value_ref, raw_ref, scale_ref, mixed_ref,
+                    gains, cosine, sine, grad_x_out, grad_proj_out, grad_out_out, gain_out,
+                    x_ref, proj_ref, grad_query, grad_key, grad_value, grad_raw, sums, slots, load_sem, send_sem, recv_sem):
+    greet(group_peers()[1])
+    loads = [pltpu.make_async_copy(x_hbm, x_ref, load_sem.at[0]), pltpu.make_async_copy(proj_hbm, proj_ref, load_sem.at[1])]
+    for load in loads:
+        load.start()
+    local, tokens = value_ref.shape[1], value_ref.shape[0]
+    grad_mixed = dot_cols(grad_ref[...], w_out_ref[...]).astype(jnp.bfloat16)
+    grad_raw[:, pl.ds(0, local)] = grad_mixed
+    for start in range(0, local, 128):
+        lanes = pl.ds(start, 128)
+        queries, keys, values, upstream = query_ref[:, lanes], key_ref[:, lanes], value_ref[:, lanes], grad_raw[:, lanes]
+        for first in reversed(range(0, tokens, BLOCK)):
+            finish = first + BLOCK
+            weights = block_weights(queries, keys, first, finish)
+            grad_weights = dot_cols(upstream[first:finish], values[:finish])
+            centre = jnp.sum(weights * grad_weights, axis=1, keepdims=True)
+            grad_scores = (weights * (grad_weights - centre)).astype(jnp.bfloat16)
+            grad_query[pl.ds(first, BLOCK), lanes] = dot_plain(grad_scores, keys[:finish])
+            key_part = dot_rows(grad_scores, queries[first:finish])
+            value_part = dot_rows(weights.astype(jnp.bfloat16), upstream[first:finish])
+            if finish == tokens:
+                grad_key[:, lanes] = key_part
+                grad_value[:, lanes] = value_part
+            else:
+                grad_key[pl.ds(0, finish), lanes] += key_part
+                grad_value[pl.ds(0, finish), lanes] += value_part
+    sums[...] = jnp.zeros(sums.shape, jnp.float32)
+    gain_out[...] = jnp.zeros(gain_out.shape, jnp.float32)
+    for i, (grad, factor) in enumerate(((grad_query, 128 ** (-0.5)), (grad_key, 1.0))):
+        scale = scale_ref[:, pl.ds(i * 128, 128)]
+        inner = None
+        for start in range(0, local, 128):
+            lanes = pl.ds(start, 128)
+            upstream = grad[:, lanes] * factor
+            normal = upstream * cosine[...] - pltpu.roll(upstream, 64, 1) * sine[...]
+            raw = raw_ref[:, pl.ds(i * local + start, 128)]
+            gain_out[pl.ds(i, 1), lanes] = jnp.sum(normal * raw * scale, axis=0, keepdims=True)
+            weighted = gains[pl.ds(i, 1), lanes] * normal
+            grad[:, lanes] = weighted
+            inner = weighted * raw if inner is None else inner + weighted * raw
+        sums[pl.ds(i, 1), :] = row_of_tokens(inner)
+    total = group_sums(sums, slots, send_sem, recv_sem)
+    for i, grad in enumerate((grad_query, grad_key)):
+        scale = scale_ref[:, pl.ds(i * 128, 128)]
+        factor = scale * scale * scale * column_of(total[i:i + 1]) / width
+        for start in range(0, local, 128):
+            lanes = pl.ds(start, 128)
+            raw = raw_ref[:, pl.ds(i * local + start, 128)]
+            grad_raw[:, pl.ds(i * local + start, 128)] = (scale * grad[:, lanes] - raw * factor).astype(jnp.bfloat16)
+    grad_raw[:, pl.ds(2 * local, local)] = grad_value[...].astype(jnp.bfloat16)
+    for load in loads:
+        load.wait()
+    grad_x_out[...] = dot_cols(grad_raw[...], proj_ref[...]).astype(jnp.bfloat16)
+    grad_proj_out[...] = dot_rows(x_ref[...], grad_raw[...]).astype(jnp.bfloat16)
+    grad_out_out[...] = dot_rows(mixed_ref[...], grad_ref[...]).astype(jnp.bfloat16)
+
+
+def attention_backward(grad_gathered, w_out_own, gathered_x, w_proj, kept, gains, cosine, sine, collective_id):
+    tokens, width = gathered_x.shape
+    local = w_proj.shape[1] // 3
+    low, wide = jnp.bfloat16, jnp.float32
+    shape, vmem = jax.ShapeDtypeStruct, pl.BlockSpec(memory_space=pltpu.VMEM)
+    dma = pltpu.SemaphoreType.DMA
+    return pl.pallas_call(
+        functools.partial(backward_kernel, width),
+        out_shape=[shape((tokens, width), low), shape(w_proj.shape, low), shape(w_out_own.shape, low), shape((8, local), wide)],
+        in_specs=[vmem, vmem, ANYSPEC, ANYSPEC] + [vmem] * 9, out_specs=[vmem] * 4,
+        scratch_shapes=[
+            pltpu.VMEM(gathered_x.shape, low), pltpu.VMEM(w_proj.shape, low),
+            pltpu.VMEM((tokens, local), wide), pltpu.VMEM((tokens, local), wide), pltpu.VMEM((tokens, local), wide),
+            pltpu.VMEM((tokens, 3 * local), low), pltpu.VMEM((8, tokens), wide), pltpu.VMEM((7, 8, tokens), wide),
+            dma((2,)), dma((7,)), dma((7,))],
+        compiler_params=pltpu.CompilerParams(collective_id=collective_id, has_side_effects=True, vmem_limit_bytes=60 * 2**20),
+    )(grad_gathered, w_out_own, gathered_x, w_proj, *kept, gains, cosine, sine)
+
+
 HEAD_DIM = 128
 SEQ_LEN = 1024
 EPSILON = 1e-05
@@ -1014,8 +1247,7 @@
         entry_rows, grad_probs_all, out_part, *grads = entry_sums(
             entry_part, grad_side, rows_h, all_cotangent, active_share, grad_gate_rows, grad_up_rows, down_use, 7
         )
-        (mixture,) = scatter_sums([out_part], True, 8)
-        return (entry_rows, grad_probs_all, mixture, *grads)
+        return (entry_rows, grad_probs_all, out_part, *grads)
     rows_h, rows_side = gather_tokens([normal_h, side], True, 6, 2)
     expert = lax.axis_index("dp") * lax.axis_size("col") + lax.axis_index("col")
     lane = jnp.arange(side.shape[1])
@@ -1076,17 +1308,8 @@
     w_proj, w_out_own = to_heads(w_query, w_key, w_value, w_out)
     (gathered_x,) = gather_tokens([normal_x], False, 2, 2)
     group_tokens = gathered_x.shape[0]
-    raw = contract(gathered_x, w_proj)
     local_width = w_proj.shape[1] // 3
-    query_raw = raw[:, :local_width]
-    key_raw = raw[:, local_width : 2 * local_width]
-    value_heads = raw[:, 2 * local_width :].astype(jnp.bfloat16)
     head_count = local_width // HEAD_DIM
-    query_square, key_square = sum_over_heads(
-        jnp.sum(query_raw * query_raw, axis=-1), jnp.sum(key_raw * key_raw, axis=-1), 4
-    )
-    inv_query = lax.rsqrt(query_square / model_width + EPSILON)[:, None]
-    inv_key = lax.rsqrt(key_square / model_width + EPSILON)[:, None]
     offset = (lax.axis_index("row") * lax.axis_size("col") + lax.axis_index("col")) * local_width
     gain_query = lax.dynamic_slice_in_dim(query_gain, offset, local_width)
     gain_key = lax.dynamic_slice_in_dim(key_gain, offset, local_width)
@@ -1094,19 +1317,35 @@
     head_shape = (group_tokens, head_count, HEAD_DIM)
     sequences = group_tokens // SEQ_LEN
     seq_shape = (sequences, SEQ_LEN, head_count, HEAD_DIM)
-    query_heads = (
-        rotate((query_raw * inv_query * gain_query).reshape(head_shape), cosine, sine_table)
-        * HEAD_DIM ** (-0.5)
-    ).astype(jnp.bfloat16)
-    key_heads = rotate(
-        (key_raw * inv_key * gain_key).reshape(head_shape), cosine, sine_table
-    ).astype(jnp.bfloat16)
-    query_seq = query_heads.reshape(seq_shape)
-    key_seq = key_heads.reshape(seq_shape)
-    value_seq = value_heads.reshape(seq_shape)
-    mixed, sums_log = by_sequence(attend_forward, (query_seq, key_seq, value_seq), sequences)
-    mixed_heads = mixed.reshape(group_tokens, local_width).astype(jnp.bfloat16)
-    attn_part = contract(mixed_heads, w_out_own).astype(jnp.bfloat16)
+    in_kernels = on_links() and sequences == 1
+    if in_kernels:
+        gains = jnp.concatenate([gain_query[None], gain_key[None], jnp.zeros((6, local_width), jnp.float32)])
+        sine_signed = jnp.where(jnp.arange(HEAD_DIM) < HEAD_DIM // 2, -sine_table[:, 0], sine_table[:, 0])
+        tables = (gains, cosine[:, 0], sine_signed)
+        attn_part, *kept = attention_forward(gathered_x, w_proj, *tables, w_out_own, 4)
+    else:
+        raw = contract(gathered_x, w_proj)
+        query_raw = raw[:, :local_width]
+        key_raw = raw[:, local_width : 2 * local_width]
+        value_heads = raw[:, 2 * local_width :].astype(jnp.bfloat16)
+        query_square, key_square = sum_over_heads(
+            jnp.sum(query_raw * query_raw, axis=-1), jnp.sum(key_raw * key_raw, axis=-1), 4
+        )
+        inv_query = lax.rsqrt(query_square / model_width + EPSILON)[:, None]
+        inv_key = lax.rsqrt(key_square / model_width + EPSILON)[:, None]
+        query_heads = (
+            rotate((query_raw * inv_query * gain_query).reshape(head_shape), cosine, sine_table)
+            * HEAD_DIM ** (-0.5)
+        ).astype(jnp.bfloat16)
+        key_heads = rotate(
+            (key_raw * inv_key * gain_key).reshape(head_shape), cosine, sine_table
+        ).astype(jnp.bfloat16)
+        query_seq = query_heads.reshape(seq_shape)
+        key_seq = key_heads.reshape(seq_shape)
+        value_seq = value_heads.reshape(seq_shape)
+        mixed, sums_log = by_sequence(attend_forward, (query_seq, key_seq, value_seq), sequences)
+        mixed_heads = mixed.reshape(group_tokens, local_width).astype(jnp.bfloat16)
+        attn_part = contract(mixed_heads, w_out_own).astype(jnp.bfloat16)
     (attn_rows,) = scatter_sums([attn_part], False, 5)
     state_rows = inputs + attn_rows
 
@@ -1147,8 +1386,6 @@
         expert_grads, rows = lax.scan(piece_step, empty, cut)
         entry_rows, grad_probs_all, mixture = [r.reshape((token_count,) + r.shape[2:]) for r in rows]
     grad_gate_w, grad_up_w, grad_down_w = expert_grads
-    block_out = (state_rows + mixture).astype(jnp.bfloat16)
-
     grad_probs = selected * grad_probs_all[:, :expert_count]
     grad_logits = (
         probabilities * (grad_probs - jnp.sum(probabilities * grad_probs, axis=-1, keepdims=True))
@@ -1159,38 +1396,41 @@
     grad_state = upstream + grad_state_part
     grad_attn = grad_state.astype(jnp.bfloat16)
     (grad_gathered,) = gather_tokens([grad_attn], False, 9, 2)
-    grad_out_own = contract_rows(mixed_heads, grad_gathered).astype(jnp.bfloat16)
-    grad_mixed = contract_cols(grad_gathered, w_out_own).astype(jnp.bfloat16)
-    grad_query_seq, grad_key_seq, grad_value_seq = by_sequence(
-        attend_backward,
-        (query_seq, key_seq, value_seq, grad_mixed.reshape(seq_shape), sums_log),
-        sequences,
-    )
-    grad_normal_q = unrotate(
-        grad_query_seq.reshape(head_shape) * HEAD_DIM ** (-0.5), cosine, sine_table
-    ).reshape(group_tokens, local_width)
-    grad_normal_k = unrotate(grad_key_seq.reshape(head_shape), cosine, sine_table).reshape(
-        group_tokens, local_width
-    )
-    weighted_q = gain_query * grad_normal_q
-    weighted_k = gain_key * grad_normal_k
-    inner_q, inner_k = sum_over_heads(
-        jnp.sum(weighted_q * query_raw, axis=-1), jnp.sum(weighted_k * key_raw, axis=-1), 10
-    )
-    grad_query_raw = (
-        inv_query * weighted_q - query_raw * inv_query**3 * inner_q[:, None] / model_width
-    )
-    grad_key_raw = inv_key * weighted_k - key_raw * inv_key**3 * inner_k[:, None] / model_width
-    grad_qgain_part = jnp.sum(grad_normal_q * query_raw * inv_query, axis=0)
-    grad_kgain_part = jnp.sum(grad_normal_k * key_raw * inv_key, axis=0)
-    grad_raw = jnp.concatenate(
-        [grad_query_raw, grad_key_raw, grad_value_seq.reshape(group_tokens, local_width)], axis=1
-    ).astype(jnp.bfloat16)
-    grad_x_part = contract_cols(grad_raw, w_proj).astype(jnp.bfloat16)
-    (grad_normal_x,) = scatter_sums([grad_x_part], False, 11)
-    grad_proj_own = contract_rows(gathered_x, grad_raw).astype(jnp.bfloat16)
-    grad_input_part, grad_attn_gain = norm_backward(inputs, inv_input, norm_attn, grad_normal_x)
-    grad_input = grad_state + grad_input_part
+    if in_kernels:
+        grad_x_part, grad_proj_own, grad_out_own, gain_parts = attention_backward(
+            grad_gathered, w_out_own, gathered_x, w_proj, kept, *tables, 10
+        )
+        grad_qgain_part, grad_kgain_part = gain_parts[0], gain_parts[1]
+    else:
+        grad_out_own = contract_rows(mixed_heads, grad_gathered).astype(jnp.bfloat16)
+        grad_mixed = contract_cols(grad_gathered, w_out_own).astype(jnp.bfloat16)
+        grad_query_seq, grad_key_seq, grad_value_seq = by_sequence(
+            attend_backward,
+            (query_seq, key_seq, value_seq, grad_mixed.reshape(seq_shape), sums_log),
+            sequences,
+        )
+        grad_normal_q = unrotate(
+            grad_query_seq.reshape(head_shape) * HEAD_DIM ** (-0.5), cosine, sine_table
+        ).reshape(group_tokens, local_width)
+        grad_normal_k = unrotate(grad_key_seq.reshape(head_shape), cosine, sine_table).reshape(
+            group_tokens, local_width
+        )
+        weighted_q = gain_query * grad_normal_q
+        weighted_k = gain_key * grad_normal_k
+        inner_q, inner_k = sum_over_heads(
+            jnp.sum(weighted_q * query_raw, axis=-1), jnp.sum(weighted_k * key_raw, axis=-1), 10
+        )
+        grad_query_raw = (
+            inv_query * weighted_q - query_raw * inv_query**3 * inner_q[:, None] / model_width
+        )
+        grad_key_raw = inv_key * weighted_k - key_raw * inv_key**3 * inner_k[:, None] / model_width
+        grad_qgain_part = jnp.sum(grad_normal_q * query_raw * inv_query, axis=0)
+        grad_kgain_part = jnp.sum(grad_normal_k * key_raw * inv_key, axis=0)
+        grad_raw = jnp.concatenate(
+            [grad_query_raw, grad_key_raw, grad_value_seq.reshape(group_tokens, local_width)], axis=1
+        ).astype(jnp.bfloat16)
+        grad_x_part = contract_cols(grad_raw, w_proj).astype(jnp.bfloat16)
+        grad_proj_own = contract_rows(gathered_x, grad_raw).astype(jnp.bfloat16)
     full_width = query_gain.shape[0]
     padded_qgain = lax.dynamic_update_slice_in_dim(
         jnp.zeros((full_width,), jnp.float32), grad_qgain_part, offset, 0
@@ -1198,9 +1438,13 @@
     padded_kgain = lax.dynamic_update_slice_in_dim(
         jnp.zeros((full_width,), jnp.float32), grad_kgain_part, offset, 0
     )
-    small = (grad_attn_gain, padded_qgain, padded_kgain, grad_moe_part, grad_router_part)
-    grad_query, grad_key, grad_value, grad_out_proj, small = last_sums(grad_proj_own, grad_out_own, small)
+    small = (padded_qgain, padded_kgain, grad_moe_part, grad_router_part)
+    grad_query, grad_key, grad_value, grad_out_proj, mixture, grad_normal_x, small = last_sums(
+        grad_proj_own, grad_out_own, small, inputs * inv_input, mixture, grad_x_part
+    )
     grad_norm_attn, grad_query_gain, grad_key_gain, grad_norm_moe, grad_router = small
+    block_out = (state_rows + mixture).astype(jnp.bfloat16)
+    grad_input = grad_state + norm_backward(inputs, inv_input, norm_attn, grad_normal_x)[0]
     return (
         block_out,
         grad_input,
@@ -1219,22 +1463,28 @@
     )
 
 
-def last_sums(grad_proj_own, grad_out_own, small):
+def last_sums(grad_proj_own, grad_out_own, small, scaled, mixed_part, entry_part):
     if on_links():
-        flat = jnp.concatenate([part.reshape(-1) for part in small])
-        proj, outp, total = finish(grad_proj_own, grad_out_own, flat.reshape(8, -1, 128), lax.axis_size("dp"), 12)
+        parts = (jnp.zeros((scaled.shape[1],), jnp.float32), *small)
+        flat = jnp.concatenate([part.reshape(-1) for part in parts])
+        proj, outp, total, mixture, grad_normal_x = finish(
+            grad_proj_own, grad_out_own, flat.reshape(8, -1, 128), scaled, mixed_part, entry_part, lax.axis_size("dp"), 12
+        )
         total, sums, start = total.reshape(-1), [], 0
-        for part in small:
+        for part in parts:
             sums.append(total[start : start + part.size].reshape(part.shape))
             start += part.size
-        return (*(proj[a].astype(jnp.float32) for a in range(3)), outp.astype(jnp.float32), sums)
+        return (*(proj[a].astype(jnp.float32) for a in range(3)), outp.astype(jnp.float32), mixture, grad_normal_x, sums)
+    (grad_normal_x,) = scatter_sums([entry_part], False, 11)
+    small = (jnp.sum(grad_normal_x * scaled, axis=0), *small)
     width = grad_proj_own.shape[1] // 3
     blocks = [
         lax.all_to_all(grad_proj_own[:, a * width : (a + 1) * width], "col", split_axis=0, concat_axis=1, tiled=True)
         for a in range(3)
     ]
     out_block = lax.all_to_all(grad_out_own, "col", split_axis=1, concat_axis=0, tiled=True)
-    return (*(total.astype(jnp.float32) for total in lax.psum((*blocks, out_block), "dp")), lax.psum(small, EVERYONE))
+    weights = [total.astype(jnp.float32) for total in lax.psum((*blocks, out_block), "dp")]
+    return (*weights, mixed_part, grad_normal_x, lax.psum(small, EVERYONE))
 
 
 def solution(mesh):

time: 782 us -> 708 us (0.905)
  the two profiles are of different devices: /device:TPU:6 before, /device:TPU:1 now
where the time goes in v3:
time: 708 us; the launch traced here: 698 us
  Pallas kernels  637 us (90%)
  other arithmetic  23.6 us (3%)
  local copies, waits for them, and re-layouts  20.7 us (3%)
  between operations  14.6 us (2%)
    pallas_call x1, Pallas kernels, finish(): pl.pallas_call(functools.partial(finish_kernel, planes), out_shape=[jax.S...  210 us
    pallas_call x1, Pallas kernels, expert_rows_on_links(): pl.pallas_call(functools.partial(expert_kernel, planes, experts), out_sha...  115 us
    pallas_call x1, Pallas kernels, entry_sums(): pl.pallas_call(functools.partial(entry_kernel, planes), out_shape=[jax.Sh...  106 us
    pallas_call x1, Pallas kernels, exchange_weights(): pl.pallas_call(exchange_kernel, out_shape=[jax.ShapeDtypeStruct((depth *...  72.4 us
    pallas_call x2, Pallas kernels, gather(): pl.pallas_call(functools.partial(gather_kernel, planes, parts, count), ou...  50.8 us
    pallas_call x1, Pallas kernels, attention_backward(): pl.pallas_call(functools.partial(backward_kernel, width), out_shape=[shap...  31.4 us
    pallas_call x1, Pallas kernels, attention_forward(): pl.pallas_call(functools.partial(forward_kernel, width), out_shape=[shape...  28.7 us
    pallas_call x1, Pallas kernels, reduce_scatter(): pl.pallas_call(functools.partial(reduce_kernel, planes, count), out_shape...  22.9 us
  transfers between devices with their start and end apart: 1, of which 0 were waited for; matrix products, arithmetic and copies ran while one was open for 2% of the time, Pallas kernels for 22%

profile of v3, /device:TPU:1, one launch (start us, length us, event | category | flops | bytes accessed | tf_op | source)
XLA Modules:
  0.0 698.5 jit_solution(8754218125084937601)
XLA Ops:
  7.2 0.0 copy-start
  7.2 0.0 all-gather.2.cloned.1.call-start
  7.2 0.7 all-gather.2.cloned.1.call-update
  7.9 0.8 dynamic_slice.6
  8.7 0.8 dynamic_slice.7
  9.5 1.2 fusion
  10.7 2.4 convert_multiply_fusion.2
  13.1 28.2 %shard_map.254.x_ref.x_hbm = bf16[1024,2048]{1,0:T(8,128)(2,1)} custom-call(bf16[128,2048]{1,0:T(8,128)(2,1)} %get-tuple-element.126.refs_0_), custom_call_target="tpu_custom_call" | custom-call | tf_op jit(solution)/shard_map/pallas_call | solution.py:100
  41.3 0.1 pad.7.clone
  41.3 72.4 %shard_map.255 = (bf16[2048,768]{1,0:T(8,128)(2,1)}, bf16[256,2048]{1,0:T(8,128)(2,1)}) custom-call(bf16[512,1024]{1,0:T(8,128)(2,1)} %wq_ref.1, bf16[512,1024]{1,0:T(8,128)(2,1)} %wk_ref.1, bf16[512,1024]{1,0:T(8,128)(2,1)} %wv_ref.1, bf16[1024,512]{1,0:T(8,128)(2,1)} %wo_ref.1), custom_call_target="tpu_custom_call" | custom-call | tf_op jit(solution)/shard_map/pallas_call | solution.py:315
  113.8 0.7 maximum_maximum_fusion.1.gains
  114.5 0.2 broadcast_multiply_fusion
  114.7 2.9 negate_select_fusion
  117.6 28.7 %shard_map.256 = (bf16[1024,2048]{1,0:T(8,128)(2,1)}, bf16[1024,256]{1,0:T(8,128)(2,1)}, bf16[1024,256]{1,0:T(8,128)(2,1)}, bf16[1024,256]{1,0:T(8,128)(2,1)}, f...) custom-call(bf16[1024,2048]{1,0:T(8,128)(2,1)} %shard_map.254.x_ref.x_hbm, ...), custom_call_target="tpu_custom_call" | custom-call | tf_op jit(solution)/shard_map/pallas_call | solution.py:979
  146.3 0.0 copy-start.2
  146.3 2.2 copy-done.2
  148.5 22.9 %shard_map.257 = f32[128,2048]{1,0:T(8,128)S(1)} custom-call(bf16[1024,2048]{1,0:T(8,128)(2,1)S(1)} %copy-done.2), custom_call_target="tpu_custom_call" | custom-call | tf_op jit(solution)/shard_map/pallas_call | solution.py:264
  171.4 0.0 copy-done.3
  171.4 0.2 multiply_reduce_fusion.2
  171.7 0.0 copy-done.16
  171.7 0.2 multiply_convert_fusion.own_h
  171.9 0.0 copy-start.4
  171.9 0.3 fusion.16
  172.1 0.1 copy.41
  172.3 0.1 copy.43
  172.4 0.1 pad.2.clone
  172.4 0.6 constant_dynamic-update-slice_fusion.4
  173.0 0.2 fusion.8
  173.2 0.1 multiply_convert_fusion.3
  173.4 0.7 maximum_maximum_fusion.own_side
  174.1 115.1 %shard_map.258 = (bf16[4096,2048]{1,0:T(8,128)(2,1)}, bf16[4096,128]{1,0:T(8,128)(2,1)}, bf16[4096,2048]{1,0:T(8,128)(2,1)}, bf16[4096,128]{1,0:T(8,128)(2,1)}, ...) custom-call(bf16[128,2048]{1,0:T(8,128)(2,1)} %copy-done.4, ...), custom_call_target="tpu_custom_call" | custom-call | tf_op jit(solution)/shard_map/pallas_call | solution.py:782
  289.2 0.0 copy-start.5
  289.2 105.6 %shard_map.259 = (f32[128,2048]{1,0:T(8,128)}, f32[128,128]{1,0:T(8,128)}, bf16[4096,2048]{1,0:T(8,128)(2,1)}, f32[2048,512]{1,0:T(8,128)}, f32[2048,512]{1,0:T(8,128)}, /*index=5*/f32[512,2048]{1,0:T(8,128)}) custom-call(bf16[4096,2048]{1,0:T(8,128)(2,1)} %get-tuple-element.47.entry_part, bf16[4096,128]{1,0:T(8,128)(2,1)} %get-tuple-element.48.route_part, ...), custom_call_target="tpu_custom_call" | custom-call | tf_op jit(solution)/shard_map/pallas_call | solution.py:870
  394.8 0.0 copy-start.11
  394.8 1.1 multiply_reduce_fusion.3
  395.9 1.0 multiply_convert_fusion.2
  396.9 0.0 copy-done.5
  396.9 0.3 fusion.17
  397.2 0.3 reshape.99
  397.5 1.7 multiply_reduce_fusion
  399.2 1.6 fusion.13
  400.8 22.6 %shard_map.260.grad_ref = bf16[1024,2048]{1,0:T(8,128)(2,1)} custom-call(bf16[128,2048]{1,0:T(8,128)(2,1)} %get-tuple-element.118.refs_0_), custom_call_target="tpu_custom_call" | custom-call | tf_op jit(solution)/shard_map/pallas_call | solution.py:100
  423.4 0.0 copy-start.14
  423.4 31.4 %shard_map.261 = (bf16[1024,2048]{1,0:T(8,128)(2,1)}, bf16[2048,768]{1,0:T(8,128)(2,1)}, bf16[256,2048]{1,0:T(8,128)(2,1)}, f32[8,256]{1,0:T(8,128)}) custom-call(bf16[1024,2048]{1,0:T(8,128)(2,1)} %shard_map.260.grad_ref, bf16[256,2048]{1,0:T(8,128)(2,1)} %get-tuple-element.45.w_out_ref, bf16[1024,2048]{1,0:T(8,128)(2,1)} %shard_map.254.x_ref.x_hbm, ...), custom_call_target="tpu_custom_call" | custom-call | tf_op jit(solution)/shard_map/pallas_call | solution.py:1054
  454.8 0.8 fusion.15
  455.6 0.2 dynamic_update_slice.6
  455.8 0.3 dynamic_update_slice.7
  456.0 0.0 copy-start.15
  456.1 0.7 copy-done.15
  456.7 209.8 %shard_map.262 = (bf16[3,512,1024]{2,1,0:T(8,128)(2,1)}, bf16[1024,512]{1,0:T(8,128)(2,1)}, f32[8,40,128]{2,1,0:T(8,128)}, f32[128,2048]{1,0:T(8,128)}, f32[128,2048]{1,0:T(8,128)}) custom-call(bf16[2048,768]{1,0:T(8,128)(2,1)} %get-tuple-element.61.proj_ref, bf16[256,2048]{1,0:T(8,128)(2,1)} %get-tuple-element.62.outp_ref, f32[8,40,128]{2,1,0:T(8,128)} %bitcast.35, ...), custom_call_target="tpu_custom_call" | custom-call | tf_op jit(solution)/shard_map/pallas_call | solution.py:574
  666.5 4.8 bitcast_convert_fusion
  671.4 0.4 slice.46
  671.7 1.0 slice.52
  672.8 2.3 copy.46
  675.1 3.0 convert_element_type.81
  678.0 1.6 fusion.5
  679.6 0.6 fusion.14
  680.3 0.0 copy-done.10
  680.3 1.7 fusion.4
  682.0 2.1 copy.57
  684.1 1.6 copy-done.7
  685.7 2.1 copy.58
  687.8 1.6 copy-done.6
  689.4 2.0 copy.59
  (38 shorter events, 0.1 us)
Async XLA Ops:
  7.2 164.7 %copy-start = (bf16[2048,16]{0,1:T(8,128)(2,1)S(1)}, bf16[2048,16]{0,1:T(8,128)(2,1)}, u32[]{:S(2)}) copy-start(bf16[2048,16]{0,1:T(8,128)(2,1)} %param.25) | copy-start | bytes 196612
  7.2 166.9 %all-gather.2.cloned.1.call-start = ((), (), s32[]{:S(2)}) async-start(), calls=%async_computation | async-start | bytes 17301504 | tf_op jit(solution)/shard_map/all_gather | solution.py:1242
  146.3 2.2 copy-start.2
  148.5 22.9 %copy-start.3 = (bf16[128,2048]{1,0:T(8,128)(2,1)S(1)}, bf16[128,2048]{1,0:T(8,128)(2,1)}, u32[]{:S(2)}) copy-start(bf16[128,2048]{1,0:T(8,128)(2,1)} %param.15) | copy-start | bytes 1572868
  148.5 23.2 %copy-start.16 = (f32[2048]{0:T(1024)S(1)}, f32[2048]{0:T(1024)}, u32[]{:S(2)}) copy-start(f32[2048]{0:T(1024)} %param.24) | copy-start | bytes 24580
  148.5 23.7 %copy-start.18 = (s32[128,8]{0,1:T(8,128)S(1)}, s32[128,8]{0,1:T(8,128)}, u32[]{:S(2)}) copy-start(s32[128,8]{0,1:T(8,128)} %param.29) | copy-start | bytes 12292
  171.9 2.2 copy-start.4
  289.2 107.7 %copy-start.5 = (bf16[128,2048]{1,0:T(8,128)(2,1)S(1)}, bf16[128,2048]{1,0:T(8,128)(2,1)}, u32[]{:S(2)}) copy-start(bf16[128,2048]{1,0:T(8,128)(2,1)} %copy-done.4) | copy-start | bytes 1572868
  394.8 4.4 copy-start.11
  423.4 32.3 %copy-start.14 = (f32[40960]{0:T(1024)S(1)}, f32[40960]{0:T(1024)}, u32[]{:S(2)}) copy-start(f32[40960]{0:T(1024)} %constant_dynamic-update-slice_fusion.4) | copy-start | bytes 491524
  456.0 0.7 copy-start.15
  666.5 4.9 copy-start.13
  671.4 6.7 copy-start.17
  672.8 7.5 %copy-start.9 = (f32[128,2048]{1,0:T(8,128)S(1)}, f32[128,2048]{1,0:T(8,128)}, u32[]{:S(2)}) copy-start(f32[128,2048]{1,0:T(8,128)} %get-tuple-element.119) | copy-start | bytes 3145732
  675.1 5.2 copy-start.10
  675.1 5.2 copy-start.12
  678.0 3.9 copy-start.8
  682.0 3.7 copy-start.7
  685.7 3.7 copy-start.6
  685.7 5.7 copy-start.1
Sparse Core Ops, SparseCore 0:
  10.9 148.9 all-gather.1

commit v4 on v3

--- a/solution.py
+++ b/solution.py
@@ -270,25 +270,20 @@
     )(*partials)
 
 
-def exchange_kernel(wq_ref, wk_ref, wv_ref, wo_ref, proj_ref, out_ref, own_sem, send_sem, recv_sem):
+def exchange_kernel(wq_ref, wk_ref, wv_ref, proj_ref, own_sem, send_sem, recv_sem):
     z, r, c = place()
     width = proj_ref.shape[1] // 3
     depth = wq_ref.shape[0]
-    out_rows, out_width = out_ref.shape[0], wo_ref.shape[1]
     greet([(z, r, c ^ j) for j in range(1, 4)])
 
     def source(a, target):
-        if a < 3:
-            return (wq_ref, wk_ref, wv_ref)[a].at[:, pl.ds(pl.multiple_of(target * width, width), width)]
-        return wo_ref.at[pl.ds(pl.multiple_of(target * out_rows, out_rows), out_rows), :]
+        return (wq_ref, wk_ref, wv_ref)[a].at[:, pl.ds(pl.multiple_of(target * width, width), width)]
 
     def spot(a, origin):
-        if a < 3:
-            return proj_ref.at[pl.ds(pl.multiple_of(origin * depth, depth), depth), pl.ds(a * width, width)]
-        return out_ref.at[:, pl.ds(pl.multiple_of(origin * out_width, out_width), out_width)]
+        return proj_ref.at[pl.ds(pl.multiple_of(origin * depth, depth), depth), pl.ds(a * width, width)]
 
     waits = []
-    for a in range(4):
+    for a in range(3):
         keep = pltpu.make_async_copy(source(a, c), spot(a, c), own_sem.at[a])
         keep.start()
         waits.append(keep.wait)
@@ -298,7 +293,7 @@
                 recv_sem=recv_sem.at[a, j - 1], device_id=(z, r, c ^ j), device_id_type=MESH)
             copy.start()
             waits.append(copy.wait_send)
-    for a in range(4):
+    for a in range(3):
         for j in range(1, 4):
             arrived = spot(a, c ^ j)
             pltpu.make_async_remote_copy(
@@ -308,84 +303,63 @@
         wait()
 
 
-def exchange_weights(w_query, w_key, w_value, w_out, collective_id):
+def exchange_weights(w_query, w_key, w_value, collective_id):
     depth, half = w_query.shape
-    kind = w_query.dtype
-    width, out_rows, out_width = half // 4, w_out.shape[0] // 4, w_out.shape[1] * 4
+    dma = pltpu.SemaphoreType.DMA
     return pl.pallas_call(
         exchange_kernel,
-        out_shape=[jax.ShapeDtypeStruct((depth * 4, 3 * width), kind), jax.ShapeDtypeStruct((out_rows, out_width), kind)],
-        in_specs=[ANYSPEC] * 4, out_specs=[ANYSPEC] * 2,
-        scratch_shapes=[pltpu.SemaphoreType.DMA((4,)), pltpu.SemaphoreType.DMA((4, 3)), pltpu.SemaphoreType.DMA((4, 3))],
+        out_shape=jax.ShapeDtypeStruct((depth * 4, 3 * (half // 4)), w_query.dtype),
+        in_specs=[ANYSPEC] * 3, out_specs=ANYSPEC,
+        scratch_shapes=[dma((3,)), dma((3, 3)), dma((3, 3))],
         compiler_params=pltpu.CompilerParams(collective_id=collective_id, has_side_effects=True),
-    )(w_query, w_key, w_value, w_out)
-
-
-def total_kernel(value_ref, out_ref, slots, send_sem, recv_sem):
-    z, r, c = place()
-    peers = [(z, r ^ (j >> 2), c ^ (j & 3)) for j in range(1, 8)]
-    greet(peers)
-    copies = []
-    for j, peer in enumerate(peers):
-        copy = pltpu.make_async_remote_copy(
-            src_ref=value_ref, dst_ref=slots.at[j], send_sem=send_sem.at[j], recv_sem=recv_sem.at[j],
-            device_id=peer, device_id_type=MESH)
-        copy.start()
-        copies.append(copy)
-    for copy in copies:
-        copy.wait()
-    here = r * 4 + c
-    total = jnp.zeros(value_ref.shape, jnp.float32)
-    for who in range(8):
-        which = here ^ who
-        term = jnp.where(which == 0, value_ref[...], slots[jnp.maximum(which - 1, 0)])
-        total = total + term
-    out_ref[...] = total
-
-
-def group_total(value, collective_id):
-    return pl.pallas_call(
-        total_kernel,
-        out_shape=jax.ShapeDtypeStruct(value.shape, jnp.float32),
-        in_specs=[pl.BlockSpec(memory_space=pltpu.VMEM)], out_specs=pl.BlockSpec(memory_space=pltpu.VMEM),
-        scratch_shapes=[pltpu.VMEM((7,) + value.shape, jnp.float32), pltpu.SemaphoreType.DMA((7,)), pltpu.SemaphoreType.DMA((7,))],
-        compiler_params=pltpu.CompilerParams(collective_id=collective_id, has_side_effects=True),
-    )(value)
+    )(w_query, w_key, w_value)
+
+
+NEAR, SMALL, WIDE, LAG, AHEAD = (8, 16, 24), (24, 30, 36), (2, 4, 4), 3, 8
 
 
 def finish_kernel(planes, proj_ref, outp_ref, small_ref, scaled_ref, mixed_part, entry_part,
                   proj_out, outp_out, small_out, mixed_out, entry_out, *scratch):
-    (proj_own, outp_own, proj_in, outp_in, small_own, slices, far_slices, own_sem, swap_send, swap_recv, down_send, down_recv,
-     up_send, up_recv, slice_send, slice_recv, far_send, far_recv, whole_send, whole_recv) = scratch[:20]
-    wide = reducer(planes, (mixed_part,), (mixed_out,), [(ref,) for ref in scratch[20:25]], scratch[25:32])
-    near = reducer(1, (entry_part,), (entry_out,), [(ref,) for ref in scratch[32:37]], scratch[37:44])
+    (proj_own, outp_own, proj_in, outp_in, proj_far, outp_far, small_own, slices, far_slices, own_sem, swap_send, swap_recv, down_send, down_recv,
+     far_down, up_send, up_recv, slice_send, slice_recv, far_send, far_recv, whole_send, whole_recv) = scratch[:23]
+    halves = 2
+    share = mixed_out.shape[1] // halves
+    wides = []
+    for h in range(halves):
+        cols = pl.ds(h * share, share)
+        buffers = [(ref.at[:, :, :, cols],) if i in (0, 1, 3) else (ref.at[:, :, cols],) for i, ref in enumerate(scratch[23:28])]
+        wides.append(reducer(planes, (mixed_part.at[:, cols],), (mixed_out.at[:, cols],), buffers, [ref.at[h:h + 1] for ref in scratch[28:35]]))
+    near = reducer(1, (entry_part,), (entry_out,), [(ref,) for ref in scratch[35:40]], scratch[40:47])
     z, r, c = place()
     here = r * 4 + c
     group = [(z, r ^ (j >> 2), c ^ (j & 3)) for j in range(1, 8)]
     greet(group + [(z ^ k, r, c) for k in range(1, planes)])
     width = proj_ref.shape[1] // 3
     depth, out_width = proj_ref.shape[0] // 4, outp_ref.shape[1] // 4
-    out_rows, step = outp_ref.shape[0], proj_ref.shape[0] // 16
-    chunks = 16
+    step, tall = depth // 8, outp_ref.shape[0] // 2
+    chunks = 32
 
     def remote(source, target, send, recv, device):
         return pltpu.make_async_remote_copy(
             src_ref=source, dst_ref=target, send_sem=send, recv_sem=recv, device_id=device, device_id_type=MESH)
 
+    def owner(i):
+        return (i - 24) // 2
+
     def piece(i, target):
-        if i < 12:
-            a, m = i // 4, i % 4
+        if i < 24:
+            a, m = i // 8, i % 8
             return proj_ref.at[pl.ds(pl.multiple_of(target * depth + m * step, step), step), pl.ds(a * width, width)]
-        return outp_ref.at[:, pl.ds(pl.multiple_of(target * out_width, out_width), out_width)]
+        return outp_ref.at[pl.ds((i % 2) * tall, tall), pl.ds(pl.multiple_of(target * out_width, out_width), out_width)]
 
     def spot(i, origin):
-        a, m = i // 4, i % 4
+        a, m = i // 8, i % 8
         return proj_own.at[a, pl.ds(m * step, step), pl.ds(pl.multiple_of(origin * width, width), width)]
 
     def rows(proj, outp, i):
-        if i < 12:
-            return proj.at[i // 4, pl.ds((i % 4) * step, step), :]
-        return outp.at[pl.ds((i - 12) * out_rows, out_rows), :]
+        if i < 24:
+            return proj.at[i // 8, pl.ds((i % 8) * step, step), :]
+        return outp.at[pl.ds((i - 24) * tall, tall), :]
 
     small_copies = []
 
@@ -401,11 +375,11 @@
             copy.start()
             small_copies.append(copy)
 
-    order = [0, 1, 2, 3, 12, 13, 4, 5, 6, 7, 14, 15, 8, 9, 10, 11]
+    order = [24, 25, 0, 1, 26, 27, 2, 3, 28, 29, 4, 5, 30, 31] + list(range(6, 24))
     swaps = []
 
     def issue(i):
-        if i < 12:
+        if i < 24:
             keep = pltpu.make_async_copy(piece(i, c), spot(i, c), own_sem.at[i])
             keep.start()
             for j in range(1, 4):
@@ -413,72 +387,99 @@
                 copy.start()
                 swaps.append(copy)
         else:
-            @pl.when(c == i - 12)
+            @pl.when(c == owner(i))
             def _():
                 pltpu.make_async_copy(piece(i, c), rows(proj_own, outp_own, i), own_sem.at[i]).start()
                 for j in range(1, 4):
                     remote(piece(i, c ^ j), rows(proj_own, outp_own, i), swap_send.at[i, j - 1], swap_recv.at[i, 0], (z, r, c ^ j)).start()
 
-    ahead = 4
+    ahead = AHEAD
     for i in order[:ahead]:
         issue(i)
     near[0](0, 0)
-    lax.fori_loop(0, planes, wide[0], 0)
+    for wide in wides:
+        lax.fori_loop(0, planes, wide[0], 0)
 
     def local_ready(i):
         target = rows(proj_own, outp_own, i)
-        if i < 12:
+        if i < 24:
             pltpu.make_async_copy(piece(i, c), spot(i, c), own_sem.at[i]).wait()
             for j in range(1, 4):
                 arrived = spot(i, c ^ j)
                 remote(arrived, arrived, swap_send.at[i, j - 1], swap_recv.at[i, j - 1], (z, r, c ^ j)).wait_recv()
         else:
-            @pl.when(c == i - 12)
+            @pl.when(c == owner(i))
             def _():
                 pltpu.make_async_copy(piece(i, c), target, own_sem.at[i]).wait()
 
-            @pl.when(c != i - 12)
+            @pl.when(c != owner(i))
             def _():
                 remote(target, target, swap_send.at[i, 0], swap_recv.at[i, 0], (z, r, c ^ 1)).wait_recv()
 
-    def combine(target, first, second, count):
+    def combine(target, sources, count):
         def body(s, _):
             at = pl.ds(pl.multiple_of(s * 32, 32), 32)
-            total = first[at].astype(jnp.float32) + second[at].astype(jnp.float32)
+            total = sources[0][at].astype(jnp.float32)
+            for source in sources[1:]:
+                total = total + source[at].astype(jnp.float32)
             target[at] = total.astype(target.dtype)
             return 0
         lax.fori_loop(0, count // 32, body, 0)
 
     def seat(i):
-        root_low = i % 2 == 0
-        spot_from_root = z if root_low else planes - 1 - z
-        up = (jnp.minimum(z + 1, planes - 1) if root_low else jnp.maximum(z - 1, 0), r, c)
-        down = (jnp.maximum(z - 1, 0) if root_low else jnp.minimum(z + 1, planes - 1), r, c)
-        return spot_from_root, up, down
-
-    def count_of(i):
-        return step if i < 12 else out_rows
-
-    def to_root(i, p):
-        _, up, down = seat(i)
-        own, arriving, result = rows(proj_own, outp_own, i), rows(proj_in, outp_in, i), rows(proj_out, outp_out, i)
-        local_ready(i)
-        if p < planes - 1:
-            remote(arriving, arriving, down_send.at[i], down_recv.at[i], up).wait_recv()
+        return z if i % 2 == 0 else planes - 1 - z
+
+    def at_seat(i, p):
+        return (p if i % 2 == 0 else planes - 1 - p, r, c)
+
+    def refs(i):
+        return [rows(proj, outp, i) for proj, outp in ((proj_own, outp_own), (proj_in, outp_in), (proj_far, outp_far), (proj_out, outp_out))]
+
+    def down_copy(i, p):
+        own, near_in, far_in, _ = refs(i)
         if p == 0:
-            combine(result, own, arriving, count_of(i))
-            remote(result, result, up_send.at[i], up_recv.at[i], up).start()
+            return remote(own, near_in, down_send.at[i], down_recv.at[i], at_seat(i, 1))
+        return remote(own, far_in, down_send.at[i], far_down.at[i], at_seat(i, p - 1))
+
+    def up_copy(i, p, target):
+        result = refs(i)[3]
+        return remote(result, result, up_send.at[i, 0 if target == 0 else 1], up_recv.at[i], at_seat(i, target))
+
+    def hop(i, h):
+        own, near_in, far_in, result = refs(i)
+
+        if h == 0:
+            for p in (0, 3):
+                @pl.when(seat(i) == p)
+                def _(p=p):
+                    local_ready(i)
+                    down_copy(i, p).start()
+        elif h == 1:
+            @pl.when(seat(i) == 2)
+            def _():
+                local_ready(i)
+                down_copy(i, 3).wait_recv()
+                combine(own, [own, far_in], own.shape[0])
+                down_copy(i, 2).start()
+        elif h == 2:
+            @pl.when(seat(i) == 1)
+            def _():
+                local_ready(i)
+                down_copy(i, 0).wait_recv()
+                down_copy(i, 2).wait_recv()
+                combine(result, [own, near_in, far_in], own.shape[0])
+                up_copy(i, 1, 0).start()
+                up_copy(i, 1, 2).start()
+        elif h == 3:
+            @pl.when(seat(i) == 2)
+            def _():
+                up_copy(i, 1, 2).wait_recv()
+                up_copy(i, 2, 3).start()
         else:
-            if p < planes - 1:
-                combine(own, own, arriving, count_of(i))
-            remote(own, arriving, down_send.at[i], down_recv.at[i], down).start()
-
-    def from_root(i, p):
-        _, up, down = seat(i)
-        result = rows(proj_out, outp_out, i)
-        remote(result, result, up_send.at[i], up_recv.at[i], down).wait_recv()
-        if p < planes - 1:
-            remote(result, result, up_send.at[i], up_recv.at[i], up).start()
+            for p in (0, 3):
+                @pl.when(seat(i) == p)
+                def _(p=p):
+                    up_copy(i, 1, p).wait_recv()
 
     def small_group():
         for j in range(1, 8):
@@ -507,59 +508,55 @@
             copy.start()
             small_copies.append(copy)
 
-    lag = 2
-    hops = 2 * planes - 1
-    top = planes - 1
-    actions = {0: [lambda: near[1](0)], 3: [lambda: near[2](0)], 6: [lambda: near[3](0), small_begin], 10: [small_group], 16: [small_far]}
-    for turn in range(planes + 2):
-        todo = []
-        if turn < planes:
-            todo.append(lambda k=top - turn: wide[1](k))
-        if 0 <= turn - 1 < planes:
-            todo.append(lambda k=top - turn + 1: wide[2](k))
-        if 0 <= turn - 2 < planes:
-            todo.append(lambda k=top - turn + 2: wide[3](k))
-        for n, action in enumerate(todo):
-            actions.setdefault(2 + 4 * turn + n, []).append(action)
-    for s in range(chunks + (hops - 1) * lag):
+    lag = LAG
+    hops = 5
+    actions = {}
+
+    def plan(slot, action):
+        actions.setdefault(slot, []).append(action)
+
+    for slot, kind in zip(NEAR, (1, 2, 3)):
+        plan(slot, lambda kind=kind: near[kind](0))
+    for slot, action in zip(SMALL, (small_begin, small_group, small_far)):
+        plan(slot, action)
+    turns = [(k, h) for k in reversed(range(planes)) for h in range(halves)]
+    for n, (k, h) in enumerate(turns):
+        for kind in (1, 2, 3):
+            plan(int(WIDE[0] + n * WIDE[1] + (kind - 1) * WIDE[2]), lambda k=k, h=h, kind=kind: wides[h][kind](k))
+    slots = chunks + (hops - 1) * lag
+    for s in range(max(slots, max(actions) + 1)):
         if s + ahead < chunks:
             issue(order[s + ahead])
         for h in range(hops):
             if 0 <= s - h * lag < chunks:
-                i = order[s - h * lag]
-                p = planes - 1 - h if h < planes else h - planes + 1
-
-                @pl.when(seat(i)[0] == p)
-                def _(i=i, p=p, h=h):
-                    if h < planes:
-                        to_root(i, p)
-                    else:
-                        from_root(i, p)
+                hop(order[s - h * lag], h)
         for action in actions.get(s, ()):
             action()
     for j in range(1, 8):
         arrived = small_out.at[here ^ j]
         remote(arrived, arrived, whole_send.at[0], whole_recv.at[here ^ j], group[j - 1]).wait_recv()
     near[4](0, 0)
-    lax.fori_loop(0, planes, wide[4], 0)
+    for wide in wides:
+        lax.fori_loop(0, planes, wide[4], 0)
     for copy in small_copies + swaps:
         copy.wait_send()
-    for i in range(12, 16):
-        @pl.when(c == i - 12)
+    for i in range(24, 32):
+        @pl.when(c == owner(i))
         def _():
             for j in range(1, 4):
                 remote(piece(i, c ^ j), rows(proj_own, outp_own, i), swap_send.at[i, j - 1], swap_recv.at[i, 0], (z, r, c ^ j)).wait_send()
     for i in range(chunks):
-        p, up, down = seat(i)
-        own, arriving, result = rows(proj_own, outp_own, i), rows(proj_in, outp_in, i), rows(proj_out, outp_out, i)
-
-        @pl.when(p > 0)
-        def _():
-            remote(own, arriving, down_send.at[i], down_recv.at[i], down).wait_send()
-
-        @pl.when(p < planes - 1)
-        def _():
-            remote(result, result, up_send.at[i], up_recv.at[i], up).wait_send()
+        @pl.when(seat(i) != 1)
+        def _(i=i):
+            down_copy(i, 0).wait_send()
+
+        @pl.when(seat(i) == 1)
+        def _(i=i):
+            up_copy(i, 1, 0).wait_send()
+
+        @pl.when(jnp.logical_or(seat(i) == 1, seat(i) == 2))
+        def _(i=i):
+            up_copy(i, 1, 2).wait_send()
 
 
 def finish(grad_proj_own, grad_out_own, small, scaled, mixed_part, entry_part, planes, collective_id):
@@ -569,7 +566,8 @@
     proj, outp = (3, depth, 4 * width), (4 * out_rows, out_width)
     vmem = pl.BlockSpec(memory_space=pltpu.VMEM)
     dma = pltpu.SemaphoreType.DMA
-    [(mixed_shape, _)], mixed_buffers, mixed_semaphores = reduce_scratch([mixed_part], planes)
+    [(mixed_shape, _)], mixed_buffers, _ = reduce_scratch([mixed_part], planes)
+    mixed_semaphores = reduce_scratch([mixed_part] * 2, planes)[2]
     [(entry_shape, _)], entry_buffers, entry_semaphores = reduce_scratch([entry_part], 1)
     return pl.pallas_call(
         functools.partial(finish_kernel, planes),
@@ -577,9 +575,9 @@
                    jax.ShapeDtypeStruct(mixed_shape, jnp.float32), jax.ShapeDtypeStruct(entry_shape, jnp.float32)],
         in_specs=[ANYSPEC, ANYSPEC, vmem, vmem, ANYSPEC, ANYSPEC], out_specs=[vmem] * 5,
         scratch_shapes=[
-            pltpu.VMEM(proj, kind), pltpu.VMEM(outp, kind), pltpu.VMEM(proj, kind), pltpu.VMEM(outp, kind),
+            pltpu.VMEM(proj, kind), pltpu.VMEM(outp, kind), pltpu.VMEM(proj, kind), pltpu.VMEM(outp, kind), pltpu.VMEM(proj, kind), pltpu.VMEM(outp, kind),
             pltpu.VMEM(small.shape, jnp.float32), pltpu.VMEM(small.shape, jnp.float32), pltpu.VMEM((planes,) + small.shape[1:], jnp.float32),
-            dma((16,)), dma((16, 3)), dma((16, 3)), dma((16,)), dma((16,)), dma((16,)), dma((16,)),
+            dma((32,)), dma((32, 3)), dma((32, 3)), dma((32,)), dma((32,)), dma((32,)), dma((32, 2)), dma((32,)),
             dma((8,)), dma((8,)), dma((planes,)), dma((planes,)), dma((8,)), dma((8,))]
         + mixed_buffers + mixed_semaphores + entry_buffers + entry_semaphores,
         compiler_params=pltpu.CompilerParams(collective_id=collective_id, has_side_effects=True, vmem_limit_bytes=58 * 2**20),
@@ -804,9 +802,9 @@
     def loads(g):
         slot = g % 2
         at = pl.ds(pl.multiple_of(g * group, group), group)
-        pairs = [(all_h, rows_h.at[slot]), (cot, rows_c.at[slot])] + [
-            (source, rows_x.at[slot, i]) for i, source in enumerate((active, grad_gate, grad_up))]
-        return [pltpu.make_async_copy(source.at[at], target, load_sem.at[slot, i]) for i, (source, target) in enumerate(pairs)]
+        pairs = [(all_h.at[at], rows_h.at[slot]), (cot.at[at], rows_c.at[slot])] + [
+            (source.at[at], rows_x.at[slot, i]) for i, source in enumerate((active, grad_gate, grad_up))]
+        return [pltpu.make_async_copy(source, target, load_sem.at[slot, i]) for i, (source, target) in enumerate(pairs)]
 
     def store(g):
         at = pl.ds(pl.multiple_of(g * group, group), group)
@@ -939,9 +937,23 @@
 
 
 def forward_kernel(width, x_ref, proj_ref, gains, cosine, sine, w_out_ref,
-                   part_out, query_out, key_out, value_out, raw_out, scale_out, mixed_out,
-                   sums, slots, send_sem, recv_sem):
+                   part_out, query_out, key_out, value_out, raw_out, scale_out, mixed_out, w_out_own,
+                   sums, slots, send_sem, recv_sem, keep_sem, swap_send, swap_recv):
     greet(group_peers()[1])
+    z, r, c = place()
+    rows, lanes_out = w_out_own.shape[0], w_out_ref.shape[1]
+
+    def piece(target):
+        return w_out_ref.at[pl.ds(pl.multiple_of(target * rows, rows), rows), :]
+
+    def spot(origin):
+        return w_out_own.at[:, pl.ds(pl.multiple_of(origin * lanes_out, lanes_out), lanes_out)]
+
+    keep = pltpu.make_async_copy(piece(c), spot(c), keep_sem.at[0])
+    keep.start()
+    swaps = [pltpu.make_async_remote_copy(
+        src_ref=piece(c ^ j), dst_ref=spot(c), send_sem=swap_send.at[j - 1], recv_sem=swap_recv.at[j - 1],
+        device_id=(z, r, c ^ j), device_id_type=MESH) for j in range(1, 4)]
     local = value_out.shape[1]
     raw = dot_plain(x_ref[...], proj_ref[...])
     raw_out[...] = raw[:, :2 * local]
@@ -951,6 +963,8 @@
         half = raw_out[:, pl.ds(i * local, local)]
         sums[pl.ds(i, 1), :] = row_of_tokens(half * half)
     total = group_sums(sums, slots, send_sem, recv_sem)
+    for swap in swaps:
+        swap.start()
     for i, (target, factor) in enumerate(((query_out, 128 ** (-0.5)), (key_out, 1.0))):
         scale = lax.rsqrt(column_of(total[i:i + 1]) / width + EPSILON)
         scale_out[:, pl.ds(i * 128, 128)] = scale
@@ -967,10 +981,13 @@
             weights = block_weights(queries, keys, first, first + BLOCK).astype(jnp.bfloat16)
             mixed = dot_plain(weights, values[:first + BLOCK])
             mixed_out[pl.ds(first, BLOCK), lanes] = mixed.astype(jnp.bfloat16)
-    part_out[...] = dot_plain(mixed_out[...], w_out_ref[...]).astype(jnp.bfloat16)
-
-
-def attention_forward(gathered_x, w_proj, gains, cosine, sine, w_out_own, collective_id):
+    keep.wait()
+    for swap in swaps:
+        swap.wait()
+    part_out[...] = dot_plain(mixed_out[...], w_out_own[...]).astype(jnp.bfloat16)
+
+
+def attention_forward(gathered_x, w_proj, gains, cosine, sine, w_out, collective_id):
     tokens, width = gathered_x.shape
     local = w_proj.shape[1] // 3
     low, wide = jnp.bfloat16, jnp.float32
@@ -979,11 +996,12 @@
     return pl.pallas_call(
         functools.partial(forward_kernel, width),
         out_shape=[shape((tokens, width), low), shape((tokens, local), low), shape((tokens, local), low), shape((tokens, local), low),
-                   shape((tokens, 2 * local), wide), shape((tokens, 256), wide), shape((tokens, local), low)],
-        in_specs=[vmem] * 6, out_specs=[vmem] * 7,
-        scratch_shapes=[pltpu.VMEM((8, tokens), wide), pltpu.VMEM((7, 8, tokens), wide), dma((7,)), dma((7,))],
+                   shape((tokens, 2 * local), wide), shape((tokens, 256), wide), shape((tokens, local), low),
+                   shape((w_out.shape[0] // 4, 4 * w_out.shape[1]), low)],
+        in_specs=[vmem] * 5 + [ANYSPEC], out_specs=[vmem] * 8,
+        scratch_shapes=[pltpu.VMEM((8, tokens), wide), pltpu.VMEM((7, 8, tokens), wide), dma((7,)), dma((7,)), dma((1,)), dma((3,)), dma((3,))],
         compiler_params=pltpu.CompilerParams(collective_id=collective_id, has_side_effects=True, vmem_limit_bytes=56 * 2**20),
-    )(gathered_x, w_proj, gains, cosine, sine, w_out_own)
+    )(gathered_x, w_proj, gains, cosine, sine, w_out)
 
 
 def backward_kernel(width, grad_ref, w_out_ref, x_hbm, proj_hbm, query_ref, key_ref, value_ref, raw_ref, scale_ref, mixed_ref,
@@ -1091,19 +1109,11 @@
     return [lax.psum_scatter(a, axes, scatter_dimension=0, tiled=True).astype(jnp.float32) for a in arrays]
 
 
-def to_heads(w_query, w_key, w_value, w_out):
+def to_heads(w_query, w_key, w_value):
     if on_links():
-        return exchange_weights(w_query, w_key, w_value, w_out, 1)
+        return exchange_weights(w_query, w_key, w_value, 1)
     pieces = [lax.all_to_all(w, "col", split_axis=1, concat_axis=0, tiled=True) for w in (w_query, w_key, w_value)]
-    return jnp.concatenate(pieces, axis=1), lax.all_to_all(w_out, "col", split_axis=0, concat_axis=1, tiled=True)
-
-
-def sum_over_heads(first_part, second_part, collective_id):
-    if on_links():
-        stacked = jnp.concatenate([first_part, second_part]).reshape(-1, 128)
-        total = group_total(stacked, collective_id).reshape(2, -1)
-        return total[0], total[1]
-    return lax.psum((first_part, second_part), GROUP)
+    return jnp.concatenate(pieces, axis=1)
 
 
 def inverse_rms(values):
@@ -1239,8 +1249,8 @@
 
 
 def expert_rows(normal_h, side, cotangent, gate_use, up_use, down_use, expert_count):
-    all_cotangent = lax.all_gather(cotangent, EVERYONE, axis=0, tiled=True)
     if on_links():
+        all_cotangent = lax.all_gather(cotangent, EVERYONE, axis=0, tiled=True)
         rows_h, _, entry_part, grad_side, active_share, grad_gate_rows, grad_up_rows = expert_rows_on_links(
             normal_h, side, all_cotangent, gate_use, up_use, down_use, expert_count, 6
         )
@@ -1248,7 +1258,7 @@
             entry_part, grad_side, rows_h, all_cotangent, active_share, grad_gate_rows, grad_up_rows, down_use, 7
         )
         return (entry_rows, grad_probs_all, out_part, *grads)
-    rows_h, rows_side = gather_tokens([normal_h, side], True, 6, 2)
+    all_cotangent, rows_h, rows_side = gather_tokens([cotangent, normal_h, side], True, 6, 2)
     expert = lax.axis_index("dp") * lax.axis_size("col") + lax.axis_index("col")
     lane = jnp.arange(side.shape[1])
     own_share = jnp.sum(
@@ -1305,7 +1315,7 @@
 
     inv_input = inverse_rms(inputs)
     normal_x = (inputs * inv_input * norm_attn).astype(jnp.bfloat16)
-    w_proj, w_out_own = to_heads(w_query, w_key, w_value, w_out)
+    w_proj = to_heads(w_query, w_key, w_value)
     (gathered_x,) = gather_tokens([normal_x], False, 2, 2)
     group_tokens = gathered_x.shape[0]
     local_width = w_proj.shape[1] // 3
@@ -1322,14 +1332,15 @@
         gains = jnp.concatenate([gain_query[None], gain_key[None], jnp.zeros((6, local_width), jnp.float32)])
         sine_signed = jnp.where(jnp.arange(HEAD_DIM) < HEAD_DIM // 2, -sine_table[:, 0], sine_table[:, 0])
         tables = (gains, cosine[:, 0], sine_signed)
-        attn_part, *kept = attention_forward(gathered_x, w_proj, *tables, w_out_own, 4)
+        attn_part, *kept, w_out_own = attention_forward(gathered_x, w_proj, *tables, w_out, 4)
     else:
+        w_out_own = lax.all_to_all(w_out, "col", split_axis=0, concat_axis=1, tiled=True)
         raw = contract(gathered_x, w_proj)
         query_raw = raw[:, :local_width]
         key_raw = raw[:, local_width : 2 * local_width]
         value_heads = raw[:, 2 * local_width :].astype(jnp.bfloat16)
-        query_square, key_square = sum_over_heads(
-            jnp.sum(query_raw * query_raw, axis=-1), jnp.sum(key_raw * key_raw, axis=-1), 4
+        query_square, key_square = lax.psum(
+            (jnp.sum(query_raw * query_raw, axis=-1), jnp.sum(key_raw * key_raw, axis=-1)), GROUP
         )
         inv_query = lax.rsqrt(query_square / model_width + EPSILON)[:, None]
         inv_key = lax.rsqrt(key_square / model_width + EPSILON)[:, None]
@@ -1417,8 +1428,8 @@
         )
         weighted_q = gain_query * grad_normal_q
         weighted_k = gain_key * grad_normal_k
-        inner_q, inner_k = sum_over_heads(
-            jnp.sum(weighted_q * query_raw, axis=-1), jnp.sum(weighted_k * key_raw, axis=-1), 10
+        inner_q, inner_k = lax.psum(
+            (jnp.sum(weighted_q * query_raw, axis=-1), jnp.sum(weighted_k * key_raw, axis=-1)), GROUP
         )
         grad_query_raw = (
             inv_query * weighted_q - query_raw * inv_query**3 * inner_q[:, None] / model_width

time: 708 us -> 681 us (0.962)
  the two profiles are of different devices: /device:TPU:1 before, /device:TPU:6 now
where the time goes in v4:
time: 681 us; the launch traced here: 672 us
  Pallas kernels  608 us (89%)
  other arithmetic  25.3 us (4%)
  local copies, waits for them, and re-layouts  20.1 us (3%)
  between operations  14.8 us (2%)
    pallas_call x1, Pallas kernels, finish(): pl.pallas_call(functools.partial(finish_kernel, planes), out_shape=[jax.S...  187 us
    pallas_call x1, Pallas kernels, expert_rows_on_links(): pl.pallas_call(functools.partial(expert_kernel, planes, experts), out_sha...  116 us
    pallas_call x1, Pallas kernels, entry_sums(): pl.pallas_call(functools.partial(entry_kernel, planes), out_shape=[jax.Sh...  104 us
    pallas_call x1, Pallas kernels, exchange_weights(): pl.pallas_call(exchange_kernel, out_shape=jax.ShapeDtypeStruct((depth * 4...  53.1 us
    pallas_call x2, Pallas kernels, gather(): pl.pallas_call(functools.partial(gather_kernel, planes, parts, count), ou...  48.2 us
    pallas_call x1, Pallas kernels, attention_forward(): pl.pallas_call(functools.partial(forward_kernel, width), out_shape=[shape...  44.5 us
    pallas_call x1, Pallas kernels, attention_backward(): pl.pallas_call(functools.partial(backward_kernel, width), out_shape=[shap...  31.4 us
    pallas_call x1, Pallas kernels, reduce_scatter(): pl.pallas_call(functools.partial(reduce_kernel, planes, count), out_shape...  24 us
  transfers between devices with their start and end apart: 1, of which 0 were waited for; matrix products, arithmetic and copies ran while one was open for 2% of the time, Pallas kernels for 22%

profile of v4, /device:TPU:6, one launch (start us, length us, event | category | flops | bytes accessed | tf_op | source)
XLA Modules:
  0.0 671.6 jit_solution(740860337850154465)
XLA Ops:
  7.2 0.0 copy-start
  7.2 0.0 all-gather.2.cloned.1.call-start
  7.2 0.7 all-gather.2.cloned.1.call-update
  7.9 0.8 dynamic_slice.6
  8.7 0.8 dynamic_slice.7
  9.5 1.2 fusion
  10.7 0.5 multiply_multiply_fusion
  11.2 2.4 convert_multiply_fusion.2
  13.6 25.9 %shard_map.254.x_ref.x_hbm = bf16[1024,2048]{1,0:T(8,128)(2,1)} custom-call(bf16[128,2048]{1,0:T(8,128)(2,1)} %get-tuple-element.124.refs_0_), custom_call_target="tpu_custom_call" | custom-call | tf_op jit(solution)/shard_map/pallas_call | solution.py:100
  39.5 0.1 pad.7.clone
  39.5 53.1 %shard_map.255.proj_ref.proj_hbm = bf16[2048,768]{1,0:T(8,128)(2,1)} custom-call(bf16[512,1024]{1,0:T(8,128)(2,1)} %wq_ref.1, bf16[512,1024]{1,0:T(8,128)(2,1)} %wk_ref.1, bf16[512,1024]{1,0:T(8,128)(2,1)} %wv_ref.1), custom_call_target="tpu_custom_call" | custom-call | tf_op jit(solution)/shard_map/pallas_call | solution.py:309
  92.7 0.7 maximum_maximum_fusion.1.gains
  93.3 0.2 broadcast_multiply_fusion
  93.6 2.9 negate_select_fusion
  96.5 44.5 %shard_map.256 = (bf16[1024,2048]{1,0:T(8,128)(2,1)}, bf16[1024,256]{1,0:T(8,128)(2,1)}, bf16[1024,256]{1,0:T(8,128)(2,1)}, bf16[1024,256]{1,0:T(8,128)(2,1)}, f...) custom-call(bf16[1024,2048]{1,0:T(8,128)(2,1)} %shard_map.254.x_ref.x_hbm, ...), custom_call_target="tpu_custom_call" | custom-call | tf_op jit(solution)/shard_map/pallas_call | solution.py:996
  141.0 0.0 copy-start.2
  141.0 2.2 copy-done.2
  143.2 24.0 %shard_map.257 = f32[128,2048]{1,0:T(8,128)S(1)} custom-call(bf16[1024,2048]{1,0:T(8,128)(2,1)S(1)} %copy-done.2), custom_call_target="tpu_custom_call" | custom-call | tf_op jit(solution)/shard_map/pallas_call | solution.py:264
  167.2 0.0 copy-done.3
  167.2 0.2 multiply_reduce_fusion.2
  167.4 0.5 multiply_multiply_fusion.1
  167.9 0.0 copy-done.15
  167.9 0.2 multiply_convert_fusion.own_h
  168.1 0.0 copy-start.4
  168.1 0.3 fusion.16
  168.4 0.1 copy.41
  168.5 0.1 copy.43
  168.6 0.1 pad.2.clone
  168.7 0.2 fusion.8
  168.9 0.1 multiply_convert_fusion.3
  169.0 0.7 maximum_maximum_fusion.own_side
  169.7 116.1 %shard_map.258 = (bf16[4096,2048]{1,0:T(8,128)(2,1)}, bf16[4096,128]{1,0:T(8,128)(2,1)}, bf16[4096,2048]{1,0:T(8,128)(2,1)}, bf16[4096,128]{1,0:T(8,128)(2,1)}, ...) custom-call(bf16[128,2048]{1,0:T(8,128)(2,1)} %copy-done.4, ...), custom_call_target="tpu_custom_call" | custom-call | tf_op jit(solution)/shard_map/pallas_call | solution.py:780
  285.8 0.0 copy-start.5
  285.9 104.2 %shard_map.259 = (f32[128,2048]{1,0:T(8,128)}, f32[128,128]{1,0:T(8,128)}, bf16[4096,2048]{1,0:T(8,128)(2,1)}, f32[2048,512]{1,0:T(8,128)}, f32[2048,512]{1,0:T(8,128)}, /*index=5*/f32[512,2048]{1,0:T(8,128)}) custom-call(bf16[4096,2048]{1,0:T(8,128)(2,1)} %get-tuple-element.44.entry_part, bf16[4096,128]{1,0:T(8,128)(2,1)} %get-tuple-element.45.route_part, ...), custom_call_target="tpu_custom_call" | custom-call | tf_op jit(solution)/shard_map/pallas_call | solution.py:868
  390.1 0.0 copy-start.11
  390.1 1.1 multiply_reduce_fusion.3
  391.2 1.0 multiply_convert_fusion.2
  392.1 0.3 fusion.17
  392.5 0.3 reshape.99
  392.8 1.7 multiply_reduce_fusion
  394.5 2.2 fusion.13
  396.7 22.4 %shard_map.260.grad_ref = bf16[1024,2048]{1,0:T(8,128)(2,1)} custom-call(bf16[128,2048]{1,0:T(8,128)(2,1)} %get-tuple-element.116.refs_0_), custom_call_target="tpu_custom_call" | custom-call | tf_op jit(solution)/shard_map/pallas_call | solution.py:100
  419.1 31.4 %shard_map.261 = (bf16[1024,2048]{1,0:T(8,128)(2,1)}, bf16[2048,768]{1,0:T(8,128)(2,1)}, bf16[256,2048]{1,0:T(8,128)(2,1)}, f32[8,256]{1,0:T(8,128)}) custom-call(bf16[1024,2048]{1,0:T(8,128)(2,1)} %shard_map.260.grad_ref, bf16[256,2048]{1,0:T(8,128)(2,1)} %get-tuple-element.52.w_out_ref, bf16[1024,2048]{1,0:T(8,128)(2,1)} %shard_map.254.x_ref.x_hbm, ...), custom_call_target="tpu_custom_call" | custom-call | tf_op jit(solution)/shard_map/pallas_call | solution.py:1072
  450.5 0.8 fusion.15
  451.3 0.2 dynamic_update_slice.6
  451.5 0.3 dynamic_update_slice.7
  451.8 0.0 copy-start.14
  451.8 0.7 copy-done.14
  452.5 186.8 %shard_map.262 = (bf16[3,512,1024]{2,1,0:T(8,128)(2,1)}, bf16[1024,512]{1,0:T(8,128)(2,1)}, f32[8,40,128]{2,1,0:T(8,128)}, f32[128,2048]{1,0:T(8,128)}, f32[128,2048]{1,0:T(8,128)}) custom-call(bf16[2048,768]{1,0:T(8,128)(2,1)} %get-tuple-element.59.proj_ref, bf16[256,2048]{1,0:T(8,128)(2,1)} %get-tuple-element.60.outp_ref, f32[8,40,128]{2,1,0:T(8,128)} %bitcast.35, ...), custom_call_target="tpu_custom_call" | custom-call | tf_op jit(solution)/shard_map/pallas_call | solution.py:572
  639.4 4.8 bitcast_convert_fusion
  644.2 0.4 slice.46
  644.6 0.0 copy-start.18
  644.6 1.0 slice.52
  645.6 2.3 copy.46
  647.9 3.0 convert_element_type.81
  650.9 1.6 fusion.5
  652.5 0.6 fusion.14
  653.1 0.0 copy-done.10
  653.1 1.7 fusion.4
  654.9 2.1 copy.57
  657.0 1.6 copy-done.7
  658.6 2.1 copy.58
  660.7 1.6 copy-done.6
  662.3 2.0 copy.59
  (38 shorter events, 0.1 us)
Async XLA Ops:
  7.2 160.9 %copy-start = (bf16[2048,16]{0,1:T(8,128)(2,1)S(1)}, bf16[2048,16]{0,1:T(8,128)(2,1)}, u32[]{:S(2)}) copy-start(bf16[2048,16]{0,1:T(8,128)(2,1)} %param.25) | copy-start | bytes 196612
  7.2 162.5 %all-gather.2.cloned.1.call-start = ((), (), s32[]{:S(2)}) async-start(), calls=%async_computation | async-start | bytes 17301504 | tf_op jit(solution)/shard_map/all_gather | solution.py:1253
  141.0 2.2 copy-start.2
  143.2 24.0 %copy-start.3 = (bf16[128,2048]{1,0:T(8,128)(2,1)S(1)}, bf16[128,2048]{1,0:T(8,128)(2,1)}, u32[]{:S(2)}) copy-start(bf16[128,2048]{1,0:T(8,128)(2,1)} %param.15) | copy-start | bytes 1572868
  143.2 24.7 %copy-start.15 = (f32[2048]{0:T(1024)S(1)}, f32[2048]{0:T(1024)}, u32[]{:S(2)}) copy-start(f32[2048]{0:T(1024)} %param.24) | copy-start | bytes 24580
  143.2 25.3 %copy-start.17 = (s32[128,8]{0,1:T(8,128)S(1)}, s32[128,8]{0,1:T(8,128)}, u32[]{:S(2)}) copy-start(s32[128,8]{0,1:T(8,128)} %param.29) | copy-start | bytes 12292
  168.1 1.6 copy-start.4
  285.8 106.3 %copy-start.5 = (bf16[128,2048]{1,0:T(8,128)(2,1)S(1)}, bf16[128,2048]{1,0:T(8,128)(2,1)}, u32[]{:S(2)}) copy-start(bf16[128,2048]{1,0:T(8,128)(2,1)} %copy-done.4) | copy-start | bytes 1572868
  390.1 4.4 copy-start.11
  451.8 0.7 copy-start.14
  639.3 4.9 copy-start.13
  644.2 6.7 copy-start.16
  644.6 8.5 %copy-start.18 = (f32[128]{0:T(128)S(1)}, f32[128]{0:T(128)}, u32[]{:S(2)}) copy-start(f32[128]{0:T(128)} %get-tuple-element.135) | copy-start | bytes 1540
  645.6 7.5 %copy-start.9 = (f32[128,2048]{1,0:T(8,128)S(1)}, f32[128,2048]{1,0:T(8,128)}, u32[]{:S(2)}) copy-start(f32[128,2048]{1,0:T(8,128)} %get-tuple-element.117) | copy-start | bytes 3145732
  647.9 5.2 copy-start.10
  647.9 5.2 copy-start.12
  650.9 3.9 copy-start.8
  654.8 3.7 copy-start.7
  658.6 3.7 copy-start.6
  658.6 5.7 copy-start.1
Sparse Core Ops, SparseCore 0:
  10.9 144.7 all-gather.1

commit v5 on v4

--- a/solution.py
+++ b/solution.py
@@ -9,6 +9,7 @@
 
 MESH = pl.DeviceIdType.MESH
 ANYSPEC = pl.BlockSpec(memory_space=pl.ANY)
+CUTS = 2
 
 def place():
     return lax.axis_index("dp"), lax.axis_index("row"), lax.axis_index("col")
@@ -20,13 +21,16 @@
     pl.semaphore_wait(barrier, len(peers))
 
 def gather_kernel(planes, parts, count, *refs):
-    ins, outs = refs[:count], refs[count:2 * count]
-    own_sem, send_sem, recv_sem = refs[2 * count:]
+    gather_steps(planes, parts, refs[:count], refs[count:2 * count], *refs[2 * count:])
+
+
+def gather_steps(planes, parts, ins, outs, own_sem, send_sem, recv_sem, more_peers=(), beside=None):
+    count = len(ins)
     z, r, c = place()
     first, second, diag = c ^ (1 + r), c ^ (2 - r), c ^ 3
     partner = (z, 1 - r, c)
     to_first, to_second = (z, r, first), (z, r, second)
-    greet([to_first, to_second, partner] + [(z ^ k, r, c) for k in range(1, planes)])
+    greet([to_first, to_second, partner] + [(z ^ k, r, c) for k in range(1, planes)] + list(more_peers))
     pieces = []
     for a in range(count):
         cut = parts if a == 0 else 1
@@ -63,6 +67,8 @@
     for i in every:
         for target in [to_first, to_second] + [(z ^ k, r, c) for k in range(1, planes)] + [partner]:
             send(i, mine, target, True)
+    if beside is not None:
+        beside()
     for a in range(count):
         keep = pltpu.make_async_copy(ins[a], outs[a].at[pl.ds(pl.multiple_of(mine * ins[a].shape[0], ins[a].shape[0]), ins[a].shape[0])], own_sem.at[a])
         keep.start()
@@ -105,19 +111,23 @@
         compiler_params=pltpu.CompilerParams(collective_id=collective_id, has_side_effects=True),
     )(*arrays)
 
-def reducer(planes, parts, outs, buffers, semaphores):
+def reducer(planes, cuts, parts, outs, buffers, semaphores):
     held, fromp, relay, near, far = buffers
     load_sem, pair_send, pair_recv, send_sem, relay_recv, near_recv, far_recv = semaphores
     z, r, c = place()
     first, second, diag = c ^ (1 + r), c ^ (2 - r), c ^ 3
     partner = (z, 1 - r, c)
     to_first, to_second = (z, r, first), (z, r, second)
-    depth = outs[0].shape[0]
+    full = outs[0].shape[0]
+    depth = full // cuts
     every = range(len(parts))
 
-    def rows(a, k, rr, cc):
-        which = (((z ^ k) if planes > 1 else 0) * 2 + rr) * 4 + cc
-        return parts[a].at[pl.ds(pl.multiple_of(which * depth, depth), depth)]
+    def cut(ref, v):
+        return ref.at[pl.ds(pl.multiple_of((v % cuts) * depth, depth), depth)]
+
+    def rows(a, v, rr, cc):
+        which = (((z ^ (v // cuts)) if planes > 1 else 0) * 2 + rr) * 4 + cc
+        return parts[a].at[pl.ds(pl.multiple_of(which * full + (v % cuts) * depth, depth), depth)]
 
     columns, partner_columns = [c, first, second, diag], [c, second, first, diag]
 
@@ -125,18 +135,27 @@
         return pltpu.make_async_remote_copy(
             src_ref=source, dst_ref=target, send_sem=send, recv_sem=recv, device_id=device, device_id_type=MESH)
 
-    def load(a, k, j):
-        return pltpu.make_async_copy(rows(a, k, r, columns[j]), held[a].at[k, j], load_sem.at[a, k, j])
-
-    def pair(a, k, j):
-        return remote(rows(a, k, 1 - r, partner_columns[j]), fromp[a].at[k, j], pair_send.at[a, k, j], pair_recv.at[a, k, j], partner)
+    def mine(a, v, j):
+        return cut(held[a].at[v // cuts, j], v)
+
+    def paired(a, v, j):
+        return cut(fromp[a].at[v // cuts, j], v)
+
+    def nearby(a, v, which):
+        return cut(near[a].at[v // cuts, which], v)
+
+    def load(a, v, j):
+        return pltpu.make_async_copy(rows(a, v, r, columns[j]), mine(a, v, j), load_sem.at[a, v, j])
+
+    def pair(a, v, j):
+        return remote(rows(a, v, 1 - r, partner_columns[j]), paired(a, v, j), pair_send.at[a, v, j], pair_recv.at[a, v, j], partner)
 
     def begin(i, _):
-        k = planes - 1 - i
+        v = planes * cuts - 1 - i
         for j in (3, 2, 1, 0):
             for a in every:
-                load(a, k, j).start()
-                pair(a, k, j).start()
+                load(a, v, j).start()
+                pair(a, v, j).start()
         return 0
 
     step_rows = min(32, depth)
@@ -151,116 +170,118 @@
             return 0
         lax.fori_loop(0, depth // step_rows, body, 0)
 
-    def ready(a, k, j):
-        load(a, k, j).wait()
-        pair(a, k, j).wait_recv()
-
-    def to_diag(a, k):
-        return remote(held[a].at[k, 3], relay[a].at[k], send_sem.at[a, k, 0], relay_recv.at[a, k], to_second)
-
-    def to_near(a, k, which):
-        source, device = (held[a].at[k, 2], to_second) if which else (held[a].at[k, 1], to_first)
-        return remote(source, near[a].at[k, which], send_sem.at[a, k, 1 + which], near_recv.at[a, k, which], device)
-
-    def to_far(a, k):
-        slot = jnp.maximum(k - 1, 0)
-        return remote(held[a].at[k, 0], far[a].at[slot], send_sem.at[a, k, 3], far_recv.at[a, slot], (z ^ k, r, c))
-
-    def to_relay(k):
+    def ready(a, v, j):
+        load(a, v, j).wait()
+        pair(a, v, j).wait_recv()
+
+    def to_diag(a, v):
+        return remote(mine(a, v, 3), cut(relay[a].at[v // cuts], v), send_sem.at[a, v, 0], relay_recv.at[a, v], to_second)
+
+    def to_near(a, v, which):
+        source, device = (mine(a, v, 2), to_second) if which else (mine(a, v, 1), to_first)
+        return remote(source, nearby(a, v, which), send_sem.at[a, v, 1 + which], near_recv.at[a, v, which], device)
+
+    def to_far(a, v):
+        slot = jnp.maximum(v - cuts, 0)
+        return remote(mine(a, v, 0), cut(far[a].at[slot // cuts], v), send_sem.at[a, v, 3], far_recv.at[a, slot], (z ^ (v // cuts), r, c))
+
+    def to_relay(v):
         for a in every:
-            ready(a, k, 3)
-            add(held[a].at[k, 3], [held[a].at[k, 3], fromp[a].at[k, 3]])
-            to_diag(a, k).start()
+            ready(a, v, 3)
+            add(mine(a, v, 3), [mine(a, v, 3), paired(a, v, 3)])
+            to_diag(a, v).start()
         for a in every:
-            ready(a, k, 2)
-            add(held[a].at[k, 2], [held[a].at[k, 2], fromp[a].at[k, 2]])
-            to_near(a, k, 1).start()
-
-    def pass_on(k):
+            ready(a, v, 2)
+            add(mine(a, v, 2), [mine(a, v, 2), paired(a, v, 2)])
+            to_near(a, v, 1).start()
+
+    def pass_on(v):
         for a in every:
-            ready(a, k, 1)
-            to_diag(a, k).wait_recv()
-            add(held[a].at[k, 1], [held[a].at[k, 1], fromp[a].at[k, 1], relay[a].at[k]])
-            to_near(a, k, 0).start()
-
-    def collect(k):
+            ready(a, v, 1)
+            to_diag(a, v).wait_recv()
+            add(mine(a, v, 1), [mine(a, v, 1), paired(a, v, 1), cut(relay[a].at[v // cuts], v)])
+            to_near(a, v, 0).start()
+
+    def collect(v):
         for a in every:
-            ready(a, k, 0)
-            to_near(a, k, 0).wait_recv()
-            to_near(a, k, 1).wait_recv()
-            terms = [held[a].at[k, 0], fromp[a].at[k, 0], near[a].at[k, 0], near[a].at[k, 1]]
-
-            @pl.when(k > 0)
+            ready(a, v, 0)
+            to_near(a, v, 0).wait_recv()
+            to_near(a, v, 1).wait_recv()
+            terms = [mine(a, v, 0), paired(a, v, 0), nearby(a, v, 0), nearby(a, v, 1)]
+
+            @pl.when(v >= cuts)
             def _():
-                add(held[a].at[k, 0], terms)
-                to_far(a, k).start()
-
-            @pl.when(k == 0)
+                add(mine(a, v, 0), terms)
+                to_far(a, v).start()
+
+            @pl.when(v < cuts)
             def _():
                 for i in range(1, planes):
-                    to_far(a, i).wait_recv()
-                add(outs[a], terms + [far[a].at[i] for i in range(planes - 1)])
-
-    def drain(k, _):
+                    to_far(a, v + i * cuts).wait_recv()
+                add(cut(outs[a], v), terms + [cut(far[a].at[i], v) for i in range(planes - 1)])
+
+    def drain(v, _):
         for a in every:
             for j in range(4):
-                pair(a, k, j).wait_send()
-            to_diag(a, k).wait_send()
-            to_near(a, k, 0).wait_send()
-            to_near(a, k, 1).wait_send()
-
-            @pl.when(k > 0)
+                pair(a, v, j).wait_send()
+            to_diag(a, v).wait_send()
+            to_near(a, v, 0).wait_send()
+            to_near(a, v, 1).wait_send()
+
+            @pl.when(v >= cuts)
             def _():
-                to_far(a, k).wait_send()
+                to_far(a, v).wait_send()
         return 0
 
     return begin, to_relay, pass_on, collect, drain
 
 
-def reduce_steps(planes, parts, outs, buffers, semaphores, filler):
+def reduce_steps(planes, cuts, parts, outs, buffers, semaphores, filler):
     z, r, c = place()
     greet([(z, r, c ^ 1), (z, r, c ^ 2), (z, 1 - r, c)] + [(z ^ k, r, c) for k in range(1, planes)])
-    begin, to_relay, pass_on, collect, drain = reducer(planes, parts, outs, buffers, semaphores)
-    lax.fori_loop(0, planes, begin, 0)
+    begin, to_relay, pass_on, collect, drain = reducer(planes, cuts, parts, outs, buffers, semaphores)
+    units = planes * cuts
+    lax.fori_loop(0, units, begin, 0)
+    lag = 1
 
     def step_body(step, _):
-        @pl.when(step < planes)
+        @pl.when(step < units)
         def _():
-            to_relay(planes - 1 - step)
-
-        @pl.when(jnp.logical_and(step >= 1, step < planes + 1))
+            to_relay(units - 1 - step)
+
+        @pl.when(jnp.logical_and(step >= lag, step < units + lag))
         def _():
-            pass_on(planes - step)
-
-        @pl.when(step >= 2)
+            pass_on(units - 1 - step + lag)
+
+        @pl.when(step >= 2 * lag)
         def _():
-            collect(planes + 1 - step)
+            collect(units - 1 - step + 2 * lag)
         if filler is not None:
             filler(step)
         return 0
 
-    lax.fori_loop(0, planes + 2, step_body, 0)
-    lax.fori_loop(0, planes, drain, 0)
-
-
-def reduce_scratch(partials, planes):
+    lax.fori_loop(0, units + 2 * lag, step_body, 0)
+    lax.fori_loop(0, units, drain, 0)
+
+
+def reduce_scratch(partials, planes, cuts):
     shapes = [((p.shape[0] // (planes * 8), p.shape[1]), p.dtype) for p in partials]
-    count, far = len(partials), max(planes - 1, 1)
+    count, far, units = len(partials), max(planes - 1, 1), planes * cuts
     dma = pltpu.SemaphoreType.DMA
     buffers = [pltpu.VMEM(lead + shape, kind) for lead in ((planes, 4), (planes, 4), (planes,), (planes, 2), (far,)) for shape, kind in shapes]
     return shapes, buffers, [
-        dma((count, planes, 4)), dma((count, planes, 4)), dma((count, planes, 4)), dma((count, planes, 4)),
-        dma((count, planes)), dma((count, planes, 2)), dma((count, far))]
+        dma((count, units, 4)), dma((count, units, 4)), dma((count, units, 4)), dma((count, units, 4)),
+        dma((count, units)), dma((count, units, 2)), dma((count, far * cuts))]
 
 
 def reduce_kernel(planes, count, *refs):
     buffers = [refs[(2 + i) * count:(3 + i) * count] for i in range(5)]
-    reduce_steps(planes, refs[:count], refs[count:2 * count], buffers, refs[7 * count:], None)
+    reduce_steps(planes, CUTS, refs[:count], refs[count:2 * count], buffers, refs[7 * count:], None)
 
 
 def reduce_scatter(partials, planes, collective_id):
     count = len(partials)
-    shapes, buffers, semaphores = reduce_scratch(partials, planes)
+    shapes, buffers, semaphores = reduce_scratch(partials, planes, CUTS)
     return pl.pallas_call(
         functools.partial(reduce_kernel, planes, count),
         out_shape=[jax.ShapeDtypeStruct(shape, jnp.float32) for shape, _ in shapes],
@@ -270,11 +291,10 @@
     )(*partials)
 
 
-def exchange_kernel(wq_ref, wk_ref, wv_ref, proj_ref, own_sem, send_sem, recv_sem):
+def opening_kernel(x_ref, wq_ref, wk_ref, wv_ref, all_x, proj_ref, own_sem, send_sem, recv_sem, keep_sem, swap_send, swap_recv):
     z, r, c = place()
     width = proj_ref.shape[1] // 3
     depth = wq_ref.shape[0]
-    greet([(z, r, c ^ j) for j in range(1, 4)])
 
     def source(a, target):
         return (wq_ref, wk_ref, wv_ref)[a].at[:, pl.ds(pl.multiple_of(target * width, width), width)]
@@ -282,37 +302,38 @@
     def spot(a, origin):
         return proj_ref.at[pl.ds(pl.multiple_of(origin * depth, depth), depth), pl.ds(a * width, width)]
 
-    waits = []
+    keeps = [pltpu.make_async_copy(source(a, c), spot(a, c), keep_sem.at[a]) for a in range(3)]
+    swaps = [pltpu.make_async_remote_copy(
+        src_ref=source(a, c ^ j), dst_ref=spot(a, c), send_sem=swap_send.at[a, j - 1], recv_sem=swap_recv.at[a, j - 1],
+        device_id=(z, r, c ^ j), device_id_type=MESH) for a in range(3) for j in range(1, 4)]
+
+    def beside():
+        for copy in keeps + swaps:
+            copy.start()
+
+    gather_steps(1, 2, (x_ref,), (all_x,), own_sem, send_sem, recv_sem, [(z, r, c ^ 3)], beside)
     for a in range(3):
-        keep = pltpu.make_async_copy(source(a, c), spot(a, c), own_sem.at[a])
-        keep.start()
-        waits.append(keep.wait)
-        for j in range(1, 4):
-            copy = pltpu.make_async_remote_copy(
-                src_ref=source(a, c ^ j), dst_ref=spot(a, c), send_sem=send_sem.at[a, j - 1],
-                recv_sem=recv_sem.at[a, j - 1], device_id=(z, r, c ^ j), device_id_type=MESH)
-            copy.start()
-            waits.append(copy.wait_send)
-    for a in range(3):
+        keeps[a].wait()
         for j in range(1, 4):
             arrived = spot(a, c ^ j)
             pltpu.make_async_remote_copy(
-                src_ref=arrived, dst_ref=arrived, send_sem=send_sem.at[a, j - 1], recv_sem=recv_sem.at[a, j - 1],
+                src_ref=arrived, dst_ref=arrived, send_sem=swap_send.at[a, j - 1], recv_sem=swap_recv.at[a, j - 1],
                 device_id=(z, r, c ^ j), device_id_type=MESH).wait_recv()
-    for wait in waits:
-        wait()
-
-
-def exchange_weights(w_query, w_key, w_value, collective_id):
+    for swap in swaps:
+        swap.wait_send()
+
+
+def opening(normal_x, w_query, w_key, w_value, collective_id):
     depth, half = w_query.shape
     dma = pltpu.SemaphoreType.DMA
+    shape = jax.ShapeDtypeStruct
     return pl.pallas_call(
-        exchange_kernel,
-        out_shape=jax.ShapeDtypeStruct((depth * 4, 3 * (half // 4)), w_query.dtype),
-        in_specs=[ANYSPEC] * 3, out_specs=ANYSPEC,
-        scratch_shapes=[dma((3,)), dma((3, 3)), dma((3, 3))],
+        opening_kernel,
+        out_shape=[shape((8 * normal_x.shape[0], normal_x.shape[1]), normal_x.dtype), shape((depth * 4, 3 * (half // 4)), w_query.dtype)],
+        in_specs=[ANYSPEC] * 4, out_specs=[ANYSPEC] * 2,
+        scratch_shapes=[dma((1,)), dma((2, 7)), dma((2, 8)), dma((3,)), dma((3, 3)), dma((3, 3))],
         compiler_params=pltpu.CompilerParams(collective_id=collective_id, has_side_effects=True),
-    )(w_query, w_key, w_value)
+    )(normal_x, w_query, w_key, w_value)
 
 
 NEAR, SMALL, WIDE, LAG, AHEAD = (8, 16, 24), (24, 30, 36), (2, 4, 4), 3, 8
@@ -322,14 +343,8 @@
                   proj_out, outp_out, small_out, mixed_out, entry_out, *scratch):
     (proj_own, outp_own, proj_in, outp_in, proj_far, outp_far, small_own, slices, far_slices, own_sem, swap_send, swap_recv, down_send, down_recv,
      far_down, up_send, up_recv, slice_send, slice_recv, far_send, far_recv, whole_send, whole_recv) = scratch[:23]
-    halves = 2
-    share = mixed_out.shape[1] // halves
-    wides = []
-    for h in range(halves):
-        cols = pl.ds(h * share, share)
-        buffers = [(ref.at[:, :, :, cols],) if i in (0, 1, 3) else (ref.at[:, :, cols],) for i, ref in enumerate(scratch[23:28])]
-        wides.append(reducer(planes, (mixed_part.at[:, cols],), (mixed_out.at[:, cols],), buffers, [ref.at[h:h + 1] for ref in scratch[28:35]]))
-    near = reducer(1, (entry_part,), (entry_out,), [(ref,) for ref in scratch[35:40]], scratch[40:47])
+    wide = reducer(planes, CUTS, (mixed_part,), (mixed_out,), [(ref,) for ref in scratch[23:28]], scratch[28:35])
+    near = reducer(1, 1, (entry_part,), (entry_out,), [(ref,) for ref in scratch[35:40]], scratch[40:47])
     z, r, c = place()
     here = r * 4 + c
     group = [(z, r ^ (j >> 2), c ^ (j & 3)) for j in range(1, 8)]
@@ -397,8 +412,7 @@
     for i in order[:ahead]:
         issue(i)
     near[0](0, 0)
-    for wide in wides:
-        lax.fori_loop(0, planes, wide[0], 0)
+    lax.fori_loop(0, planes * CUTS, wide[0], 0)
 
     def local_ready(i):
         target = rows(proj_own, outp_own, i)
@@ -519,10 +533,9 @@
         plan(slot, lambda kind=kind: near[kind](0))
     for slot, action in zip(SMALL, (small_begin, small_group, small_far)):
         plan(slot, action)
-    turns = [(k, h) for k in reversed(range(planes)) for h in range(halves)]
-    for n, (k, h) in enumerate(turns):
+    for n in range(planes * CUTS):
         for kind in (1, 2, 3):
-            plan(int(WIDE[0] + n * WIDE[1] + (kind - 1) * WIDE[2]), lambda k=k, h=h, kind=kind: wides[h][kind](k))
+            plan(int(WIDE[0] + n * WIDE[1] + (kind - 1) * WIDE[2]), lambda v=planes * CUTS - 1 - n, kind=kind: wide[kind](v))
     slots = chunks + (hops - 1) * lag
     for s in range(max(slots, max(actions) + 1)):
         if s + ahead < chunks:
@@ -536,8 +549,7 @@
         arrived = small_out.at[here ^ j]
         remote(arrived, arrived, whole_send.at[0], whole_recv.at[here ^ j], group[j - 1]).wait_recv()
     near[4](0, 0)
-    for wide in wides:
-        lax.fori_loop(0, planes, wide[4], 0)
+    lax.fori_loop(0, planes * CUTS, wide[4], 0)
     for copy in small_copies + swaps:
         copy.wait_send()
     for i in range(24, 32):
@@ -566,9 +578,8 @@
     proj, outp = (3, depth, 4 * width), (4 * out_rows, out_width)
     vmem = pl.BlockSpec(memory_space=pltpu.VMEM)
     dma = pltpu.SemaphoreType.DMA
-    [(mixed_shape, _)], mixed_buffers, _ = reduce_scratch([mixed_part], planes)
-    mixed_semaphores = reduce_scratch([mixed_part] * 2, planes)[2]
-    [(entry_shape, _)], entry_buffers, entry_semaphores = reduce_scratch([entry_part], 1)
+    [(mixed_shape, _)], mixed_buffers, mixed_semaphores = reduce_scratch([mixed_part], planes, CUTS)
+    [(entry_shape, _)], entry_buffers, entry_semaphores = reduce_scratch([entry_part], 1, 1)
     return pl.pallas_call(
         functools.partial(finish_kernel, planes),
         out_shape=[jax.ShapeDtypeStruct(proj, kind), jax.ShapeDtypeStruct(outp, kind), jax.ShapeDtypeStruct(small.shape, small.dtype),
@@ -843,8 +854,7 @@
         mixed_stage[...] = jnp.dot(rows_x[slot, 0], down_use[...], preferred_element_type=jnp.float32).astype(jnp.bfloat16)
         store(g).start()
 
-    steps = planes + 2
-    per_step = -(-groups // (steps - 2))
+    per_step = -(-groups // (planes * CUTS))
 
     def filler(step):
         def body(i, _):
@@ -854,14 +864,14 @@
             return 0
         lax.fori_loop(0, per_step, body, 0)
 
-    reduce_steps(planes, (entry_part, route_part), (entry_out, route_out), buffers, semaphores, filler)
+    reduce_steps(planes, CUTS, (entry_part, route_part), (entry_out, route_out), buffers, semaphores, filler)
     store(groups - 1).wait()
 
 
 def entry_sums(entry_part, route_part, all_h, cot, active, grad_gate, grad_up, w_down, collective_id):
     planes = lax.axis_size("dp")
     partials = [entry_part, route_part]
-    shapes, buffers, semaphores = reduce_scratch(partials, planes)
+    shapes, buffers, semaphores = reduce_scratch(partials, planes, CUTS)
     (count, width), hidden, group = shapes[0][0], w_down.shape[0], 256
     low, wide, vmem, dma = jnp.bfloat16, jnp.float32, pltpu.VMEM, pltpu.SemaphoreType.DMA
     kept = pl.BlockSpec(memory_space=pltpu.VMEM)
@@ -1109,11 +1119,12 @@
     return [lax.psum_scatter(a, axes, scatter_dimension=0, tiled=True).astype(jnp.float32) for a in arrays]
 
 
-def to_heads(w_query, w_key, w_value):
+def open_attention(normal_x, w_query, w_key, w_value):
     if on_links():
-        return exchange_weights(w_query, w_key, w_value, 1)
+        return opening(normal_x, w_query, w_key, w_value, 1)
     pieces = [lax.all_to_all(w, "col", split_axis=1, concat_axis=0, tiled=True) for w in (w_query, w_key, w_value)]
-    return jnp.concatenate(pieces, axis=1)
+    (gathered_x,) = gather_tokens([normal_x], False, 2, 2)
+    return gathered_x, jnp.concatenate(pieces, axis=1)
 
 
 def inverse_rms(values):
@@ -1315,8 +1326,7 @@
 
     inv_input = inverse_rms(inputs)
     normal_x = (inputs * inv_input * norm_attn).astype(jnp.bfloat16)
-    w_proj = to_heads(w_query, w_key, w_value)
-    (gathered_x,) = gather_tokens([normal_x], False, 2, 2)
+    gathered_x, w_proj = open_attention(normal_x, w_query, w_key, w_value)
     group_tokens = gathered_x.shape[0]
     local_width = w_proj.shape[1] // 3
     head_count = local_width // HEAD_DIM
@@ -1402,7 +1412,7 @@
         probabilities * (grad_probs - jnp.sum(probabilities * grad_probs, axis=-1, keepdims=True))
     ).astype(jnp.bfloat16)
     grad_normal_h = entry_rows + contract_cols(grad_logits, w_router)
-    grad_router_part = contract_rows(normal_h, grad_logits)
+    grad_router_part = contract_rows(grad_logits, normal_h)
     grad_state_part, grad_moe_part = norm_backward(state_rows, inv_state, norm_moe, grad_normal_h)
     grad_state = upstream + grad_state_part
     grad_attn = grad_state.astype(jnp.bfloat16)
@@ -1454,6 +1464,7 @@
         grad_proj_own, grad_out_own, small, inputs * inv_input, mixture, grad_x_part
     )
     grad_norm_attn, grad_query_gain, grad_key_gain, grad_norm_moe, grad_router = small
+    grad_router = grad_router.T
     block_out = (state_rows + mixture).astype(jnp.bfloat16)
     grad_input = grad_state + norm_backward(inputs, inv_input, norm_attn, grad_normal_x)[0]
     return (

time: 681 us -> 661 us (0.971)
  Pallas kernels: 608 us -> 595 us
    pallas_call x2 -> x1, Pallas kernels: 48.2 us -> 22.6 us  [gather(): pl.pallas_call(functools.partial(gather_kernel, planes, parts, count), ou...]
    pallas_call x1, Pallas kernels: 53.1 us -> 74.1 us  [opening(): pl.pallas_call(opening_kernel, out_shape=[shape((8 * normal_x.shape[0], n...]
    pallas_call x1, Pallas kernels: 104 us -> 92.6 us  [entry_sums(): pl.pallas_call(functools.partial(entry_kernel, planes), out_shape=[jax.Sh...]
    unnamed x46 -> x42, local copies, waits for them, and re-layouts: 14.6 us -> 12.4 us
where the time goes in v5:
time: 661 us; the launch traced here: 651 us
  Pallas kernels  595 us (90%)
  other arithmetic  22 us (3%)
  local copies, waits for them, and re-layouts  16.8 us (3%)
  between operations  14.8 us (2%)
    pallas_call x1, Pallas kernels, finish(): pl.pallas_call(functools.partial(finish_kernel, planes), out_shape=[jax.S...  187 us
    pallas_call x1, Pallas kernels, expert_rows_on_links(): pl.pallas_call(functools.partial(expert_kernel, planes, experts), out_sha...  116 us
    pallas_call x1, Pallas kernels, entry_sums(): pl.pallas_call(functools.partial(entry_kernel, planes), out_shape=[jax.Sh...  92.6 us
    pallas_call x1, Pallas kernels, opening(): pl.pallas_call(opening_kernel, out_shape=[shape((8 * normal_x.shape[0], n...  74.1 us
    pallas_call x1, Pallas kernels, attention_forward(): pl.pallas_call(functools.partial(forward_kernel, width), out_shape=[shape...  48.7 us
    pallas_call x1, Pallas kernels, attention_backward(): pl.pallas_call(functools.partial(backward_kernel, width), out_shape=[shap...  31.4 us
    pallas_call x1, Pallas kernels, gather(): pl.pallas_call(functools.partial(gather_kernel, planes, parts, count), ou...  22.6 us
    pallas_call x1, Pallas kernels, reduce_scatter(): pl.pallas_call(functools.partial(reduce_kernel, planes, count), out_shape...  22.2 us
  transfers between devices with their start and end apart: 1, of which 0 were waited for; matrix products, arithmetic and copies ran while one was open for 2% of the time, Pallas kernels for 22%

profile of v5, /device:TPU:6, one launch (start us, length us, event | category | flops | bytes accessed | tf_op | source)
XLA Modules:
  0.0 651.4 jit_solution(6800153484388400980)
XLA Ops:
  7.2 0.0 copy-start
  7.2 0.0 all-gather.2.cloned.1.call-start
  7.2 0.7 all-gather.2.cloned.1.call-update
  7.9 0.8 dynamic_slice.6
  8.7 0.8 dynamic_slice.7
  9.5 0.1 pad.7.clone
  9.5 1.2 fusion
  10.8 2.4 convert_multiply_fusion.2
  13.2 74.1 %shard_map.254 = (bf16[1024,2048]{1,0:T(8,128)(2,1)}, bf16[2048,768]{1,0:T(8,128)(2,1)}) custom-call(bf16[128,2048]{1,0:T(8,128)(2,1)} %get-tuple-element.86.x_ref, bf16[512,1024]{1,0:T(8,128)(2,1)} %wq_ref.1, bf16[512,1024]{1,0:T(8,128)(2,1)} %wk_ref.1, bf16[512,1024]{1,0:T(8,128)(2,1)} %wv_ref.1), custom_call_target="tpu_custom_call" | custom-call | tf_op jit(solution)/shard_map/pallas_call | solution.py:330
  87.3 0.7 maximum_maximum_fusion.1.gains
  87.9 0.2 broadcast_multiply_fusion
  88.1 2.9 negate_select_fusion
  91.1 48.7 %shard_map.255 = (bf16[1024,2048]{1,0:T(8,128)(2,1)}, bf16[1024,256]{1,0:T(8,128)(2,1)}, bf16[1024,256]{1,0:T(8,128)(2,1)}, bf16[1024,256]{1,0:T(8,128)(2,1)}, f...) custom-call(bf16[1024,2048]{1,0:T(8,128)(2,1)} %get-tuple-element.45.x_ref.x_hb, ...), custom_call_target="tpu_custom_call" | custom-call | tf_op jit(solution)/shard_map/pallas_call | solution.py:1006
  139.8 0.0 copy-start.2
  139.8 2.2 copy-done.2
  142.0 22.2 %shard_map.256 = f32[128,2048]{1,0:T(8,128)S(1)} custom-call(bf16[1024,2048]{1,0:T(8,128)(2,1)S(1)} %copy-done.2), custom_call_target="tpu_custom_call" | custom-call | tf_op jit(solution)/shard_map/pallas_call | solution.py:285
  164.2 0.0 copy-done.3
  164.2 0.2 multiply_reduce_fusion.2
  164.5 0.0 copy-done.14
  164.5 0.2 multiply_convert_fusion.own_h
  164.7 0.0 copy-done
  164.7 0.0 copy-start.4
  164.7 0.3 fusion.16
  164.9 0.1 copy.34
  165.0 0.0 copy-done.16
  165.1 0.1 copy.36
  165.2 0.1 pad.2.clone
  165.3 0.2 fusion.8
  165.4 0.1 multiply_convert_fusion.3
  165.6 0.7 maximum_maximum_fusion.own_side
  166.3 0.0 copy-done.4
  166.3 116.3 %shard_map.257 = (bf16[4096,2048]{1,0:T(8,128)(2,1)}, bf16[4096,128]{1,0:T(8,128)(2,1)}, bf16[4096,2048]{1,0:T(8,128)(2,1)}, bf16[4096,128]{1,0:T(8,128)(2,1)}, ...) custom-call(bf16[128,2048]{1,0:T(8,128)(2,1)} %copy-done.4, ...), custom_call_target="tpu_custom_call" | custom-call | tf_op jit(solution)/shard_map/pallas_call | solution.py:791
  282.6 0.0 copy-start.5
  282.6 92.6 %shard_map.258 = (f32[128,2048]{1,0:T(8,128)}, f32[128,128]{1,0:T(8,128)}, bf16[4096,2048]{1,0:T(8,128)(2,1)}, f32[2048,512]{1,0:T(8,128)}, f32[2048,512]{1,0:T(8,128)}, /*index=5*/f32[512,2048]{1,0:T(8,128)}) custom-call(bf16[4096,2048]{1,0:T(8,128)(2,1)} %get-tuple-element.48.entry_part, bf16[4096,128]{1,0:T(8,128)(2,1)} %get-tuple-element.49.route_part, ...), custom_call_target="tpu_custom_call" | custom-call | tf_op jit(solution)/shard_map/pallas_call | solution.py:878
  375.2 0.0 copy-start.10
  375.2 1.1 multiply_reduce_fusion.3
  376.3 1.0 multiply_convert_fusion.2
  377.3 0.0 copy-done.5
  377.3 0.2 convolution_bitcast_fusion
  377.5 1.7 multiply_reduce_fusion
  379.2 0.0 copy-done.10
  379.2 1.2 fusion.13
  380.5 22.6 %shard_map.259.grad_ref = bf16[1024,2048]{1,0:T(8,128)(2,1)} custom-call(bf16[128,2048]{1,0:T(8,128)(2,1)} %get-tuple-element.78.refs_0_), custom_call_target="tpu_custom_call" | custom-call | tf_op jit(solution)/shard_map/pallas_call | solution.py:106
  403.1 31.4 %shard_map.260 = (bf16[1024,2048]{1,0:T(8,128)(2,1)}, bf16[2048,768]{1,0:T(8,128)(2,1)}, bf16[256,2048]{1,0:T(8,128)(2,1)}, f32[8,256]{1,0:T(8,128)}) custom-call(bf16[1024,2048]{1,0:T(8,128)(2,1)} %shard_map.259.grad_ref, bf16[256,2048]{1,0:T(8,128)(2,1)} %get-tuple-element.56.w_out_ref, bf16[1024,2048]{1,0:T(8,128)(2,1)} %get-tuple-element.45.x_ref.x_hbm, ...), custom_call_target="tpu_custom_call" | custom-call | tf_op jit(solution)/shard_map/pallas_call | solution.py:1082
  434.5 0.8 fusion.15
  435.3 0.2 dynamic_update_slice.6
  435.5 0.3 dynamic_update_slice.7
  435.8 0.0 copy-start.13
  435.8 0.7 copy-done.13
  436.4 186.9 %shard_map.261 = (bf16[3,512,1024]{2,1,0:T(8,128)(2,1)}, bf16[1024,512]{1,0:T(8,128)(2,1)}, f32[8,40,128]{2,1,0:T(8,128)}, f32[128,2048]{1,0:T(8,128)}, f32[128,2048]{1,0:T(8,128)}) custom-call(bf16[2048,768]{1,0:T(8,128)(2,1)} %get-tuple-element.63.proj_ref, bf16[256,2048]{1,0:T(8,128)(2,1)} %get-tuple-element.64.outp_ref, f32[8,40,128]{2,1,0:T(8,128)} %bitcast.41, ...), custom_call_target="tpu_custom_call" | custom-call | tf_op jit(solution)/shard_map/pallas_call | solution.py:583
  623.3 0.0 copy-start.11
  623.4 0.0 copy-start.15
  623.4 4.9 bitcast_convert_fusion
  628.3 1.6 convert_element_type.81
  629.9 0.2 fusion.5
  630.2 0.0 copy-done.12
  630.2 0.7 slice_bitcast_fusion
  630.9 0.6 fusion.14
  631.5 3.2 fusion.4
  634.7 2.1 copy.48
  636.8 1.6 copy-done.7
  638.4 2.1 copy.49
  640.5 1.6 copy-done.6
  642.1 2.0 copy.50
  (32 shorter events, 0.2 us)
Async XLA Ops:
  7.2 157.5 %copy-start = (bf16[2048,16]{0,1:T(8,128)(2,1)S(1)}, bf16[2048,16]{0,1:T(8,128)(2,1)}, u32[]{:S(2)}) copy-start(bf16[2048,16]{0,1:T(8,128)(2,1)} %param.25) | copy-start | bytes 196612
  7.2 159.1 %all-gather.2.cloned.1.call-start = ((), (), s32[]{:S(2)}) async-start(), calls=%async_computation | async-start | bytes 17301504 | tf_op jit(solution)/shard_map/all_gather | solution.py:1264
  139.8 2.2 copy-start.2
  142.0 22.2 %copy-start.3 = (bf16[128,2048]{1,0:T(8,128)(2,1)S(1)}, bf16[128,2048]{1,0:T(8,128)(2,1)}, u32[]{:S(2)}) copy-start(bf16[128,2048]{1,0:T(8,128)(2,1)} %param.15) | copy-start | bytes 1572868
  142.0 22.5 %copy-start.14 = (f32[2048]{0:T(1024)S(1)}, f32[2048]{0:T(1024)}, u32[]{:S(2)}) copy-start(f32[2048]{0:T(1024)} %param.24) | copy-start | bytes 24580
  142.0 23.0 %copy-start.16 = (s32[128,8]{0,1:T(8,128)S(1)}, s32[128,8]{0,1:T(8,128)}, u32[]{:S(2)}) copy-start(s32[128,8]{0,1:T(8,128)} %param.29) | copy-start | bytes 12292
  164.7 1.6 copy-start.4
  282.6 94.7 %copy-start.5 = (bf16[128,2048]{1,0:T(8,128)(2,1)S(1)}, bf16[128,2048]{1,0:T(8,128)(2,1)}, u32[]{:S(2)}) copy-start(bf16[128,2048]{1,0:T(8,128)(2,1)} %copy-done.4) | copy-start | bytes 1572868
  375.2 4.0 copy-start.10
  435.8 0.7 copy-start.13
  623.3 5.0 copy-start.11
  623.3 6.6 %copy-start.9 = (f32[128,2048]{1,0:T(8,128)S(1)}, f32[128,2048]{1,0:T(8,128)}, u32[]{:S(2)}) copy-start(f32[128,2048]{1,0:T(8,128)} %get-tuple-element.69) | copy-start | bytes 3145732
  623.4 6.6 %copy-start.15 = (f32[2048]{0:T(1024)S(1)}, f32[2048]{0:T(1024)}, u32[]{:S(2)}) copy-start(f32[2048]{0:T(1024)} %param.17) | copy-start | bytes 24580
  628.3 1.8 copy-start.12
  630.2 4.5 copy-start.8
  634.7 3.7 copy-start.7
  638.4 3.7 copy-start.6
  638.4 5.7 copy-start.1
Sparse Core Ops, SparseCore 0:
  10.9 147.4 all-gather.1

commit v6 on v5

--- a/solution.py
+++ b/solution.py
@@ -2,6 +2,7 @@
 
 import jax
 import jax.numpy as jnp
+import numpy as np
 from jax import lax
 from jax.experimental import pallas as pl
 from jax.experimental.pallas import tpu as pltpu
@@ -31,6 +32,8 @@
     partner = (z, 1 - r, c)
     to_first, to_second = (z, r, first), (z, r, second)
     greet([to_first, to_second, partner] + [(z ^ k, r, c) for k in range(1, planes)] + list(more_peers))
+    if beside is not None:
+        beside()
     pieces = []
     for a in range(count):
         cut = parts if a == 0 else 1
@@ -67,8 +70,6 @@
     for i in every:
         for target in [to_first, to_second] + [(z ^ k, r, c) for k in range(1, planes)] + [partner]:
             send(i, mine, target, True)
-    if beside is not None:
-        beside()
     for a in range(count):
         keep = pltpu.make_async_copy(ins[a], outs[a].at[pl.ds(pl.multiple_of(mine * ins[a].shape[0], ins[a].shape[0]), ins[a].shape[0])], own_sem.at[a])
         keep.start()
@@ -291,7 +292,7 @@
     )(*partials)
 
 
-def opening_kernel(x_ref, wq_ref, wk_ref, wv_ref, all_x, proj_ref, own_sem, send_sem, recv_sem, keep_sem, swap_send, swap_recv):
+def opening_kernel(x_ref, gain_ref, wq_ref, wk_ref, wv_ref, all_x, proj_ref, normal, own_sem, send_sem, recv_sem, keep_sem, swap_send, swap_recv):
     z, r, c = place()
     width = proj_ref.shape[1] // 3
     depth = wq_ref.shape[0]
@@ -310,8 +311,11 @@
     def beside():
         for copy in keeps + swaps:
             copy.start()
-
-    gather_steps(1, 2, (x_ref,), (all_x,), own_sem, send_sem, recv_sem, [(z, r, c ^ 3)], beside)
+        rows = x_ref[...].astype(jnp.float32)
+        scale = lax.rsqrt(jnp.mean(rows * rows, axis=1, keepdims=True) + EPSILON)
+        normal[...] = (rows * scale * gain_ref[...]).astype(jnp.bfloat16)
+
+    gather_steps(1, 2, (normal,), (all_x,), own_sem, send_sem, recv_sem, [(z, r, c ^ 3)], beside)
     for a in range(3):
         keeps[a].wait()
         for j in range(1, 4):
@@ -323,17 +327,17 @@
         swap.wait_send()
 
 
-def opening(normal_x, w_query, w_key, w_value, collective_id):
+def opening(hidden, gain, w_query, w_key, w_value, collective_id):
     depth, half = w_query.shape
     dma = pltpu.SemaphoreType.DMA
     shape = jax.ShapeDtypeStruct
     return pl.pallas_call(
         opening_kernel,
-        out_shape=[shape((8 * normal_x.shape[0], normal_x.shape[1]), normal_x.dtype), shape((depth * 4, 3 * (half // 4)), w_query.dtype)],
-        in_specs=[ANYSPEC] * 4, out_specs=[ANYSPEC] * 2,
-        scratch_shapes=[dma((1,)), dma((2, 7)), dma((2, 8)), dma((3,)), dma((3, 3)), dma((3, 3))],
+        out_shape=[shape((8 * hidden.shape[0], hidden.shape[1]), jnp.bfloat16), shape((depth * 4, 3 * (half // 4)), w_query.dtype)],
+        in_specs=[pl.BlockSpec(memory_space=pltpu.VMEM)] * 2 + [ANYSPEC] * 3, out_specs=[ANYSPEC] * 2,
+        scratch_shapes=[pltpu.VMEM(hidden.shape, jnp.bfloat16), dma((1,)), dma((2, 7)), dma((2, 8)), dma((3,)), dma((3, 3)), dma((3, 3))],
         compiler_params=pltpu.CompilerParams(collective_id=collective_id, has_side_effects=True),
-    )(normal_x, w_query, w_key, w_value)
+    )(hidden, gain, w_query, w_key, w_value)
 
 
 NEAR, SMALL, WIDE, LAG, AHEAD = (8, 16, 24), (24, 30, 36), (2, 4, 4), 3, 8
@@ -1119,9 +1123,9 @@
     return [lax.psum_scatter(a, axes, scatter_dimension=0, tiled=True).astype(jnp.float32) for a in arrays]
 
 
-def open_attention(normal_x, w_query, w_key, w_value):
+def open_attention(hidden_in, norm_attn, normal_x, w_query, w_key, w_value):
     if on_links():
-        return opening(normal_x, w_query, w_key, w_value, 1)
+        return opening(hidden_in, norm_attn[None], w_query, w_key, w_value, 1)
     pieces = [lax.all_to_all(w, "col", split_axis=1, concat_axis=0, tiled=True) for w in (w_query, w_key, w_value)]
     (gathered_x,) = gather_tokens([normal_x], False, 2, 2)
     return gathered_x, jnp.concatenate(pieces, axis=1)
@@ -1155,11 +1159,11 @@
 
 
 def turn_tables(total_rows, seq_length, head_width):
-    positions = (jnp.arange(total_rows) % seq_length).astype(jnp.float32)
-    inverse = THETA ** (-jnp.arange(0, head_width, 2, dtype=jnp.float32) / head_width)
-    angles = positions[:, None] * inverse[None, :]
-    angles = jnp.concatenate([angles, angles], axis=-1)
-    return (jnp.cos(angles)[:, None, :], jnp.sin(angles)[:, None, :])
+    positions = (np.arange(total_rows) % seq_length).astype(np.float32)
+    inverse = np.float32(THETA) ** (-np.arange(0, head_width, 2, dtype=np.float32) / np.float32(head_width))
+    angles = positions[:, None] * inverse.astype(np.float32)[None, :]
+    angles = np.concatenate([angles, angles], axis=-1).astype(np.float64)
+    return (np.cos(angles)[:, None, :].astype(np.float32), np.sin(angles)[:, None, :].astype(np.float32))
 
 
 def rotate(values, cosine, sine_table):
@@ -1326,7 +1330,7 @@
 
     inv_input = inverse_rms(inputs)
     normal_x = (inputs * inv_input * norm_attn).astype(jnp.bfloat16)
-    gathered_x, w_proj = open_attention(normal_x, w_query, w_key, w_value)
+    gathered_x, w_proj = open_attention(hidden_in, norm_attn, normal_x, w_query, w_key, w_value)
     group_tokens = gathered_x.shape[0]
     local_width = w_proj.shape[1] // 3
     head_count = local_width // HEAD_DIM
@@ -1340,8 +1344,8 @@
     in_kernels = on_links() and sequences == 1
     if in_kernels:
         gains = jnp.concatenate([gain_query[None], gain_key[None], jnp.zeros((6, local_width), jnp.float32)])
-        sine_signed = jnp.where(jnp.arange(HEAD_DIM) < HEAD_DIM // 2, -sine_table[:, 0], sine_table[:, 0])
-        tables = (gains, cosine[:, 0], sine_signed)
+        sine_signed = np.where(np.arange(HEAD_DIM) < HEAD_DIM // 2, -sine_table[:, 0], sine_table[:, 0])
+        tables = (gains, jnp.asarray(cosine[:, 0]), jnp.asarray(sine_signed))
         attn_part, *kept, w_out_own = attention_forward(gathered_x, w_proj, *tables, w_out, 4)
     else:
         w_out_own = lax.all_to_all(w_out, "col", split_axis=0, concat_axis=1, tiled=True)

time: 661 us -> 654 us (0.989)
  transfers between devices with their start and end apart: 1 -> 1, of which waited for: 0 -> 0; matrix products, arithmetic and copies ran while one was open for 2% -> 1% of each run, Pallas kernels for 22% -> 23%
where the time goes in v6:
time: 654 us; the launch traced here: 647 us
  Pallas kernels  596 us (91%)
  local copies, waits for them, and re-layouts  16.9 us (3%)
  other arithmetic  16.5 us (3%)
  between operations  14.6 us (2%)
    pallas_call x1, Pallas kernels, finish(): pl.pallas_call(functools.partial(finish_kernel, planes), out_shape=[jax.S...  187 us
    pallas_call x1, Pallas kernels, expert_rows_on_links(): pl.pallas_call(functools.partial(expert_kernel, planes, experts), out_sha...  117 us
    pallas_call x1, Pallas kernels, entry_sums(): pl.pallas_call(functools.partial(entry_kernel, planes), out_shape=[jax.Sh...  92.6 us
    pallas_call x1, Pallas kernels, opening(): pl.pallas_call(opening_kernel, out_shape=[shape((8 * hidden.shape[0], hid...  76.8 us
    pallas_call x1, Pallas kernels, attention_forward(): pl.pallas_call(functools.partial(forward_kernel, width), out_shape=[shape...  45.6 us
    pallas_call x1, Pallas kernels, attention_backward(): pl.pallas_call(functools.partial(backward_kernel, width), out_shape=[shap...  31.4 us
    pallas_call x1, Pallas kernels, reduce_scatter(): pl.pallas_call(functools.partial(reduce_kernel, planes, count), out_shape...  23.3 us
    pallas_call x1, Pallas kernels, gather(): pl.pallas_call(functools.partial(gather_kernel, planes, parts, count), ou...  22.7 us
  transfers between devices with their start and end apart: 1, of which 0 were waited for; matrix products, arithmetic and copies ran while one was open for 1% of the time, Pallas kernels for 23%

profile of v6, /device:TPU:6, one launch (start us, length us, event | category | flops | bytes accessed | tf_op | source)
XLA Modules:
  0.0 646.7 jit_solution(14058308154771239800)
XLA Ops:
  7.2 0.0 copy-start
  7.2 0.0 all-gather.2.cloned.1.call-start
  7.2 0.7 all-gather.2.cloned.1.call-update
  7.9 0.8 dynamic_slice.6
  8.7 0.8 dynamic_slice.7
  9.5 0.1 pad.5.clone
  9.5 76.8 %shard_map.272 = (bf16[1024,2048]{1,0:T(8,128)(2,1)}, bf16[2048,768]{1,0:T(8,128)(2,1)}) custom-call(bf16[128,2048]{1,0:T(8,128)(2,1)} %x_ref.1, f32[1,2048]{1,0:T(1,128)} %bitcast.43, bf16[512,1024]{1,0:T(8,128)(2,1)} %wq_ref.1, bf16[512,1024]{1,0:T(8,128)(2,1)} %wk_ref.1, bf16[512,1024]{1,0:T(8,128)(2,1)} %wv_ref.1), custom_call_target="tpu_custom_call" | custom-call | tf_op jit(solution)/shard_map/pallas_call | solution.py:334
  86.4 0.7 maximum_maximum_fusion.1.gains
  87.0 45.6 %shard_map.273 = (bf16[1024,2048]{1,0:T(8,128)(2,1)}, bf16[1024,256]{1,0:T(8,128)(2,1)}, bf16[1024,256]{1,0:T(8,128)(2,1)}, bf16[1024,256]{1,0:T(8,128)(2,1)}, f...) custom-call(bf16[1024,2048]{1,0:T(8,128)(2,1)} %get-tuple-element.45.x_ref.x_hb, ...), custom_call_target="tpu_custom_call" | custom-call | tf_op jit(solution)/shard_map/pallas_call | solution.py:1010
  132.6 0.0 copy-start.2
  132.6 2.3 copy-done.2
  134.9 23.3 %shard_map.274 = f32[128,2048]{1,0:T(8,128)S(1)} custom-call(bf16[1024,2048]{1,0:T(8,128)(2,1)S(1)} %copy-done.2), custom_call_target="tpu_custom_call" | custom-call | tf_op jit(solution)/shard_map/pallas_call | solution.py:286
  158.2 0.0 copy-done.3
  158.2 0.0 copy-start.16
  158.2 0.2 fusion
  158.4 1.3 multiply_reduce_fusion.2
  159.7 0.0 copy-done.14
  159.7 0.2 multiply_convert_fusion.own_h
  159.9 0.0 copy-done
  159.9 0.0 copy-start.4
  159.9 0.3 fusion.11
  160.1 0.1 copy.36
  160.3 0.0 copy-done.16
  160.3 0.1 copy.38
  160.4 0.1 pad.2.clone
  160.5 0.2 fusion.7
  160.6 0.1 multiply_convert_fusion.2
  160.8 0.7 maximum_maximum_fusion.own_side
  161.5 0.0 copy-done.4
  161.5 116.6 %shard_map.275 = (bf16[4096,2048]{1,0:T(8,128)(2,1)}, bf16[4096,128]{1,0:T(8,128)(2,1)}, bf16[4096,2048]{1,0:T(8,128)(2,1)}, bf16[4096,128]{1,0:T(8,128)(2,1)}, ...) custom-call(bf16[128,2048]{1,0:T(8,128)(2,1)} %copy-done.4, ...), custom_call_target="tpu_custom_call" | custom-call | tf_op jit(solution)/shard_map/pallas_call | solution.py:795
  278.1 0.0 copy-start.5
  278.1 92.6 %shard_map.276 = (f32[128,2048]{1,0:T(8,128)}, f32[128,128]{1,0:T(8,128)}, bf16[4096,2048]{1,0:T(8,128)(2,1)}, f32[2048,512]{1,0:T(8,128)}, f32[2048,512]{1,0:T(8,128)}, /*index=5*/f32[512,2048]{1,0:T(8,128)}) custom-call(bf16[4096,2048]{1,0:T(8,128)(2,1)} %get-tuple-element.48.entry_part, bf16[4096,128]{1,0:T(8,128)(2,1)} %get-tuple-element.49.route_part, ...), custom_call_target="tpu_custom_call" | custom-call | tf_op jit(solution)/shard_map/pallas_call | solution.py:882
  370.7 0.0 copy-start.10
  370.7 1.1 multiply_reduce_fusion.3
  371.8 1.0 multiply_convert_fusion.1
  372.8 0.0 copy-done.5
  372.8 0.2 convolution_bitcast_fusion
  373.0 1.7 multiply_reduce_fusion
  374.7 0.0 copy-done.10
  374.7 1.2 fusion.8
  376.0 22.7 %shard_map.277.grad_ref = bf16[1024,2048]{1,0:T(8,128)(2,1)} custom-call(bf16[128,2048]{1,0:T(8,128)(2,1)} %get-tuple-element.78.refs_0_), custom_call_target="tpu_custom_call" | custom-call | tf_op jit(solution)/shard_map/pallas_call | solution.py:107
  398.6 31.4 %shard_map.278 = (bf16[1024,2048]{1,0:T(8,128)(2,1)}, bf16[2048,768]{1,0:T(8,128)(2,1)}, bf16[256,2048]{1,0:T(8,128)(2,1)}, f32[8,256]{1,0:T(8,128)}) custom-call(bf16[1024,2048]{1,0:T(8,128)(2,1)} %shard_map.277.grad_ref, bf16[256,2048]{1,0:T(8,128)(2,1)} %get-tuple-element.56.w_out_ref, bf16[1024,2048]{1,0:T(8,128)(2,1)} %get-tuple-element.45.x_ref.x_hbm, ...), custom_call_target="tpu_custom_call" | custom-call | tf_op jit(solution)/shard_map/pallas_call | solution.py:1086
  430.0 0.8 fusion.10
  430.8 0.2 dynamic_update_slice.6
  431.0 0.3 dynamic_update_slice.7
  431.3 0.0 copy-start.13
  431.3 0.7 copy-done.13
  432.0 186.9 %shard_map.279 = (bf16[3,512,1024]{2,1,0:T(8,128)(2,1)}, bf16[1024,512]{1,0:T(8,128)(2,1)}, f32[8,40,128]{2,1,0:T(8,128)}, f32[128,2048]{1,0:T(8,128)}, f32[128,2048]{1,0:T(8,128)}) custom-call(bf16[2048,768]{1,0:T(8,128)(2,1)} %get-tuple-element.63.proj_ref, bf16[256,2048]{1,0:T(8,128)(2,1)} %get-tuple-element.64.outp_ref, f32[8,40,128]{2,1,0:T(8,128)} %bitcast.42, ...), custom_call_target="tpu_custom_call" | custom-call | tf_op jit(solution)/shard_map/pallas_call | solution.py:587
  618.9 0.0 copy-start.15
  618.9 4.9 bitcast_convert_fusion
  623.9 0.0 copy-done.11
  623.9 1.6 convert_element_type.67
  625.5 0.0 copy-done.9
  625.5 0.2 fusion.5
  625.8 0.7 slice_bitcast_fusion
  626.4 0.6 fusion.9
  627.1 3.2 fusion.4
  630.2 0.0 copy-done.8
  630.2 2.1 copy.50
  632.4 1.6 copy-done.7
  633.9 2.1 copy.51
  636.1 1.6 copy-done.6
  637.6 2.0 copy.52
  639.7 0.0 copy-done.1
  (26 shorter events, 0.1 us)
Async XLA Ops:
  7.2 152.7 %copy-start = (bf16[2048,16]{0,1:T(8,128)(2,1)S(1)}, bf16[2048,16]{0,1:T(8,128)(2,1)}, u32[]{:S(2)}) copy-start(bf16[2048,16]{0,1:T(8,128)(2,1)} %param.27) | copy-start | bytes 196612
  7.2 154.3 %all-gather.2.cloned.1.call-start = ((), (), s32[]{:S(2)}) async-start(), calls=%async_computation | async-start | bytes 17301504 | tf_op jit(solution)/shard_map/all_gather | solution.py:1268
  132.6 2.3 copy-start.2
  134.9 23.3 %copy-start.3 = (bf16[128,2048]{1,0:T(8,128)(2,1)S(1)}, bf16[128,2048]{1,0:T(8,128)(2,1)}, u32[]{:S(2)}) copy-start(bf16[128,2048]{1,0:T(8,128)(2,1)} %x_ref.1) | copy-start | bytes 1572868
  134.9 24.8 %copy-start.14 = (f32[2048]{0:T(1024)S(1)}, f32[2048]{0:T(1024)}, u32[]{:S(2)}) copy-start(f32[2048]{0:T(1024)} %param.26) | copy-start | bytes 24580
  158.2 2.1 copy-start.16
  159.9 1.6 copy-start.4
  278.1 94.7 %copy-start.5 = (bf16[128,2048]{1,0:T(8,128)(2,1)S(1)}, bf16[128,2048]{1,0:T(8,128)(2,1)}, u32[]{:S(2)}) copy-start(bf16[128,2048]{1,0:T(8,128)(2,1)} %copy-done.4) | copy-start | bytes 1572868
  370.7 4.0 copy-start.10
  431.3 0.7 copy-start.13
  618.9 5.0 copy-start.11
  618.9 6.6 %copy-start.9 = (f32[128,2048]{1,0:T(8,128)S(1)}, f32[128,2048]{1,0:T(8,128)}, u32[]{:S(2)}) copy-start(f32[128,2048]{1,0:T(8,128)} %get-tuple-element.69) | copy-start | bytes 3145732
  618.9 6.6 %copy-start.15 = (f32[2048]{0:T(1024)S(1)}, f32[2048]{0:T(1024)}, u32[]{:S(2)}) copy-start(f32[2048]{0:T(1024)} %param.19) | copy-start | bytes 24580
  623.9 1.8 copy-start.12
  625.8 4.5 copy-start.8
  630.2 3.7 copy-start.7
  633.9 3.7 copy-start.6
  633.9 5.7 copy-start.1
Sparse Core Ops, SparseCore 0:
  10.9 150.3 all-gather.1

commit v7 on v6

--- a/solution.py
+++ b/solution.py
@@ -807,10 +807,12 @@
 
 
 def entry_kernel(planes, entry_part, route_part, all_h, cot, active, grad_gate, grad_up, w_down,
-                 entry_out, route_out, mixed_out, acc_gate, acc_up, acc_down, *scratch):
+                 entry_out, route_out, mixed_out, gate_grad, up_grad, down_grad, *scratch):
     buffers = [scratch[2 * i:2 * i + 2] for i in range(5)]
     semaphores = scratch[10:17]
-    down_use, rows_h, rows_c, rows_x, mixed_stage, down_sem, load_sem, store_sem = scratch[17:]
+    down_use, rows_h, rows_c, rows_x, mixed_stage, acc_gate, acc_up, acc_down, down_sem, load_sem, store_sem, grad_sem = scratch[17:]
+    leaves = [pltpu.make_async_copy(source, target, grad_sem.at[i]) for i, (source, target) in enumerate((
+        (acc_gate, gate_grad), (acc_up, up_grad), (acc_down, down_grad)))]
     group = rows_h.shape[1]
     groups = all_h.shape[0] // group
 
@@ -858,6 +860,11 @@
         mixed_stage[...] = jnp.dot(rows_x[slot, 0], down_use[...], preferred_element_type=jnp.float32).astype(jnp.bfloat16)
         store(g).start()
 
+        @pl.when(g == groups - 1)
+        def _():
+            for leave in leaves:
+                leave.start()
+
     per_step = -(-groups // (planes * CUTS))
 
     def filler(step):
@@ -870,6 +877,8 @@
 
     reduce_steps(planes, CUTS, (entry_part, route_part), (entry_out, route_out), buffers, semaphores, filler)
     store(groups - 1).wait()
+    for leave in leaves:
+        leave.wait()
 
 
 def entry_sums(entry_part, route_part, all_h, cot, active, grad_gate, grad_up, w_down, collective_id):
@@ -884,10 +893,11 @@
         out_shape=[jax.ShapeDtypeStruct(shape, wide) for shape, _ in shapes] + [
             jax.ShapeDtypeStruct(entry_part.shape, low), jax.ShapeDtypeStruct((width, hidden), wide),
             jax.ShapeDtypeStruct((width, hidden), wide), jax.ShapeDtypeStruct((hidden, width), wide)],
-        in_specs=[ANYSPEC] * 8, out_specs=[kept, kept, ANYSPEC, kept, kept, kept],
+        in_specs=[ANYSPEC] * 8, out_specs=[kept, kept] + [ANYSPEC] * 4,
         scratch_shapes=buffers + semaphores + [
             vmem((hidden, width), low), vmem((2, group, width), low), vmem((2, group, width), low), vmem((2, 3, group, hidden), low),
-            vmem((group, width), low), dma((1,)), dma((2, 5)), dma((1,))],
+            vmem((group, width), low), vmem((width, hidden), wide), vmem((width, hidden), wide), vmem((hidden, width), wide),
+            dma((1,)), dma((2, 5)), dma((1,)), dma((3,))],
         compiler_params=pltpu.CompilerParams(collective_id=collective_id, has_side_effects=True, vmem_limit_bytes=60 * 2**20),
     )(entry_part, route_part, all_h, cot, active, grad_gate, grad_up, w_down)
 
@@ -1019,8 +1029,8 @@
 
 
 def backward_kernel(width, grad_ref, w_out_ref, x_hbm, proj_hbm, query_ref, key_ref, value_ref, raw_ref, scale_ref, mixed_ref,
-                    gains, cosine, sine, grad_x_out, grad_proj_out, grad_out_out, gain_out,
-                    x_ref, proj_ref, grad_query, grad_key, grad_value, grad_raw, sums, slots, load_sem, send_sem, recv_sem):
+                    gains, cosine, sine, grad_x_hbm, grad_proj_hbm, grad_out_out, gain_out,
+                    grad_x_out, grad_proj_out, leave_sem, x_ref, proj_ref, grad_query, grad_key, grad_value, grad_raw, sums, slots, load_sem, send_sem, recv_sem):
     greet(group_peers()[1])
     loads = [pltpu.make_async_copy(x_hbm, x_ref, load_sem.at[0]), pltpu.make_async_copy(proj_hbm, proj_ref, load_sem.at[1])]
     for load in loads:
@@ -1072,9 +1082,14 @@
     grad_raw[:, pl.ds(2 * local, local)] = grad_value[...].astype(jnp.bfloat16)
     for load in loads:
         load.wait()
+    leaves = [pltpu.make_async_copy(grad_x_out, grad_x_hbm, leave_sem.at[0]), pltpu.make_async_copy(grad_proj_out, grad_proj_hbm, leave_sem.at[1])]
     grad_x_out[...] = dot_cols(grad_raw[...], proj_ref[...]).astype(jnp.bfloat16)
+    leaves[0].start()
     grad_proj_out[...] = dot_rows(x_ref[...], grad_raw[...]).astype(jnp.bfloat16)
+    leaves[1].start()
     grad_out_out[...] = dot_rows(mixed_ref[...], grad_ref[...]).astype(jnp.bfloat16)
+    for leave in leaves:
+        leave.wait()
 
 
 def attention_backward(grad_gathered, w_out_own, gathered_x, w_proj, kept, gains, cosine, sine, collective_id):
@@ -1086,8 +1101,9 @@
     return pl.pallas_call(
         functools.partial(backward_kernel, width),
         out_shape=[shape((tokens, width), low), shape(w_proj.shape, low), shape(w_out_own.shape, low), shape((8, local), wide)],
-        in_specs=[vmem, vmem, ANYSPEC, ANYSPEC] + [vmem] * 9, out_specs=[vmem] * 4,
+        in_specs=[vmem, vmem, ANYSPEC, ANYSPEC] + [vmem] * 9, out_specs=[ANYSPEC, ANYSPEC, vmem, vmem],
         scratch_shapes=[
+            pltpu.VMEM((tokens, width), low), pltpu.VMEM(w_proj.shape, low), dma((2,)),
             pltpu.VMEM(gathered_x.shape, low), pltpu.VMEM(w_proj.shape, low),
             pltpu.VMEM((tokens, local), wide), pltpu.VMEM((tokens, local), wide), pltpu.VMEM((tokens, local), wide),
             pltpu.VMEM((tokens, 3 * local), low), pltpu.VMEM((8, tokens), wide), pltpu.VMEM((7, 8, tokens), wide),

time: 654 us -> 651 us (level)
  no operation moved by 1% of the time
where the time goes in v7:
time: 651 us; the launch traced here: 644 us
  Pallas kernels  593 us (91%)
  local copies, waits for them, and re-layouts  16.9 us (3%)
  other arithmetic  16.5 us (3%)
  between operations  14.6 us (2%)
    pallas_call x1, Pallas kernels, finish(): pl.pallas_call(functools.partial(finish_kernel, planes), out_shape=[jax.S...  187 us
    pallas_call x1, Pallas kernels, expert_rows_on_links(): pl.pallas_call(functools.partial(expert_kernel, planes, experts), out_sha...  117 us
    pallas_call x1, Pallas kernels, entry_sums(): pl.pallas_call(functools.partial(entry_kernel, planes), out_shape=[jax.Sh...  88.8 us
    pallas_call x1, Pallas kernels, opening(): pl.pallas_call(opening_kernel, out_shape=[shape((8 * hidden.shape[0], hid...  76.8 us
    pallas_call x1, Pallas kernels, attention_forward(): pl.pallas_call(functools.partial(forward_kernel, width), out_shape=[shape...  45.6 us
    pallas_call x1, Pallas kernels, attention_backward(): pl.pallas_call(functools.partial(backward_kernel, width), out_shape=[shap...  32.1 us
    pallas_call x1, Pallas kernels, reduce_scatter(): pl.pallas_call(functools.partial(reduce_kernel, planes, count), out_shape...  23.3 us
    pallas_call x1, Pallas kernels, gather(): pl.pallas_call(functools.partial(gather_kernel, planes, parts, count), ou...  22.7 us
  transfers between devices with their start and end apart: 1, of which 0 were waited for; matrix products, arithmetic and copies ran while one was open for 1% of the time, Pallas kernels for 23%

profile of v7, /device:TPU:6, one launch (start us, length us, event | category | flops | bytes accessed | tf_op | source)
XLA Modules:
  0.0 643.6 jit_solution(6582887365874310985)
XLA Ops:
  7.2 0.0 copy-start
  7.2 0.0 all-gather.2.cloned.1.call-start
  7.2 0.7 all-gather.2.cloned.1.call-update
  7.9 0.8 dynamic_slice.6
  8.7 0.8 dynamic_slice.7
  9.5 0.1 pad.5.clone
  9.5 76.8 %shard_map.272 = (bf16[1024,2048]{1,0:T(8,128)(2,1)}, bf16[2048,768]{1,0:T(8,128)(2,1)}) custom-call(bf16[128,2048]{1,0:T(8,128)(2,1)} %x_ref.1, f32[1,2048]{1,0:T(1,128)} %bitcast.43, bf16[512,1024]{1,0:T(8,128)(2,1)} %wq_ref.1, bf16[512,1024]{1,0:T(8,128)(2,1)} %wk_ref.1, bf16[512,1024]{1,0:T(8,128)(2,1)} %wv_ref.1), custom_call_target="tpu_custom_call" | custom-call | tf_op jit(solution)/shard_map/pallas_call | solution.py:334
  86.4 0.7 maximum_maximum_fusion.1.gains
  87.0 45.6 %shard_map.273 = (bf16[1024,2048]{1,0:T(8,128)(2,1)}, bf16[1024,256]{1,0:T(8,128)(2,1)}, bf16[1024,256]{1,0:T(8,128)(2,1)}, bf16[1024,256]{1,0:T(8,128)(2,1)}, f...) custom-call(bf16[1024,2048]{1,0:T(8,128)(2,1)} %get-tuple-element.45.x_ref.x_hb, ...), custom_call_target="tpu_custom_call" | custom-call | tf_op jit(solution)/shard_map/pallas_call | solution.py:1020
  132.6 0.0 copy-start.2
  132.6 2.3 copy-done.2
  134.9 23.3 %shard_map.274 = f32[128,2048]{1,0:T(8,128)S(1)} custom-call(bf16[1024,2048]{1,0:T(8,128)(2,1)S(1)} %copy-done.2), custom_call_target="tpu_custom_call" | custom-call | tf_op jit(solution)/shard_map/pallas_call | solution.py:286
  158.2 0.0 copy-done.3
  158.2 0.0 copy-start.16
  158.2 0.2 fusion
  158.4 1.3 multiply_reduce_fusion.2
  159.7 0.0 copy-done.14
  159.7 0.2 multiply_convert_fusion.own_h
  159.9 0.0 copy-done
  159.9 0.0 copy-start.4
  159.9 0.3 fusion.11
  160.1 0.1 copy.36
  160.3 0.0 copy-done.16
  160.3 0.1 copy.38
  160.4 0.1 pad.2.clone
  160.5 0.2 fusion.7
  160.6 0.1 multiply_convert_fusion.2
  160.8 0.7 maximum_maximum_fusion.own_side
  161.5 0.0 copy-done.4
  161.5 116.6 %shard_map.275 = (bf16[4096,2048]{1,0:T(8,128)(2,1)}, bf16[4096,128]{1,0:T(8,128)(2,1)}, bf16[4096,2048]{1,0:T(8,128)(2,1)}, bf16[4096,128]{1,0:T(8,128)(2,1)}, ...) custom-call(bf16[128,2048]{1,0:T(8,128)(2,1)} %copy-done.4, ...), custom_call_target="tpu_custom_call" | custom-call | tf_op jit(solution)/shard_map/pallas_call | solution.py:795
  278.1 0.0 copy-start.5
  278.1 88.8 %shard_map.276 = (f32[128,2048]{1,0:T(8,128)}, f32[128,128]{1,0:T(8,128)}, bf16[4096,2048]{1,0:T(8,128)(2,1)}, f32[2048,512]{1,0:T(8,128)}, f32[2048,512]{1,0:T(8,128)}, /*index=5*/f32[512,2048]{1,0:T(8,128)}) custom-call(bf16[4096,2048]{1,0:T(8,128)(2,1)} %get-tuple-element.48.entry_part, bf16[4096,128]{1,0:T(8,128)(2,1)} %get-tuple-element.49.route_part, ...), custom_call_target="tpu_custom_call" | custom-call | tf_op jit(solution)/shard_map/pallas_call | solution.py:891
  366.9 0.0 copy-start.10
  366.9 1.1 multiply_reduce_fusion.3
  368.0 1.0 multiply_convert_fusion.1
  369.0 0.0 copy-done.5
  369.0 0.2 convolution_bitcast_fusion
  369.2 1.7 multiply_reduce_fusion
  370.9 0.0 copy-done.10
  370.9 1.2 fusion.8
  372.1 22.7 %shard_map.277.grad_ref = bf16[1024,2048]{1,0:T(8,128)(2,1)} custom-call(bf16[128,2048]{1,0:T(8,128)(2,1)} %get-tuple-element.78.refs_0_), custom_call_target="tpu_custom_call" | custom-call | tf_op jit(solution)/shard_map/pallas_call | solution.py:107
  394.8 32.1 %shard_map.278 = (bf16[1024,2048]{1,0:T(8,128)(2,1)}, bf16[2048,768]{1,0:T(8,128)(2,1)}, bf16[256,2048]{1,0:T(8,128)(2,1)}, f32[8,256]{1,0:T(8,128)}) custom-call(bf16[1024,2048]{1,0:T(8,128)(2,1)} %shard_map.277.grad_ref, bf16[256,2048]{1,0:T(8,128)(2,1)} %get-tuple-element.56.w_out_ref, bf16[1024,2048]{1,0:T(8,128)(2,1)} %get-tuple-element.45.x_ref.x_hbm, ...), custom_call_target="tpu_custom_call" | custom-call | tf_op jit(solution)/shard_map/pallas_call | solution.py:1101
  426.9 0.8 fusion.10
  427.7 0.2 dynamic_update_slice.6
  427.9 0.3 dynamic_update_slice.7
  428.2 0.0 copy-start.13
  428.2 0.7 copy-done.13
  428.8 186.9 %shard_map.279 = (bf16[3,512,1024]{2,1,0:T(8,128)(2,1)}, bf16[1024,512]{1,0:T(8,128)(2,1)}, f32[8,40,128]{2,1,0:T(8,128)}, f32[128,2048]{1,0:T(8,128)}, f32[128,2048]{1,0:T(8,128)}) custom-call(bf16[2048,768]{1,0:T(8,128)(2,1)} %get-tuple-element.63.proj_ref, bf16[256,2048]{1,0:T(8,128)(2,1)} %get-tuple-element.64.outp_ref, f32[8,40,128]{2,1,0:T(8,128)} %bitcast.42, ...), custom_call_target="tpu_custom_call" | custom-call | tf_op jit(solution)/shard_map/pallas_call | solution.py:587
  615.8 0.0 copy-start.11
  615.8 0.0 copy-start.9
  615.8 0.0 copy-start.15
  615.8 4.9 bitcast_convert_fusion
  620.8 0.0 copy-done.11
  620.8 1.6 convert_element_type.67
  622.4 0.2 fusion.5
  622.6 0.0 copy-done.12
  622.6 0.7 slice_bitcast_fusion
  623.3 0.6 fusion.9
  623.9 3.2 fusion.4
  627.1 2.1 copy.50
  629.2 1.6 copy-done.7
  630.8 2.1 copy.51
  632.9 1.6 copy-done.6
  634.5 2.0 copy.52
  (26 shorter events, 0.1 us)
Async XLA Ops:
  7.2 152.7 %copy-start = (bf16[2048,16]{0,1:T(8,128)(2,1)S(1)}, bf16[2048,16]{0,1:T(8,128)(2,1)}, u32[]{:S(2)}) copy-start(bf16[2048,16]{0,1:T(8,128)(2,1)} %param.27) | copy-start | bytes 196612
  7.2 154.3 %all-gather.2.cloned.1.call-start = ((), (), s32[]{:S(2)}) async-start(), calls=%async_computation | async-start | bytes 17301504 | tf_op jit(solution)/shard_map/all_gather | solution.py:1284
  132.6 2.3 copy-start.2
  134.9 23.3 %copy-start.3 = (bf16[128,2048]{1,0:T(8,128)(2,1)S(1)}, bf16[128,2048]{1,0:T(8,128)(2,1)}, u32[]{:S(2)}) copy-start(bf16[128,2048]{1,0:T(8,128)(2,1)} %x_ref.1) | copy-start | bytes 1572868
  134.9 24.8 %copy-start.14 = (f32[2048]{0:T(1024)S(1)}, f32[2048]{0:T(1024)}, u32[]{:S(2)}) copy-start(f32[2048]{0:T(1024)} %param.26) | copy-start | bytes 24580
  158.2 2.1 copy-start.16
  159.9 1.6 copy-start.4
  278.1 90.9 %copy-start.5 = (bf16[128,2048]{1,0:T(8,128)(2,1)S(1)}, bf16[128,2048]{1,0:T(8,128)(2,1)}, u32[]{:S(2)}) copy-start(bf16[128,2048]{1,0:T(8,128)(2,1)} %copy-done.4) | copy-start | bytes 1572868
  366.9 4.0 copy-start.10
  428.2 0.7 copy-start.13
  615.8 5.0 copy-start.11
  615.8 6.6 %copy-start.9 = (f32[128,2048]{1,0:T(8,128)S(1)}, f32[128,2048]{1,0:T(8,128)}, u32[]{:S(2)}) copy-start(f32[128,2048]{1,0:T(8,128)} %get-tuple-element.69) | copy-start | bytes 3145732
  615.8 6.6 %copy-start.15 = (f32[2048]{0:T(1024)S(1)}, f32[2048]{0:T(1024)}, u32[]{:S(2)}) copy-start(f32[2048]{0:T(1024)} %param.19) | copy-start | bytes 24580
  620.7 1.8 copy-start.12
  622.6 4.5 copy-start.8
  627.1 3.7 copy-start.7
  630.8 3.7 copy-start.6
  630.8 5.7 copy-start.1
Sparse Core Ops, SparseCore 0:
  10.9 150.3 all-gather.1
